TPU v7x, 128 devices: a whole 4x4x4 slice. The times are simulated.
128 devices in a mesh: seq: 16 (over x, y_lo, core), head: 8 (over z, y_hi).
Axes of the slice: x: 4, y: 4 (y_hi: 2, y_lo: 2; y = y_hi * 2 + y_lo), z: 4, core: 2. Of those that a mesh axis runs over, the one named last changes fastest.
Arguments:
- queries: bfloat16 [12288, 2048], P(('seq', 'head')), may hold values from -8 to 8
- keys: bfloat16 [12288, 2048], P(('seq', 'head')), may hold values from -8 to 8
- values: bfloat16 [12288, 2048], P(('seq', 'head')), may hold values from -6 to 6
- cotangent: bfloat16 [12288, 2048], P(('seq', 'head')), may hold values from -6 to 6
- neighbours: int32 [192, 27], replicated, may hold values from -1 to 191, as said below
Outputs:
- output: bfloat16 [12288, 2048], P(('seq', 'head'))
- grad_query: bfloat16 [12288, 2048], P(('seq', 'head'))
- grad_key: bfloat16 [12288, 2048], P(('seq', 'head'))
- grad_value: bfloat16 [12288, 2048], P(('seq', 'head'))
Inputs may be any that keep to these rules, and one draw needn't show every extreme that they name: `neighbours`: row g lists distinct tiles, always g itself; a listed tile's frame, tile row and tile column each differ from g's by at most one; -1 marks an empty slot; slots stand in any order.
All inputs are finite; a program needn't handle non-finite values.
Results may differ from a plain program's by a relative error of at most 0.015.
Values may be sent and summed in bfloat16 or wider, within the bound.
No kernel may reach another device: no remote copies, remote signals or barrier semaphores. Data moves between devices by JAX's collectives and lax.ppermute only.
A program may use at most 128 MiB of HBM per device.

v0:
```python
import math

import jax
import jax.numpy as jnp
from jax import lax
from jax.sharding import PartitionSpec as P

TILE = 64
TILES_F = 12
SLOTS = 27
HD = 128
F_DEV = 1


masked_score = -1e30


def extended(cells, sides, width):
    for axis, dim in sides:
        count = lax.axis_size(axis)
        ends = count - 1
        head = lax.slice_in_dim(cells, 0, width, axis=dim)
        tail = lax.slice_in_dim(cells, cells.shape[dim] - width, cells.shape[dim], axis=dim)
        cells = jnp.concatenate(
            [
                lax.ppermute(tail, axis, [(i, (i + 1) % count) for i in range(ends)]),
                cells,
                lax.ppermute(head, axis, [((i + 1) % count, i) for i in range(ends)]),
            ],
            axis=dim,
        )
    return cells


def shifted(array, axis, by):
    peers = lax.axis_size(axis)
    pairs = [(i, i + by) for i in range(peers) if 0 <= i + by < peers]
    return lax.ppermute(array, axis, pairs)


def split_heads(rows, head_count):
    return rows.reshape(rows.shape[0], rows.shape[1], head_count, rows.shape[2] // head_count)


def tile_probs(query_heads, key_heads, key_mask, log_total, score_scale):
    scores = (
        jnp.einsum("btnd,bknd->bntk", query_heads, key_heads, preferred_element_type=jnp.float32)
        * score_scale
    )
    scores = jnp.where(key_mask[:, None, None, :], scores, masked_score)
    row_max = jnp.max(scores, axis=-1, keepdims=True)
    log_total = row_max + jnp.log(jnp.sum(jnp.exp(scores - row_max), axis=-1, keepdims=True))
    return (jnp.exp(scores - log_total), log_total)


def pair_grads(probs, probs_low, grad_dot, query_heads, value_heads, cot_heads, score_scale):
    grad_prob = jnp.einsum(
        "btnd,bknd->bntk", cot_heads, value_heads, preferred_element_type=jnp.float32
    )
    grad_score = (
        probs * (grad_prob - jnp.transpose(grad_dot, (0, 2, 1))[..., None]) * score_scale
    ).astype(jnp.bfloat16)
    grad_key = jnp.einsum(
        "bntk,btnd->bknd", grad_score, query_heads, preferred_element_type=jnp.float32
    )
    grad_value = jnp.einsum(
        "bntk,btnd->bknd", probs_low, cot_heads, preferred_element_type=jnp.float32
    )
    block_tiles, key_len = (grad_key.shape[0], grad_key.shape[1])
    grad_pair = jnp.concatenate(
        [grad_key.reshape(block_tiles, key_len, -1), grad_value.reshape(block_tiles, key_len, -1)],
        axis=-1,
    )
    return (grad_score, grad_pair)


def attend_both(query_blk, kv_near, key_mask, cot_blk, head_count):
    feature_width = query_blk.shape[2]
    score_scale = 1.0 / math.sqrt(feature_width // head_count)
    query_heads = split_heads(query_blk, head_count)
    key_heads = split_heads(kv_near[:, :, :feature_width], head_count)
    value_heads = split_heads(kv_near[:, :, feature_width:], head_count)
    cot_heads = split_heads(cot_blk, head_count)
    probs, log_total = tile_probs(query_heads, key_heads, key_mask, None, score_scale)
    probs_low = probs.astype(jnp.bfloat16)
    output = jnp.einsum(
        "bntk,bknd->btnd", probs_low, value_heads, preferred_element_type=jnp.float32
    ).astype(jnp.bfloat16)
    grad_dot = jnp.sum(cot_heads.astype(jnp.float32) * output.astype(jnp.float32), axis=-1)
    grad_score, grad_pair = pair_grads(
        probs, probs_low, grad_dot, query_heads, value_heads, cot_heads, score_scale
    )
    grad_query = jnp.einsum(
        "bntk,bknd->btnd", grad_score, key_heads, preferred_element_type=jnp.float32
    ).astype(jnp.bfloat16)
    shape_rows = query_blk.shape
    stats = jnp.concatenate([jnp.transpose(log_total[..., 0], (0, 2, 1)), grad_dot], axis=-1)
    return (output.reshape(shape_rows), grad_query.reshape(shape_rows), stats, grad_pair)


def shards(queries, keys, values, cotangent, neighbours):
    query_seq = lax.all_to_all(queries, "head", split_axis=1, concat_axis=0, tiled=True)
    keys_seq, values_seq = (
        lax.all_to_all(keys, "head", split_axis=1, concat_axis=0, tiled=True),
        lax.all_to_all(values, "head", split_axis=1, concat_axis=0, tiled=True),
    )
    cot_seq = lax.all_to_all(cotangent, "head", split_axis=1, concat_axis=0, tiled=True)
    feature_width = query_seq.shape[1]
    head_count = feature_width // HD
    frame_tok = TILE * TILES_F
    own_tiles = F_DEV * TILES_F
    ext_tiles = own_tiles + 2 * TILES_F
    all_tiles = lax.axis_size("seq") * own_tiles
    first_tile = lax.axis_index("seq") * own_tiles
    base_tile = first_tile - TILES_F
    block_tiles = TILES_F // 4
    kv_pair = jnp.concatenate([keys_seq, values_seq], axis=1)
    kv_ext = extended(kv_pair, (("seq", 0),), frame_tok)
    pair_tiles = jnp.concatenate(
        [
            kv_ext.reshape(ext_tiles, TILE, 2 * feature_width),
            jnp.zeros((1, TILE, 2 * feature_width), jnp.bfloat16),
        ],
        axis=0,
    )

    def near_pairs(index_blk):
        return jnp.take(pair_tiles, index_blk, axis=0).reshape(
            index_blk.shape[0], SLOTS * TILE, 2 * feature_width
        )

    query_tiles = query_seq.reshape(own_tiles, TILE, feature_width)
    cot_tiles = cot_seq.reshape(own_tiles, TILE, feature_width)
    tile_ids = first_tile + jnp.arange(own_tiles, dtype=jnp.int32)
    present = (tile_ids >= 0) & (tile_ids < all_tiles)
    rows_listed = jnp.take(neighbours, jnp.clip(tile_ids, 0, neighbours.shape[0] - 1), axis=0)
    relative = rows_listed - base_tile
    usable = present[:, None] & (rows_listed >= 0) & (relative >= 0) & (relative < ext_tiles)
    own_index = jnp.where(usable, relative, ext_tiles)

    def own_step(grad_buffer, block_id):
        first_row = block_id * block_tiles
        query_blk = lax.dynamic_slice_in_dim(query_tiles, first_row, block_tiles, 0)
        cot_blk = lax.dynamic_slice_in_dim(cot_tiles, first_row, block_tiles, 0)
        index_blk = lax.dynamic_slice_in_dim(own_index, first_row, block_tiles, 0)
        usable_blk = lax.dynamic_slice_in_dim(usable, first_row, block_tiles, 0)
        key_mask = jnp.repeat(usable_blk, TILE, axis=1)
        output, grad_query, stats, grad_pair = attend_both(
            query_blk, near_pairs(index_blk), key_mask, cot_blk, head_count
        )
        grad_buffer = grad_buffer.at[index_blk].add(
            grad_pair.reshape(block_tiles, SLOTS, TILE, 2 * feature_width)
        )
        return (grad_buffer, (output, grad_query, stats))

    start_buffer = jnp.zeros((ext_tiles + 1, TILE, 2 * feature_width), jnp.float32)
    grad_buffer, (outputs, grad_queries, own_stats) = lax.scan(
        own_step, start_buffer, jnp.arange(own_tiles // block_tiles, dtype=jnp.int32)
    )
    own_rows = F_DEV * frame_tok
    output_rows = outputs.reshape(own_rows, feature_width)
    grad_query_rows = grad_queries.reshape(own_rows, feature_width)
    upper_part = grad_buffer[:TILES_F]
    lower_part = grad_buffer[TILES_F + own_tiles : ext_tiles]
    from_next = shifted(upper_part.astype(jnp.bfloat16), "seq", -1).astype(upper_part.dtype)
    from_prev = shifted(lower_part.astype(jnp.bfloat16), "seq", 1).astype(lower_part.dtype)
    own_grad = grad_buffer[TILES_F : TILES_F + own_tiles]
    own_grad = own_grad.at[:TILES_F].add(from_prev)
    own_grad = own_grad.at[own_tiles - TILES_F :].add(from_next)
    grad_rows = own_grad.reshape(own_rows, 2 * feature_width)
    grad_key_rows = grad_rows[:, :feature_width].astype(jnp.bfloat16)
    grad_value_rows = grad_rows[:, feature_width:].astype(jnp.bfloat16)
    output, grad_query, grad_key, grad_value = (
        lax.all_to_all(output_rows, "head", split_axis=0, concat_axis=1, tiled=True),
        lax.all_to_all(grad_query_rows, "head", split_axis=0, concat_axis=1, tiled=True),
        lax.all_to_all(grad_key_rows, "head", split_axis=0, concat_axis=1, tiled=True),
        lax.all_to_all(grad_value_rows, "head", split_axis=0, concat_axis=1, tiled=True),
    )
    return (output, grad_query, grad_key, grad_value)


def solution(mesh):
    placed = (
        P(("seq", "head"), None),
        P(("seq", "head"), None),
        P(("seq", "head"), None),
        P(("seq", "head"), None),
        P(),
    )
    return jax.shard_map(
        shards,
        mesh=mesh,
        in_specs=placed,
        out_specs=(
            P(("seq", "head"), None),
            P(("seq", "head"), None),
            P(("seq", "head"), None),
            P(("seq", "head"), None),
        ),
        check_vma=False,
    )
```

profile of v0, /device:TPU:2, one launch (start us, length us, event | category | flops | bytes accessed | tf_op | source)
XLA Modules:
  0.0 530.6 jit_solution(12701251037464737702)
XLA Ops:
  2.5 8.1 %all-to-all-start.1 = ((bf16[96,8,256]{2,0,1:T(8,128)(2,1)}), bf16[96,8,256]{2,0,1:T(8,128)(2,1)S(1)}, u32[]{:S(2)}, u32[]{:S(2)}) async-start(bf16[96,8,256]{2,0,1:T(8,128)(2,1)} %bitcast.83), calls=%async_computation.1 | async-start | bytes 786432 | tf_op jit(solution)/shard_map/all_to_all | solution.py:104
  12.3 8.4 %all-to-all-done.1 = bf16[96,8,256]{2,0,1:T(8,128)(2,1)S(1)} async-done(((bf16[96,8,256]{2,0,1:T(8,128)(2,1)}), bf16[96,8,256]{2,0,1:T(8,128)(2,1)S(1)}, u32[]{:S(2)}, u32[]{:S(2)}) %all-to-all-start.1) | async-done | bytes 393248 | tf_op jit(solution)/shard_map/all_to_all | solution.py:104
  25.0 8.6 %all-to-all-done.2 = bf16[96,8,256]{2,0,1:T(8,128)(2,1)S(1)} async-done(((bf16[96,8,256]{2,0,1:T(8,128)(2,1)}), bf16[96,8,256]{2,0,1:T(8,128)(2,1)S(1)}, u32[]{:S(2)}, u32[]{:S(2)}) %all-to-all-start.2) | async-done | bytes 393248 | tf_op jit(solution)/shard_map/all_to_all | solution.py:105
  44.0 9.8 %all-to-all-done = bf16[96,8,256]{2,0,1:T(8,128)(2,1)S(1)} async-done(((bf16[96,8,256]{2,0,1:T(8,128)(2,1)}), bf16[96,8,256]{2,0,1:T(8,128)(2,1)S(1)}, u32[]{:S(2)}, u32[]{:S(2)}) %all-to-all-start) | async-done | bytes 393248 | tf_op jit(solution)/shard_map/all_to_all | solution.py:102
  58.4 9.1 %all-to-all-done.3 = bf16[96,8,256]{2,0,1:T(8,128)(2,1)S(1)} async-done(((bf16[96,8,256]{2,0,1:T(8,128)(2,1)}), bf16[96,8,256]{2,0,1:T(8,128)(2,1)S(1)}, u32[]{:S(2)}, u32[]{:S(2)}) %all-to-all-start.3) | async-done | bytes 393248 | tf_op jit(solution)/shard_map/all_to_all | solution.py:107
  70.3 389.3 %while.18 = (s32[]{:T(128)}, f32[37,64,512]{2,1,0:T(8,128)}, bf16[4,3,64,256]{3,2,1,0:T(8,128)(2,1)}, bf16[4,3,64,256]{3,2,1,0:T(8,128)(2,1)}, s32[4]{0:T(128)S(...) while((s32[]{:T(128)}, f32[37,64,512]{2,1,0:T(8,128)}, ...), condition=%wide.region_5.6_spmd, body=%wide.region_0.5_spmd.sunk | while | flops 1036763904 | bytes 215138368 | solution.py:157
  78.8 8.2 %copy.158 = bf16[3,1728,512]{1,2,0:T(8,128)(2,1)} copy(bf16[3,1728,512]{2,1,0:T(8,128)(2,1)} %bitcast.132) | data formatting | bytes 10616832 | tf_op jit(solution)/shard_map/while/body/eval_jaxpr/jit(_take)/gather | solution.py:128
  97.7 7.5 %copy.159 = f32[3,1728,2,128]{3,2,1,0:T(2,128)} copy(f32[3,1728,2,128]{3,1,2,0:T(8,128)S(1)} %convolution_bitcast_fusion.4) | data formatting | bytes 10616832 | tf_op jit(solution)/shard_map/while/body/eval_jaxpr/bntk,btnd->bknd/transpose | solution.py:66
  105.1 8.2 %concatenate.26 = f32[3,27,64,256]{3,2,1,0:T(8,128)} reshape(f32[3,1728,2,128]{3,2,1,0:T(2,128)} %copy.159) | data formatting | bytes 10616832 | tf_op jit(solution)/shard_map/while/body/eval_jaxpr/concatenate | solution.py:70
  114.3 7.5 %copy.160 = f32[3,1728,2,128]{3,2,1,0:T(2,128)} copy(f32[3,1728,2,128]{3,1,2,0:T(8,128)S(1)} %convolution_bitcast_fusion.5) | data formatting | bytes 10616832 | tf_op jit(solution)/shard_map/while/body/eval_jaxpr/bntk,btnd->bknd/transpose | solution.py:63
  121.8 8.0 %concatenate.27 = f32[3,27,64,256]{3,2,1,0:T(8,128)} reshape(f32[3,1728,2,128]{3,2,1,0:T(2,128)} %copy.160) | data formatting | bytes 10616832 | tf_op jit(solution)/shard_map/while/body/eval_jaxpr/concatenate | solution.py:70
  129.8 10.0 %pad_maximum_fusion.4 = f32[3,27,64,512]{3,2,1,0:T(8,128)} fusion(f32[3,27,64,256]{3,2,1,0:T(8,128)} %concatenate.26, f32[3,27,64,256]{3,2,1,0:T(8,128)} %concatenate.27), kind=kLoop, calls=%fused_computation.3.clone.1 | loop fusion | flops 2654208 | bytes 21233664 | tf_op jit(solution)/shard_map/while/body/eval_jaxpr/concatenate | solution.py:70
  139.9 27.8 %scatter_fusion = f32[37,64,512]{2,1,0:T(8,128)} fusion(f32[37,64,512]{2,1,0:T(8,128)} %get-tuple-element.236, s32[81]{0:T(128)S(1)} %reshape.231, f32[81,64,512]{2,1,0:T(8,128)} %bitcast.127), kind=kCustom, calls=%fused_computation.2.clone.1 | custom fusion | flops 2654208 | bytes 31850820 | tf_op jit(solution)/shard_map/while/body/eval_jaxpr/scatter-add | solution.py:151
  176.2 8.2 %copy.158 = bf16[3,1728,512]{1,2,0:T(8,128)(2,1)} copy(bf16[3,1728,512]{2,1,0:T(8,128)(2,1)} %bitcast.132) | data formatting | bytes 10616832 | tf_op jit(solution)/shard_map/while/body/eval_jaxpr/jit(_take)/gather | solution.py:128
  195.1 7.5 %copy.159 = f32[3,1728,2,128]{3,2,1,0:T(2,128)} copy(f32[3,1728,2,128]{3,1,2,0:T(8,128)S(1)} %convolution_bitcast_fusion.4) | data formatting | bytes 10616832 | tf_op jit(solution)/shard_map/while/body/eval_jaxpr/bntk,btnd->bknd/transpose | solution.py:66
  202.6 8.2 %concatenate.26 = f32[3,27,64,256]{3,2,1,0:T(8,128)} reshape(f32[3,1728,2,128]{3,2,1,0:T(2,128)} %copy.159) | data formatting | bytes 10616832 | tf_op jit(solution)/shard_map/while/body/eval_jaxpr/concatenate | solution.py:70
  219.3 8.0 %concatenate.27 = f32[3,27,64,256]{3,2,1,0:T(8,128)} reshape(f32[3,1728,2,128]{3,2,1,0:T(2,128)} %copy.160) | data formatting | bytes 10616832 | tf_op jit(solution)/shard_map/while/body/eval_jaxpr/concatenate | solution.py:70
  227.3 10.0 %pad_maximum_fusion.4 = f32[3,27,64,512]{3,2,1,0:T(8,128)} fusion(f32[3,27,64,256]{3,2,1,0:T(8,128)} %concatenate.26, f32[3,27,64,256]{3,2,1,0:T(8,128)} %concatenate.27), kind=kLoop, calls=%fused_computation.3.clone.1 | loop fusion | flops 2654208 | bytes 21233664 | tf_op jit(solution)/shard_map/while/body/eval_jaxpr/concatenate | solution.py:70
  237.4 27.7 %scatter_fusion = f32[37,64,512]{2,1,0:T(8,128)} fusion(f32[37,64,512]{2,1,0:T(8,128)} %get-tuple-element.236, s32[81]{0:T(128)S(1)} %reshape.231, f32[81,64,512]{2,1,0:T(8,128)} %bitcast.127), kind=kCustom, calls=%fused_computation.2.clone.1 | custom fusion | flops 2654208 | bytes 31850820 | tf_op jit(solution)/shard_map/while/body/eval_jaxpr/scatter-add | solution.py:151
  273.6 8.2 %copy.158 = bf16[3,1728,512]{1,2,0:T(8,128)(2,1)} copy(bf16[3,1728,512]{2,1,0:T(8,128)(2,1)} %bitcast.132) | data formatting | bytes 10616832 | tf_op jit(solution)/shard_map/while/body/eval_jaxpr/jit(_take)/gather | solution.py:128
  300.0 8.2 %concatenate.26 = f32[3,27,64,256]{3,2,1,0:T(8,128)} reshape(f32[3,1728,2,128]{3,2,1,0:T(2,128)} %copy.159) | data formatting | bytes 10616832 | tf_op jit(solution)/shard_map/while/body/eval_jaxpr/concatenate | solution.py:70
  316.7 8.0 %concatenate.27 = f32[3,27,64,256]{3,2,1,0:T(8,128)} reshape(f32[3,1728,2,128]{3,2,1,0:T(2,128)} %copy.160) | data formatting | bytes 10616832 | tf_op jit(solution)/shard_map/while/body/eval_jaxpr/concatenate | solution.py:70
  324.7 10.0 %pad_maximum_fusion.4 = f32[3,27,64,512]{3,2,1,0:T(8,128)} fusion(f32[3,27,64,256]{3,2,1,0:T(8,128)} %concatenate.26, f32[3,27,64,256]{3,2,1,0:T(8,128)} %concatenate.27), kind=kLoop, calls=%fused_computation.3.clone.1 | loop fusion | flops 2654208 | bytes 21233664 | tf_op jit(solution)/shard_map/while/body/eval_jaxpr/concatenate | solution.py:70
  334.8 27.6 %scatter_fusion = f32[37,64,512]{2,1,0:T(8,128)} fusion(f32[37,64,512]{2,1,0:T(8,128)} %get-tuple-element.236, s32[81]{0:T(128)S(1)} %reshape.231, f32[81,64,512]{2,1,0:T(8,128)} %bitcast.127), kind=kCustom, calls=%fused_computation.2.clone.1 | custom fusion | flops 2654208 | bytes 31850820 | tf_op jit(solution)/shard_map/while/body/eval_jaxpr/scatter-add | solution.py:151
  371.0 8.2 %copy.158 = bf16[3,1728,512]{1,2,0:T(8,128)(2,1)} copy(bf16[3,1728,512]{2,1,0:T(8,128)(2,1)} %bitcast.132) | data formatting | bytes 10616832 | tf_op jit(solution)/shard_map/while/body/eval_jaxpr/jit(_take)/gather | solution.py:128
  397.4 8.2 %concatenate.26 = f32[3,27,64,256]{3,2,1,0:T(8,128)} reshape(f32[3,1728,2,128]{3,2,1,0:T(2,128)} %copy.159) | data formatting | bytes 10616832 | tf_op jit(solution)/shard_map/while/body/eval_jaxpr/concatenate | solution.py:70
  414.0 8.0 %concatenate.27 = f32[3,27,64,256]{3,2,1,0:T(8,128)} reshape(f32[3,1728,2,128]{3,2,1,0:T(2,128)} %copy.160) | data formatting | bytes 10616832 | tf_op jit(solution)/shard_map/while/body/eval_jaxpr/concatenate | solution.py:70
  422.0 10.0 %pad_maximum_fusion.4 = f32[3,27,64,512]{3,2,1,0:T(8,128)} fusion(f32[3,27,64,256]{3,2,1,0:T(8,128)} %concatenate.26, f32[3,27,64,256]{3,2,1,0:T(8,128)} %concatenate.27), kind=kLoop, calls=%fused_computation.3.clone.1 | loop fusion | flops 2654208 | bytes 21233664 | tf_op jit(solution)/shard_map/while/body/eval_jaxpr/concatenate | solution.py:70
  432.1 27.5 %scatter_fusion = f32[37,64,512]{2,1,0:T(8,128)} fusion(f32[37,64,512]{2,1,0:T(8,128)} %get-tuple-element.236, s32[81]{0:T(128)S(1)} %reshape.231, f32[81,64,512]{2,1,0:T(8,128)} %bitcast.127), kind=kCustom, calls=%fused_computation.2.clone.1 | custom fusion | flops 2654208 | bytes 31850820 | tf_op jit(solution)/shard_map/while/body/eval_jaxpr/scatter-add | solution.py:151
  462.5 9.3 %collective-permute-start.2 = (bf16[12,64,512]{2,1,0:T(8,128)(2,1)S(1)}, bf16[12,64,512]{2,1,0:T(8,128)(2,1)S(1)}, u32[]{:S(2)}, u32[]{:S(2)}) collective-permute-start(bf16[12,64,512]{2,1,0:T(8,128)(2,1)S(1)} %get-tuple-element.132), channel_id=1, source_target_pairs={{0,8},{8,16},{16,24},{24,32},{32,40},{40,48},{48,56},{56,64},{64,7... | collective-permute-start | bytes 2359304 | tf_op jit(solution)/shard_map/ppermute | solution.py:38
  473.8 16.0 %all_to_all.146 = bf16[8,96,256]{2,1,0:T(8,128)(2,1)S(1)} all-to-all(bf16[8,96,256]{2,1,0:T(8,128)(2,1)S(1)} %bitcast.150), channel_id=1, replica_groups=mesh['seq'=16,'head'=8] {'head'}, dimensions={0} | all-to-all | bytes 786432 | tf_op jit(solution)/shard_map/all_to_all | solution.py:174
  504.7 12.2 %all_to_all.147 = bf16[8,96,256]{2,1,0:T(8,128)(2,1)S(1)} all-to-all(bf16[8,96,256]{2,1,0:T(8,128)(2,1)S(1)} %bitcast.145), channel_id=1, replica_groups=mesh['seq'=16,'head'=8] {'head'}, dimensions={0} | all-to-all | bytes 786432 | tf_op jit(solution)/shard_map/all_to_all | solution.py:176
  (221 shorter events, 173.9 us)
Async XLA Ops:
  0.6 23.6 %copy-start.8 = (bf16[96,2048]{1,0:T(8,128)(2,1)S(1)}, bf16[96,2048]{1,0:T(8,128)(2,1)}, u32[]{:S(2)}) copy-start(bf16[96,2048]{1,0:T(8,128)(2,1)} %param.15) | copy-start | bytes 1179652
  2.5 39.9 %copy-start.11 = (s32[192,27]{0,1:T(8,128)S(1)}, s32[192,27]{0,1:T(8,128)}, u32[]{:S(2)}) copy-start(s32[192,27]{0,1:T(8,128)} %param.19) | copy-start | bytes 62212
  2.5 40.0 %copy-start.9 = (bf16[96,2048]{1,0:T(8,128)(2,1)S(1)}, bf16[96,2048]{1,0:T(8,128)(2,1)}, u32[]{:S(2)}) copy-start(bf16[96,2048]{1,0:T(8,128)(2,1)} %param.18) | copy-start | bytes 1179652
  2.5 18.3 %all-to-all-start.1 = ((bf16[96,8,256]{2,0,1:T(8,128)(2,1)}), bf16[96,8,256]{2,0,1:T(8,128)(2,1)S(1)}, u32[]{:S(2)}, u32[]{:S(2)}) async-start(bf16[96,8,256]{2,0,1:T(8,128)(2,1)} %bitcast.83), calls=%async_computation.1 | async-start | bytes 786432 | tf_op jit(solution)/shard_map/all_to_all | solution.py:104
  20.7 12.9 %all-to-all-start.2 = ((bf16[96,8,256]{2,0,1:T(8,128)(2,1)}), bf16[96,8,256]{2,0,1:T(8,128)(2,1)S(1)}, u32[]{:S(2)}, u32[]{:S(2)}) async-start(bf16[96,8,256]{2,0,1:T(8,128)(2,1)} %bitcast.82), calls=%async_computation.2 | async-start | bytes 786432 | tf_op jit(solution)/shard_map/all_to_all | solution.py:105
  34.5 23.5 %collective-permute-start.1 = (bf16[768,512]{1,0:T(8,128)(2,1)}, bf16[768,512]{1,0:T(8,128)(2,1)S(1)}, u32[]{:S(2)}, u32[]{:S(2)}) collective-permute-start(bf16[768,512]{1,0:T(8,128)(2,1)} %pad_maximum_fusion.2), channel_id=1, source_target_pairs={{8,0},{16,8},{24,16},{32,24},{40,32},{48,40},{56,48},{64,56},{72,6... | collective-permute-start | bytes 2359304 | tf_op jit(solution)/shard_map/ppermute | solution.py:28
  36.5 21.6 %collective-permute-start = (bf16[768,512]{1,0:T(8,128)(2,1)}, bf16[768,512]{1,0:T(8,128)(2,1)S(1)}, u32[]{:S(2)}, u32[]{:S(2)}) collective-permute-start(bf16[768,512]{1,0:T(8,128)(2,1)} %pad_maximum_fusion.2), channel_id=1, source_target_pairs={{0,8},{8,16},{16,24},{24,32},{32,40},{40,48},{48,56},{56,64},{64,7... | collective-permute-start | bytes 2359304 | tf_op jit(solution)/shard_map/ppermute | solution.py:26
  38.9 15.0 %all-to-all-start = ((bf16[96,8,256]{2,0,1:T(8,128)(2,1)}), bf16[96,8,256]{2,0,1:T(8,128)(2,1)S(1)}, u32[]{:S(2)}, u32[]{:S(2)}) async-start(bf16[96,8,256]{2,0,1:T(8,128)(2,1)} %bitcast.84), calls=%async_computation | async-start | bytes 786432 | tf_op jit(solution)/shard_map/all_to_all | solution.py:102
  53.9 13.6 %all-to-all-start.3 = ((bf16[96,8,256]{2,0,1:T(8,128)(2,1)}), bf16[96,8,256]{2,0,1:T(8,128)(2,1)S(1)}, u32[]{:S(2)}, u32[]{:S(2)}) async-start(bf16[96,8,256]{2,0,1:T(8,128)(2,1)} %bitcast.81), calls=%async_computation.3 | async-start | bytes 786432 | tf_op jit(solution)/shard_map/all_to_all | solution.py:107
  139.9 27.8 %copy-start.3 = (bf16[37,64,512]{2,1,0:T(8,128)(2,1)S(1)}, bf16[37,64,512]{2,1,0:T(8,128)(2,1)}, u32[]{:S(2)}) copy-start(bf16[37,64,512]{2,1,0:T(8,128)(2,1)} %copy-done.2) | copy-start | bytes 7274500 | tf_op jit(solution)/shard_map/while
  139.9 27.8 %copy-start.5 = (bf16[12,64,256]{2,1,0:T(8,128)(2,1)S(1)}, bf16[12,64,256]{2,1,0:T(8,128)(2,1)}, u32[]{:S(2)}) copy-start(bf16[12,64,256]{2,1,0:T(8,128)(2,1)} %copy-done.4) | copy-start | bytes 1179652 | tf_op jit(solution)/shard_map/while
  139.9 27.8 %copy-start.7 = (bf16[12,64,256]{2,1,0:T(8,128)(2,1)S(1)}, bf16[12,64,256]{2,1,0:T(8,128)(2,1)}, u32[]{:S(2)}) copy-start(bf16[12,64,256]{2,1,0:T(8,128)(2,1)} %copy-done.6) | copy-start | bytes 1179652 | tf_op jit(solution)/shard_map/while
  167.7 8.5 %copy-start.2 = (bf16[37,64,512]{2,1,0:T(8,128)(2,1)}, bf16[37,64,512]{2,1,0:T(8,128)(2,1)S(1)}, u32[]{:S(2)}) copy-start(bf16[37,64,512]{2,1,0:T(8,128)(2,1)S(1)} %get-tuple-element.257) | copy-start | bytes 7274500 | tf_op jit(solution)/shard_map/while
  167.7 8.5 %copy-start.4 = (bf16[12,64,256]{2,1,0:T(8,128)(2,1)}, bf16[12,64,256]{2,1,0:T(8,128)(2,1)S(1)}, u32[]{:S(2)}) copy-start(bf16[12,64,256]{2,1,0:T(8,128)(2,1)S(1)} %get-tuple-element.255) | copy-start | bytes 1179652 | tf_op jit(solution)/shard_map/while
  237.4 27.7 %copy-start.3 = (bf16[37,64,512]{2,1,0:T(8,128)(2,1)S(1)}, bf16[37,64,512]{2,1,0:T(8,128)(2,1)}, u32[]{:S(2)}) copy-start(bf16[37,64,512]{2,1,0:T(8,128)(2,1)} %copy-done.2) | copy-start | bytes 7274500 | tf_op jit(solution)/shard_map/while
  237.4 27.7 %copy-start.5 = (bf16[12,64,256]{2,1,0:T(8,128)(2,1)S(1)}, bf16[12,64,256]{2,1,0:T(8,128)(2,1)}, u32[]{:S(2)}) copy-start(bf16[12,64,256]{2,1,0:T(8,128)(2,1)} %copy-done.4) | copy-start | bytes 1179652 | tf_op jit(solution)/shard_map/while
  237.4 27.7 %copy-start.7 = (bf16[12,64,256]{2,1,0:T(8,128)(2,1)S(1)}, bf16[12,64,256]{2,1,0:T(8,128)(2,1)}, u32[]{:S(2)}) copy-start(bf16[12,64,256]{2,1,0:T(8,128)(2,1)} %copy-done.6) | copy-start | bytes 1179652 | tf_op jit(solution)/shard_map/while
  265.1 8.5 %copy-start.2 = (bf16[37,64,512]{2,1,0:T(8,128)(2,1)}, bf16[37,64,512]{2,1,0:T(8,128)(2,1)S(1)}, u32[]{:S(2)}) copy-start(bf16[37,64,512]{2,1,0:T(8,128)(2,1)S(1)} %get-tuple-element.257) | copy-start | bytes 7274500 | tf_op jit(solution)/shard_map/while
  265.1 8.5 %copy-start.4 = (bf16[12,64,256]{2,1,0:T(8,128)(2,1)}, bf16[12,64,256]{2,1,0:T(8,128)(2,1)S(1)}, u32[]{:S(2)}) copy-start(bf16[12,64,256]{2,1,0:T(8,128)(2,1)S(1)} %get-tuple-element.255) | copy-start | bytes 1179652 | tf_op jit(solution)/shard_map/while
  334.8 27.7 %copy-start.3 = (bf16[37,64,512]{2,1,0:T(8,128)(2,1)S(1)}, bf16[37,64,512]{2,1,0:T(8,128)(2,1)}, u32[]{:S(2)}) copy-start(bf16[37,64,512]{2,1,0:T(8,128)(2,1)} %copy-done.2) | copy-start | bytes 7274500 | tf_op jit(solution)/shard_map/while
  334.8 27.7 %copy-start.5 = (bf16[12,64,256]{2,1,0:T(8,128)(2,1)S(1)}, bf16[12,64,256]{2,1,0:T(8,128)(2,1)}, u32[]{:S(2)}) copy-start(bf16[12,64,256]{2,1,0:T(8,128)(2,1)} %copy-done.4) | copy-start | bytes 1179652 | tf_op jit(solution)/shard_map/while
  334.8 27.7 %copy-start.7 = (bf16[12,64,256]{2,1,0:T(8,128)(2,1)S(1)}, bf16[12,64,256]{2,1,0:T(8,128)(2,1)}, u32[]{:S(2)}) copy-start(bf16[12,64,256]{2,1,0:T(8,128)(2,1)} %copy-done.6) | copy-start | bytes 1179652 | tf_op jit(solution)/shard_map/while
  362.5 8.5 %copy-start.2 = (bf16[37,64,512]{2,1,0:T(8,128)(2,1)}, bf16[37,64,512]{2,1,0:T(8,128)(2,1)S(1)}, u32[]{:S(2)}) copy-start(bf16[37,64,512]{2,1,0:T(8,128)(2,1)S(1)} %get-tuple-element.257) | copy-start | bytes 7274500 | tf_op jit(solution)/shard_map/while
  362.5 8.5 %copy-start.4 = (bf16[12,64,256]{2,1,0:T(8,128)(2,1)}, bf16[12,64,256]{2,1,0:T(8,128)(2,1)S(1)}, u32[]{:S(2)}) copy-start(bf16[12,64,256]{2,1,0:T(8,128)(2,1)S(1)} %get-tuple-element.255) | copy-start | bytes 1179652 | tf_op jit(solution)/shard_map/while
  432.1 27.6 %copy-start.3 = (bf16[37,64,512]{2,1,0:T(8,128)(2,1)S(1)}, bf16[37,64,512]{2,1,0:T(8,128)(2,1)}, u32[]{:S(2)}) copy-start(bf16[37,64,512]{2,1,0:T(8,128)(2,1)} %copy-done.2) | copy-start | bytes 7274500 | tf_op jit(solution)/shard_map/while
  432.1 27.6 %copy-start.5 = (bf16[12,64,256]{2,1,0:T(8,128)(2,1)S(1)}, bf16[12,64,256]{2,1,0:T(8,128)(2,1)}, u32[]{:S(2)}) copy-start(bf16[12,64,256]{2,1,0:T(8,128)(2,1)} %copy-done.4) | copy-start | bytes 1179652 | tf_op jit(solution)/shard_map/while
  432.1 27.6 %copy-start.7 = (bf16[12,64,256]{2,1,0:T(8,128)(2,1)S(1)}, bf16[12,64,256]{2,1,0:T(8,128)(2,1)}, u32[]{:S(2)}) copy-start(bf16[12,64,256]{2,1,0:T(8,128)(2,1)} %copy-done.6) | copy-start | bytes 1179652 | tf_op jit(solution)/shard_map/while
  462.4 11.4 %copy-start.10 = (bf16[4,3,64,256]{3,2,1,0:T(8,128)(2,1)S(1)}, bf16[4,3,64,256]{3,2,1,0:T(8,128)(2,1)}, u32[]{:S(2)}) copy-start(bf16[4,3,64,256]{3,2,1,0:T(8,128)(2,1)} %get-tuple-element.98) | copy-start | bytes 1179652
  462.5 32.7 %collective-permute-start.2 = (bf16[12,64,512]{2,1,0:T(8,128)(2,1)S(1)}, bf16[12,64,512]{2,1,0:T(8,128)(2,1)S(1)}, u32[]{:S(2)}, u32[]{:S(2)}) collective-permute-start(bf16[12,64,512]{2,1,0:T(8,128)(2,1)S(1)} %get-tuple-element.132), channel_id=1, source_target_pairs={{0,8},{8,16},{16,24},{24,32},{32,40},{40,48},{48,56},{56,64},{64,7... | collective-permute-start | bytes 2359304 | tf_op jit(solution)/shard_map/ppermute | solution.py:38
  471.9 23.3 %collective-permute-start.3 = (bf16[12,64,512]{2,1,0:T(8,128)(2,1)S(1)}, bf16[12,64,512]{2,1,0:T(8,128)(2,1)}, u32[]{:S(2)}, u32[]{:S(2)}) collective-permute-start(bf16[12,64,512]{2,1,0:T(8,128)(2,1)S(1)} %get-tuple-element.133), channel_id=1, source_target_pairs={{8,0},{16,8},{24,16},{32,24},{40,32},{48,40},{56,48},{64,56},{72,6... | collective-permute-start | bytes 2359304 | tf_op jit(solution)/shard_map/ppermute | solution.py:38
  489.8 14.9 %all-to-all-start.5 = ((bf16[8,96,256]{2,1,0:T(8,128)(2,1)}), bf16[8,96,256]{2,1,0:T(8,128)(2,1)S(1)}, u32[]{:S(2)}, u32[]{:S(2)}) async-start(bf16[8,96,256]{2,1,0:T(8,128)(2,1)} %bitcast.22), calls=%async_computation.5 | async-start | bytes 786432 | tf_op jit(solution)/shard_map/all_to_all | solution.py:175
  516.9 12.9 %all-to-all-start.7 = ((bf16[8,96,256]{2,1,0:T(8,128)(2,1)}), bf16[8,96,256]{2,1,0:T(8,128)(2,1)S(1)}, u32[]{:S(2)}, u32[]{:S(2)}) async-start(bf16[8,96,256]{2,1,0:T(8,128)(2,1)} %bitcast.27), calls=%async_computation.7 | async-start | bytes 786432 | tf_op jit(solution)/shard_map/all_to_all | solution.py:177
  (14 other events, 61.3 us)
where the time goes:
time: 539 us; the launch traced here: 531 us
  local copies, waits for them, and re-layouts  209 us (39%)
  other arithmetic  171 us (32%)
  waiting for transfers between devices  49.8 us (9%)
  starting transfers between devices  43.5 us (8%)
  blocking collectives  28.2 us (5%)
  matrix products  24.3 us (5%)
    scatter-add x4, other arithmetic, own_step(): grad_buffer.at[index_blk]  111 us
    concatenate x8, local copies, waits for them, and re-layouts, pair_grads(): jnp.concatenate([grad_key.reshape(block_tiles, key_len, -1), grad_value.r...  64.8 us
    gather x8, local copies, waits for them, and re-layouts, near_pairs(): jnp.take(pair_tiles, index_blk, axis=0)  55.1 us
    concatenate x4, other arithmetic, pair_grads(): jnp.concatenate([grad_key.reshape(block_tiles, key_len, -1), grad_value.r...  40.2 us
    transpose x4, local copies, waits for them, and re-layouts, pair_grads(): jnp.einsum('bntk,btnd->bknd', probs_low, cot_heads, preferred_element_typ...  29.9 us
    transpose x4, local copies, waits for them, and re-layouts, pair_grads(): jnp.einsum('bntk,btnd->bknd', grad_score, query_heads, preferred_element_...  29.9 us
    all_to_all x1, blocking collectives, shards(): lax.all_to_all(output_rows, 'head', split_axis=0, concat_axis=1, tiled=True)  16 us
    all_to_all x1, blocking collectives, shards(): lax.all_to_all(grad_key_rows, 'head', split_axis=0, concat_axis=1, tiled=...  12.2 us
  transfers between devices with their start and end apart: 10, of which 6 were waited for; matrix products, arithmetic and copies ran while one was open for 2% of the time, Pallas kernels for 0%

commit v1 on v0

v1 whole, which is shorter than its diff:
```python
import functools
import math

import jax
import jax.numpy as jnp
from jax import lax
from jax.experimental import pallas as pl
from jax.experimental.pallas import tpu as pltpu
from jax.sharding import Mesh, PartitionSpec as P

TILE = 64
TILES_F = 12
HD = 128
FRAME = TILE * TILES_F
BLOCK = 4 * TILE
SLOTS_F = 5
CHUNKS = 8
CHUNK = FRAME // CHUNKS
PLANE = 16
MASKED = -1e30
SCALE = 1.0 / math.sqrt(HD)
LOG2E = 1.4426950408889634
ANY = pl.BlockSpec(memory_space=pl.ANY)
F32 = jnp.float32
BF16 = jnp.bfloat16


def pack_kernel(q_ref, k_ref, v_ref, c_ref, out_ref):
    for a, ref in enumerate((q_ref, k_ref, v_ref, c_ref)):
        for g in range(PLANE):
            out_ref[g, a] = ref[:, g * HD : (g + 1) * HD]


def pack(q, k, v, c):
    return pl.pallas_call(
        pack_kernel,
        out_shape=jax.ShapeDtypeStruct((PLANE, 4, CHUNK, HD), BF16),
        name="pack",
    )(q, k, v, c)


def unpack_kernel(in_ref, *out_refs):
    for a, ref in enumerate(out_refs):
        for g in range(PLANE):
            ref[:, g * HD : (g + 1) * HD] = in_ref[g, a]


def unpack(packed):
    shape = jax.ShapeDtypeStruct((CHUNK, PLANE * HD), BF16)
    return pl.pallas_call(unpack_kernel, out_shape=(shape,) * 4, name="unpack")(packed)


def nt(a, b):
    return lax.dot_general(a, b, (((1,), (1,)), ((), ())), preferred_element_type=F32)


def nn(a, b):
    return lax.dot_general(a, b, (((1,), (0,)), ((), ())), preferred_element_type=F32)


def tn(a, b):
    return lax.dot_general(a, b, (((0,), (0,)), ((), ())), preferred_element_type=F32)


def group_rows(x):
    return x.reshape(x.shape[0] // 8, 8, x.shape[1])


def attend_kernel(
    core_ref, mine_ref, swap_ref, edge_ref, bias_ref,
    packed_ref, gswap_ref, gedge_ref, gown_ref,
    q_s, c_s, k_s, v_s, s_s, p_s, d_s, o_s, dq_s, dk_s, dv_s, gb_s, sems, out_sems,
):
    core = core_ref[0]

    def copy(src, dst, n):
        return pltpu.make_async_copy(src, dst, sems.at[n])

    def mine(frame, a):
        return mine_ref.at[pl.ds(frame * CHUNKS, CHUNKS), a]

    fixed = []
    for f in range(2):
        fixed.append(copy(mine(f, 0), q_s.at[f], f))
        fixed.append(copy(mine(f, 3), c_s.at[f], 2 + f))
        fixed.append(copy(mine(f, 1), k_s.at[1 + 2 * f], 4 + f))
        fixed.append(copy(mine(f, 2), v_s.at[1 + 2 * f], 6 + f))
    for cp in fixed:
        cp.start()

    def halo_copies(which):
        slots = ((2, 4), 0) if which == 0 else ((0, 2), 4)
        cps = []
        for a, dst in enumerate((k_s, v_s)):
            for f in range(2):
                src = swap_ref.at[pl.ds(f * CHUNKS, CHUNKS), a]
                cps.append(copy(src, dst.at[slots[0][f]], 8 + 2 * a + f))
            cps.append(copy(edge_ref.at[:, a], dst.at[slots[1]], 12 + a))
        return cps

    for which in range(2):
        @pl.when(core == which)
        def _():
            for cp in halo_copies(which):
                cp.start()

    dk_s[...] = jnp.zeros_like(dk_s)
    dv_s[...] = jnp.zeros_like(dv_s)
    for cp in fixed:
        cp.wait()
    for cp in halo_copies(0):
        cp.wait()

    qf = q_s.reshape(2 * FRAME, HD)
    cf = c_s.reshape(2 * FRAME, HD)
    kf = k_s.reshape(SLOTS_F * FRAME, HD)
    vf = v_s.reshape(SLOTS_F * FRAME, HD)
    of = o_s.reshape(2 * FRAME, HD)
    dqf = dq_s.reshape(2 * FRAME, HD)

    def frame_step(f, carry):
        for r in range(3):
            lo, n = ((0, 2 * BLOCK), (0, 3 * BLOCK), (BLOCK, 2 * BLOCK))[r]
            rows = pl.ds(pl.multiple_of(f * FRAME + r * BLOCK, BLOCK), BLOCK)
            q = qf[rows, :]
            c = cf[rows, :]

            def keys(s):
                return pl.ds(pl.multiple_of((2 * f + s) * FRAME + lo, BLOCK), n)

            top = None
            for s in range(3):
                st = nt(kf[keys(s), :], q)
                for t in range(n // TILE):
                    tile = (2 * f + s) * TILES_F + lo // TILE + t
                    x = st[t * TILE : (t + 1) * TILE] + bias_ref[pl.ds(tile, 1), pl.ds(pl.multiple_of(f * FRAME + r * BLOCK, BLOCK), BLOCK)]
                    s_s[s * n + t * TILE : s * n + (t + 1) * TILE, :] = x
                    part = jnp.max(group_rows(x), axis=0)
                    top = part if top is None else jnp.maximum(top, part)
            top = jnp.max(top, axis=0, keepdims=True) * (SCALE * LOG2E)
            total = jnp.zeros((8, BLOCK), F32)
            for t in range(3 * n // TILE):
                sl = slice(t * TILE, (t + 1) * TILE)
                e = jnp.exp2(s_s[sl, :] * (SCALE * LOG2E) - top)
                s_s[sl, :] = e
                total = total + jnp.sum(group_rows(e), axis=0)
            inv = 1.0 / jnp.sum(total, axis=0, keepdims=True)
            for t in range(3 * n // TILE):
                sl = slice(t * TILE, (t + 1) * TILE)
                p_s[sl, :] = (s_s[sl, :] * inv).astype(BF16)
            o = None
            for s in range(3):
                part = tn(p_s[s * n : (s + 1) * n, :], vf[keys(s), :])
                o = part if o is None else o + part
            o = o.astype(BF16)
            of[rows, :] = o
            dots = jnp.sum((c.astype(F32) * o.astype(F32)).T, axis=0, keepdims=True)
            inv_scale = inv * SCALE
            dq = None
            for s in range(3):
                dp = nt(vf[keys(s), :], c)
                for t in range(n // TILE):
                    sl = slice(s * n + t * TILE, s * n + (t + 1) * TILE)
                    d_s[sl, :] = (s_s[sl, :] * inv_scale * (dp[t * TILE : (t + 1) * TILE] - dots)).astype(BF16)
                dv_s[keys(s), :] += nn(p_s[s * n : (s + 1) * n, :], c)
                dk_s[keys(s), :] += nn(d_s[s * n : (s + 1) * n, :], q)
                part = tn(d_s[s * n : (s + 1) * n, :], kf[keys(s), :])
                dq = part if dq is None else dq + part
            dqf[rows, :] = dq.astype(BF16)
        return carry

    lax.fori_loop(0, 2, frame_step, 0)

    outs = []

    def out_copy(src, dst):
        cp = pltpu.make_async_copy(src, dst, out_sems.at[len(outs)])
        cp.start()
        outs.append(cp)

    for f in range(2):
        out_copy(o_s.at[f], packed_ref.at[pl.ds(f * CHUNKS, CHUNKS), 0])
        out_copy(dq_s.at[f], packed_ref.at[pl.ds(f * CHUNKS, CHUNKS), 1])
    for a, acc in enumerate((dk_s, dv_s)):
        for f in range(2):
            out_copy(acc.at[pl.ds((1 + 2 * f) * FRAME, FRAME)], gown_ref.at[f, a])
        for i, first in enumerate((2, 4)):
            slot = first - 2 * core
            gb_s[a, i] = acc[pl.ds(pl.multiple_of(slot * FRAME, FRAME), FRAME), :].astype(BF16)
            out_copy(gb_s.at[a, i], gswap_ref.at[i, a])
        gb_s[a, 2] = acc[pl.ds(pl.multiple_of(4 * core * FRAME, FRAME), FRAME), :].astype(BF16)
        out_copy(gb_s.at[a, 2], gedge_ref.at[a])
    for cp in outs:
        cp.wait()


def attend(core, mine, swap, edge, bias):
    tokens = 2 * FRAME
    return pl.pallas_call(
        attend_kernel,
        in_specs=[pl.BlockSpec(memory_space=pltpu.SMEM), ANY, ANY, ANY, pl.BlockSpec(memory_space=pltpu.VMEM)],
        out_specs=(ANY,) * 4,
        out_shape=(
            jax.ShapeDtypeStruct((PLANE, 4, CHUNK, HD), BF16),
            jax.ShapeDtypeStruct((2, 2, FRAME, HD), BF16),
            jax.ShapeDtypeStruct((2, FRAME, HD), BF16),
            jax.ShapeDtypeStruct((2, 2, FRAME, HD), F32),
        ),
        scratch_shapes=[
            pltpu.VMEM((2, CHUNKS, CHUNK, HD), BF16),
            pltpu.VMEM((2, CHUNKS, CHUNK, HD), BF16),
            pltpu.VMEM((SLOTS_F, CHUNKS, CHUNK, HD), BF16),
            pltpu.VMEM((SLOTS_F, CHUNKS, CHUNK, HD), BF16),
            pltpu.VMEM((9 * BLOCK, BLOCK), F32),
            pltpu.VMEM((9 * BLOCK, BLOCK), BF16),
            pltpu.VMEM((9 * BLOCK, BLOCK), BF16),
            pltpu.VMEM((2, CHUNKS, CHUNK, HD), BF16),
            pltpu.VMEM((2, CHUNKS, CHUNK, HD), BF16),
            pltpu.VMEM((SLOTS_F * FRAME, HD), F32),
            pltpu.VMEM((SLOTS_F * FRAME, HD), F32),
            pltpu.VMEM((2, 3, FRAME, HD), BF16),
            pltpu.SemaphoreType.DMA((14,)),
            pltpu.SemaphoreType.DMA((14,)),
        ],
        name="attend",
    )(core, mine, swap, edge, bias)


def join_kernel(core_ref, packed_ref, own_ref, swap_ref, edge_ref, out_ref, sum_s, sems):
    core = core_ref[0]
    outs = []
    for f in range(2):
        here = jnp.where(core == f, 1.0, 0.0)
        for a in range(2):
            for h in range(CHUNKS):
                sl = slice(h * CHUNK, (h + 1) * CHUNK)
                x = own_ref[f, a, sl, :] + swap_ref[f, a, sl, :].astype(F32)
                x = x + edge_ref[a, sl, :].astype(F32) * here
                sum_s[f, a, h] = x.astype(BF16)
            cp = pltpu.make_async_copy(
                sum_s.at[f, a], out_ref.at[pl.ds(f * CHUNKS, CHUNKS), 2 + a], sems.at[2 * f + a]
            )
            cp.start()
            outs.append(cp)
    for cp in outs:
        cp.wait()


def join(core, packed, own, swap, edge):
    vmem = pl.BlockSpec(memory_space=pltpu.VMEM)
    return pl.pallas_call(
        join_kernel,
        in_specs=[pl.BlockSpec(memory_space=pltpu.SMEM), ANY, vmem, vmem, vmem],
        out_specs=ANY,
        out_shape=jax.ShapeDtypeStruct((PLANE, 4, CHUNK, HD), BF16),
        scratch_shapes=[pltpu.VMEM((2, 2, CHUNKS, CHUNK, HD), BF16), pltpu.SemaphoreType.DMA((4,))],
        input_output_aliases={1: 0},
        name="join",
    )(core, packed, own, swap, edge)


def tile_bias(neighbours, first, base):
    rows = jnp.concatenate(
        [lax.dynamic_slice_in_dim(neighbours, first + 2 * f * TILES_F, TILES_F, 0) for f in range(2)], axis=0
    )
    rel = jnp.where(rows >= 0, rows - base, -1)
    tiles = jnp.arange(SLOTS_F * TILES_F, dtype=jnp.int32)
    hit = jnp.any(rel[None, :, :] == tiles[:, None, None], axis=2)
    return jnp.repeat(jnp.where(hit, 0.0, MASKED).astype(F32), TILE, axis=1)


def shards(queries, keys, values, cotangent, neighbours):
    plane = ("yl", "head")
    ring = lax.axis_size("sx")
    across = []
    for i in range(ring - 1):
        across.append((2 * i + 1, 2 * i + 2))
        across.append((2 * i + 2, 2 * i + 1))
    swap_pairs = [(0, 1), (1, 0)]
    core = lax.axis_index("co")
    x = lax.axis_index("sx")
    first = (4 * x + core) * TILES_F
    bias = tile_bias(neighbours, first, first - TILES_F)
    core_arr = jnp.full((1,), core, jnp.int32)

    mine = lax.all_to_all(pack(queries, keys, values, cotangent), plane, split_axis=0, concat_axis=0, tiled=True)
    kv = mine[:, 1:3]
    kv_edge = lax.dynamic_slice_in_dim(kv, core * CHUNKS, CHUNKS, 0)
    edge = lax.ppermute(kv_edge, ("sx", "co"), across)
    swap = lax.ppermute(kv, "co", swap_pairs)
    packed, gswap, gedge, gown = attend(core_arr, mine, swap, edge, bias)
    gedge_in = lax.ppermute(gedge, ("sx", "co"), across)
    gswap_in = lax.ppermute(gswap, "co", swap_pairs)
    packed = join(core_arr, packed, gown, gswap_in, gedge_in)
    return unpack(lax.all_to_all(packed, plane, split_axis=0, concat_axis=0, tiled=True))


def solution(mesh):
    view = Mesh(mesh.devices.reshape(mesh.devices.shape[0] // 4, 2, 2, -1), ("sx", "yl", "co", "head"))
    rows = P(("sx", "yl", "co", "head"), None)
    return jax.shard_map(
        shards,
        mesh=view,
        in_specs=(rows,) * 4 + (P(),),
        out_specs=(rows,) * 4,
        check_vma=False,
    )
```

time: 539 us -> 106 us (0.20); the launches traced: 531 us -> 106 us
  local copies, waits for them, and re-layouts: 209 us -> 3.04 us
  other arithmetic: 171 us -> 0.24 us
  starting transfers between devices: 43.5 us -> 4.15 us
  waiting for transfers between devices: 49.8 us -> 13.1 us
  blocking collectives: 28.2 us -> 57.8 us
  Pallas kernels: 0 us -> 26.8 us
  matrix products: 24.3 us -> 0 us
    scatter-add x4 -> x0, other arithmetic: 111 us -> none  [own_step(): grad_buffer.at[index_blk]]
    concatenate x9 -> x0, local copies, waits for them, and re-layouts: 65 us -> none  [the longest x8 64.8 us: pair_grads(): jnp.concatenate([grad_key.reshape(block_tiles, key_len, -1), grad_value.r...]
    transpose x8 -> x0, local copies, waits for them, and re-layouts: 59.9 us -> none  [the longest x4 29.9 us: pair_grads(): jnp.einsum('bntk,btnd->bknd', probs_low, cot_heads, preferred_element_typ...]
    gather x9 -> x0, local copies, waits for them, and re-layouts: 55.7 us -> none  [the longest x8 55.1 us: near_pairs(): jnp.take(pair_tiles, index_blk, axis=0)]
    all_to_all x6 -> x0, waiting for transfers between devices: 49.8 us -> none  [the longest x1 9.85 us: shards(): lax.all_to_all(queries, 'head', split_axis=1, concat_axis=0, tiled=True)]
    concatenate x6 -> x0, other arithmetic: 41.3 us -> none  [the longest x4 40.2 us: pair_grads(): jnp.concatenate([grad_key.reshape(block_tiles, key_len, -1), grad_value.r...]
    all_to_all x2, blocking collectives: 28.2 us -> 57.8 us  [the longest x1 30.4 us: shards(): lax.all_to_all(pack(queries, keys, values, cotangent), plane, split_axis=...]
    all_to_all x6 -> x0, starting transfers between devices: 28 us -> none  [the longest x1 8.08 us: shards(): lax.all_to_all(keys, 'head', split_axis=1, concat_axis=0, tiled=True)]
  transfers between devices with their start and end apart: 10 -> 4, of which waited for: 6 -> 2; matrix products, arithmetic and copies ran while one was open for 2% -> 2% of each run, Pallas kernels for 0% -> 0%
where the time goes in v1:
time: 106 us
  blocking collectives  57.8 us (55%)
  Pallas kernels  26.8 us (25%)
  waiting for transfers between devices  13.1 us (12%)
  starting transfers between devices  4.15 us (4%)
  local copies, waits for them, and re-layouts  3.04 us (3%)
    all_to_all x1, blocking collectives, shards(): lax.all_to_all(pack(queries, keys, values, cotangent), plane, split_axis=...  30.4 us
    all_to_all x1, blocking collectives, shards(): lax.all_to_all(packed, plane, split_axis=0, concat_axis=0, tiled=True)  27.5 us
    pallas_call x1, Pallas kernels, attend(): pl.pallas_call(attend_kernel, in_specs=[pl.BlockSpec(memory_space=pltpu.S...  18.4 us
    ppermute x1, waiting for transfers between devices, shards(): gedge_in = lax.ppermute(gedge, ('sx', 'co'), across)  7.38 us
    ppermute x1, waiting for transfers between devices, shards(): edge = lax.ppermute(kv_edge, ('sx', 'co'), across)  5.68 us
    pallas_call x1, Pallas kernels, unpack(): pl.pallas_call(unpack_kernel, out_shape=(shape,) * 4, name='unpack')(packed)  2.91 us
    pallas_call x1, Pallas kernels, pack(): pl.pallas_call(pack_kernel, out_shape=jax.ShapeDtypeStruct((PLANE, 4, CHU...  2.77 us
    pallas_call x1, Pallas kernels, join(): pl.pallas_call(join_kernel, in_specs=[pl.BlockSpec(memory_space=pltpu.SME...  2.73 us
  transfers between devices with their start and end apart: 4, of which 2 were waited for; matrix products, arithmetic and copies ran while one was open for 2% of the time, Pallas kernels for 0%

profile of v1, /device:TPU:2, one launch (start us, length us, event | category | flops | bytes accessed | tf_op | source)
XLA Modules:
  0.0 105.8 jit_solution(1934632161182829510)
XLA Ops:
  0.6 2.8 %pack.1 = bf16[16,4,96,128]{3,2,1,0:T(8,128)(2,1)} custom-call(bf16[96,2048]{1,0:T(8,128)(2,1)} %q_ref.1, bf16[96,2048]{1,0:T(8,128)(2,1)} %k_ref.1, bf16[96,2048]{1,0:T(8,128)(2,1)} %v_ref.1, bf16[96,2048]{1,0:T(8,128)(2,1)} %c_ref.1), custom_call_target="tpu_custom_call" | custom-call | tf_op jit(solution)/shard_map/pack/pallas_call | solution.py:35
  3.4 30.4 %all_to_all.10.mine_ref = bf16[16,4,96,128]{3,2,1,0:T(8,128)(2,1)S(1)} all-to-all(bf16[16,4,96,128]{3,2,1,0:T(8,128)(2,1)} %pack.1), channel_id=1, replica_groups=mesh['sx'=4,'yl'=2,'co'=2,'head'=8] {'yl','head'}, dimensions={0} | all-to-all | bytes 3145728 | tf_op jit(solution)/shard_map/all_to_all | solution.py:286
  33.8 0.0 copy-start
  33.8 0.0 copy-start.3
  33.8 0.1 slice.4
  33.8 0.1 collective-permute-start
  33.9 0.6 copy-done.3
  34.5 0.1 constant_dynamic-slice_fusion.1
  34.6 2.0 %collective-permute-start.1 = (bf16[8,2,96,128]{3,2,1,0:T(8,128)(2,1)S(1)}, bf16[8,2,96,128]{3,2,1,0:T(8,128)(2,1)}, u32[]{:S(2)}, u32[]{:S(2)}) collective-permute-start(bf16[8,2,96,128]{3,2,1,0:T(8,128)(2,1)S(1)} %constant_dynamic-slice_fusion.2), channel_id=1, source_target_pairs={{8,32},{32,8},{40,64},{64,40},{72,96},{96,72},{9,33},{33,9},{41,65... | collective-permute-start | bytes 1179656 | tf_op jit(solution)/shard_map/ppermute | solution.py:289
  36.6 0.1 subtract_select_fusion
  36.7 0.2 fusion
  36.8 0.1 copy.11
  36.9 0.2 broadcast_in_dim.24
  37.2 0.0 copy-done
  37.2 0.9 reshape.40.bias_ref
  38.2 5.7 %collective-permute-done.1.edge_ref = bf16[8,2,96,128]{3,2,1,0:T(8,128)(2,1)} collective-permute-done((bf16[8,2,96,128]{3,2,1,0:T(8,128)(2,1)S(1)}, bf16[8,2,96,128]{3,2,1,0:T(8,128)(2,1)}, u32[]{:S(2)}, u32[]{:S(2)}) %collective-permute-start.1) | collective-permute-done | bytes 393248 | tf_op jit(solution)/shard_map/ppermute | solution.py:289
  43.8 0.0 collective-permute-done.swap_ref
  43.8 18.4 %attend.1 = (bf16[16,4,96,128]{3,2,1,0:T(8,128)(2,1)}, bf16[2,2,768,128]{3,2,1,0:T(8,128)(2,1)}, bf16[2,768,128]{2,1,0:T(8,128)(2,1)}, f32[2,2,768,128]{3,2,1,0:T(8,128)}) custom-call(s32[1]{0:T(128)} %bitcast.core_ref, bf16[16,4,96,128]{3,2,1,0:T(8,128)(2,1)} %copy-done, bf16[16,2,96,128]{3,2,1,0:T(8,128)(2,1)} %collective-permute-done.swap_ref, ...), custom_call_target="tpu_custom_call" | custom-call | tf_op jit(solution)/shard_map/attend/pallas_call | solution.py:199
  62.2 0.2 collective-permute-start.2
  62.4 1.9 %collective-permute-start.3 = (bf16[2,768,128]{2,1,0:T(8,128)(2,1)}, bf16[2,768,128]{2,1,0:T(8,128)(2,1)S(1)}, u32[]{:S(2)}, u32[]{:S(2)}) collective-permute-start(bf16[2,768,128]{2,1,0:T(8,128)(2,1)} %get-tuple-element.11), channel_id=1, source_target_pairs={{8,32},{32,8},{40,64},{64,40},{72,96},{96,72},{9,33},{33,9},{41,65... | collective-permute-start | bytes 1179656 | tf_op jit(solution)/shard_map/ppermute | solution.py:292
  64.3 7.4 %collective-permute-done.3.edge_ref = bf16[2,768,128]{2,1,0:T(8,128)(2,1)S(1)} collective-permute-done((bf16[2,768,128]{2,1,0:T(8,128)(2,1)}, bf16[2,768,128]{2,1,0:T(8,128)(2,1)S(1)}, u32[]{:S(2)}, u32[]{:S(2)}) %collective-permute-start.3) | collective-permute-done | bytes 393248 | tf_op jit(solution)/shard_map/ppermute | solution.py:292
  71.7 0.0 copy-start.2
  71.7 0.0 collective-permute-done.2.swap_ref
  71.7 0.0 copy-start.1
  71.7 0.7 copy-done.2
  72.5 0.3 copy-done.1
  72.7 2.7 %join.1 = bf16[16,4,96,128]{3,2,1,0:T(8,128)(2,1)} custom-call(s32[1]{0:T(128)} %bitcast.core_ref, bf16[16,4,96,128]{3,2,1,0:T(8,128)(2,1)} %get-tuple-element.8.packed_ref, f32[2,2,768,128]{3,2,1,0:T(8,128)} %get-tuple-element.9.own_ref, bf16[2,2,768,128]{3,2,1,0:T(8,128)(2,1)} %copy-done.1, ...), custom_call_target="tpu_custom_call", output_to_operand_aliasing={{}: (1, {})} | custom-call | tf_op jit(solution)/shard_map/join/pallas_call | solution.py:251
  75.4 27.5 %all_to_all.11.in_ref = bf16[16,4,96,128]{3,2,1,0:T(8,128)(2,1)} all-to-all(bf16[16,4,96,128]{3,2,1,0:T(8,128)(2,1)} %join.1), channel_id=1, replica_groups=mesh['sx'=4,'yl'=2,'co'=2,'head'=8] {'yl','head'}, dimensions={0} | all-to-all | bytes 3145728 | tf_op jit(solution)/shard_map/all_to_all | solution.py:295
  102.9 2.9 %unpack.1 = (bf16[96,2048]{1,0:T(8,128)(2,1)}, bf16[96,2048]{1,0:T(8,128)(2,1)}, bf16[96,2048]{1,0:T(8,128)(2,1)}, bf16[96,2048]{1,0:T(8,128)(2,1)}) custom-call(bf16[16,4,96,128]{3,2,1,0:T(8,128)(2,1)} %all_to_all.11.in_ref), custom_call_target="tpu_custom_call" | custom-call | tf_op jit(solution)/shard_map/unpack/pallas_call | solution.py:50
  (2 shorter events, 0.0 us)
Async XLA Ops:
  33.8 3.4 %copy-start = (bf16[16,4,96,128]{3,2,1,0:T(8,128)(2,1)}, bf16[16,4,96,128]{3,2,1,0:T(8,128)(2,1)S(1)}, u32[]{:S(2)}) copy-start(bf16[16,4,96,128]{3,2,1,0:T(8,128)(2,1)S(1)} %all_to_all.10.mine_ref) | copy-start | bytes 4718596
  33.8 0.8 copy-start.3
  33.8 10.0 %collective-permute-start = (bf16[16,2,96,128]{3,2,1,0:T(8,128)(2,1)S(1)}, bf16[16,2,96,128]{3,2,1,0:T(8,128)(2,1)}, u32[]{:S(2)}, u32[]{:S(2)}) collective-permute-start(bf16[16,2,96,128]{3,2,1,0:T(8,128)(2,1)S(1)} %slice.4), channel_id=1, source_target_pairs={{0,8},{8,0},{1,9},{9,1},{2,10},{10,2},{3,11},{11,3},{4,12},{12,4},... | collective-permute-start | bytes 2359304 | tf_op jit(solution)/shard_map/ppermute | solution.py:290
  34.6 9.2 %collective-permute-start.1 = (bf16[8,2,96,128]{3,2,1,0:T(8,128)(2,1)S(1)}, bf16[8,2,96,128]{3,2,1,0:T(8,128)(2,1)}, u32[]{:S(2)}, u32[]{:S(2)}) collective-permute-start(bf16[8,2,96,128]{3,2,1,0:T(8,128)(2,1)S(1)} %constant_dynamic-slice_fusion.2), channel_id=1, source_target_pairs={{8,32},{32,8},{40,64},{64,40},{72,96},{96,72},{9,33},{33,9},{41,65... | collective-permute-start | bytes 1179656 | tf_op jit(solution)/shard_map/ppermute | solution.py:289
  62.2 9.5 %collective-permute-start.2 = (bf16[2,2,768,128]{3,2,1,0:T(8,128)(2,1)}, bf16[2,2,768,128]{3,2,1,0:T(8,128)(2,1)S(1)}, u32[]{:S(2)}, u32[]{:S(2)}) collective-permute-start(bf16[2,2,768,128]{3,2,1,0:T(8,128)(2,1)} %get-tuple-element.10), channel_id=1, source_target_pairs={{0,8},{8,0},{1,9},{9,1},{2,10},{10,2},{3,11},{11,3},{4,12},{12,4},... | collective-permute-start | bytes 2359304 | tf_op jit(solution)/shard_map/ppermute | solution.py:293
  62.4 9.3 %collective-permute-start.3 = (bf16[2,768,128]{2,1,0:T(8,128)(2,1)}, bf16[2,768,128]{2,1,0:T(8,128)(2,1)S(1)}, u32[]{:S(2)}, u32[]{:S(2)}) collective-permute-start(bf16[2,768,128]{2,1,0:T(8,128)(2,1)} %get-tuple-element.11), channel_id=1, source_target_pairs={{8,32},{32,8},{40,64},{64,40},{72,96},{96,72},{9,33},{33,9},{41,65... | collective-permute-start | bytes 1179656 | tf_op jit(solution)/shard_map/ppermute | solution.py:292
  71.7 0.7 copy-start.2
  71.7 1.0 copy-start.1

commit v2 on v1

v2 whole, which is shorter than its diff:
```python
import functools
import math

import jax
import jax.numpy as jnp
from jax import lax
from jax.experimental import pallas as pl
from jax.experimental.pallas import tpu as pltpu
from jax.sharding import Mesh, PartitionSpec as P

TILE = 64
TILES_F = 12
HD = 128
FRAME = TILE * TILES_F
BLOCK = 4 * TILE
KEYS = 3 * FRAME
CHUNKS = 8
CHUNK = FRAME // CHUNKS
PLANE = 16
MASKED = -1e30
SCALE = 1.0 / math.sqrt(HD)
LOG2E = 1.4426950408889634
ANY = pl.BlockSpec(memory_space=pl.ANY)
F32 = jnp.float32
BF16 = jnp.bfloat16


def pack_kernel(q_ref, k_ref, v_ref, c_ref, out_ref):
    for a, ref in enumerate((q_ref, k_ref, v_ref, c_ref)):
        for g in range(PLANE):
            out_ref[g, a] = ref[:, g * HD : (g + 1) * HD]


def pack(q, k, v, c):
    return pl.pallas_call(
        pack_kernel,
        out_shape=jax.ShapeDtypeStruct((PLANE, 4, CHUNK, HD), BF16),
        name="pack",
    )(q, k, v, c)


def unpack_kernel(in_ref, *out_refs):
    for a, ref in enumerate(out_refs):
        for g in range(PLANE):
            ref[:, g * HD : (g + 1) * HD] = in_ref[g, a]


def unpack(packed):
    shape = jax.ShapeDtypeStruct((CHUNK, PLANE * HD), BF16)
    return pl.pallas_call(unpack_kernel, out_shape=(shape,) * 2, name="unpack")(packed)


def nt(a, b):
    return lax.dot_general(a, b, (((1,), (1,)), ((), ())), preferred_element_type=F32)


def nn(a, b):
    return lax.dot_general(a, b, (((1,), (0,)), ((), ())), preferred_element_type=F32)


def group_rows(x):
    return x.reshape(x.shape[0] // 8, 8, x.shape[1])


def marks(shape, dim, row):
    return (lax.broadcasted_iota(jnp.int32, shape, dim) == row).astype(F32)


SPANS = ((0, 2 * BLOCK), (0, 3 * BLOCK), (BLOCK, 2 * BLOCK))


def attend_kernel(edge, core_ref, *refs):
    refs = list(refs)
    mine_ref, swap_ref = refs[:2]
    del refs[:2]
    edge_ref = refs.pop(0) if edge else None
    bias_ref = refs.pop(0)
    if edge:
        old_swap_ref = refs[2]
        del refs[:3]
    out_ref, gown_ref, gswap_ref = refs[:3]
    del refs[:3]
    gedge_ref = refs.pop(0) if edge else None
    (q_s, c_s, k_s, v_s, hot_s, kt_s, vt_s, qt_s, ct_s, s_s, p_s, d_s, o_s, dq_s, gb_s, old_s, sems, out_sems) = refs

    core = core_ref[0]
    frame = core if edge else 1 - core

    def part(ref, index, a):
        return ref.at[pl.ds(index * CHUNKS, CHUNKS), a]

    ins = {}

    def load(name, src, dst):
        cp = pltpu.make_async_copy(src, dst, sems.at[len(ins)])
        cp.start()
        ins[name] = cp

    load("q", part(mine_ref, frame, 0), q_s)
    for a, dst in ((1, k_s), (2, v_s)):
        load((a, 1), part(mine_ref, frame, a), dst.at[1])
        if edge:
            load((a, 0), edge_ref.at[:, a - 1], dst.at[0])
            load((a, 2), part(swap_ref, core, a - 1), dst.at[2])
        else:
            load((a, 0), part(swap_ref, 0, a - 1), dst.at[0])
            load((a, 2), part(swap_ref, 1, a - 1), dst.at[2])
    load("c", part(mine_ref, frame, 3), c_s)
    if edge:
        for a in range(2):
            load(("old", a), part(old_swap_ref, core, a), old_s.at[a])

    lane = lax.broadcasted_iota(jnp.int32, (TILE, HD), 1)
    for t in range(3 * TILES_F):
        hot_s[t * TILE : (t + 1) * TILE, :] = (lane == t).astype(F32).astype(BF16)
    qt_s[HD:, :] = bias_ref[...]
    vt_s[HD:, :] = marks((16, KEYS), 0, 0).astype(BF16)
    for cp in ins.values():
        cp.wait()

    qf = q_s.reshape(FRAME, HD)
    cf = c_s.reshape(FRAME, HD)
    kf = k_s.reshape(KEYS, HD)
    vf = v_s.reshape(KEYS, HD)
    of = o_s.reshape(FRAME, HD)
    dqf = dq_s.reshape(FRAME, HD)
    gf = gb_s.reshape(2 * KEYS, HD)
    oldf = old_s.reshape(2 * FRAME, HD)

    qt_s[:HD, :] = qf[...].T

    def keys(s, lo, n):
        return slice(s * FRAME + lo, s * FRAME + lo + n)

    tops = {}

    def score(r):
        lo, n = SPANS[r]
        cols = slice(r * BLOCK, (r + 1) * BLOCK)
        qt = qt_s[:, cols]
        top = None
        for s in range(3):
            for b in range(n // BLOCK):
                ks = keys(s, lo + b * BLOCK, BLOCK)
                st = nn(jnp.concatenate([kf[ks, :], hot_s[ks, :]], axis=1), qt)
                s_s[r, s * n + b * BLOCK : s * n + (b + 1) * BLOCK, :] = st
                got = jnp.max(group_rows(st), axis=0)
                top = got if top is None else jnp.maximum(top, got)
        tops[r] = jnp.max(top, axis=0, keepdims=True) * (SCALE * LOG2E)

    def soften(r):
        lo, n = SPANS[r]
        cols = slice(r * BLOCK, (r + 1) * BLOCK)
        for s in range(3):
            for t in range(n // TILE):
                e = jnp.exp2(s_s[r, s * n + t * TILE : s * n + (t + 1) * TILE, :] * (SCALE * LOG2E) - tops[r])
                p_s[s, lo + t * TILE : lo + (t + 1) * TILE, cols] = e.astype(BF16)

    tails = {}

    def finish(r):
        lo, n = SPANS[r]
        cols = slice(r * BLOCK, (r + 1) * BLOCK)
        ot = None
        for s in range(3):
            got = nn(vt_s[:, keys(s, lo, n)], p_s[s, lo : lo + n, cols])
            ot = got if ot is None else ot + got
        inv = 1.0 / ot[HD : HD + 1]
        out = (ot[:HD] * inv).astype(BF16)
        of[cols, :] = out.T
        c2 = (ct_s[:HD, cols].astype(F32) * (inv * SCALE)).astype(BF16)
        ct_s[:HD, cols] = c2
        dots = -jnp.sum(c2.astype(F32) * out.astype(F32), axis=0, keepdims=True)
        high = dots.astype(BF16).astype(F32)
        mid = (dots - high).astype(BF16).astype(F32)
        low = dots - high - mid
        shape = (HD, BLOCK)
        tail = marks(shape, 0, 0) * high + marks(shape, 0, 1) * mid + marks(shape, 0, 2) * low
        ct_s[HD:, cols] = tail.astype(BF16)

    unit = (lax.broadcasted_iota(jnp.int32, (BLOCK, HD), 1) < 3).astype(F32).astype(BF16)

    def back(r):
        lo, n = SPANS[r]
        cols = slice(r * BLOCK, (r + 1) * BLOCK)
        c2 = ct_s[:, cols]
        dqt = None
        for s in range(3):
            for b in range(n // BLOCK):
                ks = keys(s, lo + b * BLOCK, BLOCK)
                dp = nn(jnp.concatenate([vf[ks, :], unit], axis=1), c2)
                at = slice(lo + b * BLOCK, lo + (b + 1) * BLOCK)
                d_s[s, at, cols] = p_s[s, at, cols] * dp.astype(BF16)
            got = nn(kt_s[:, keys(s, lo, n)], d_s[s, lo : lo + n, cols])
            dqt = got if dqt is None else dqt + got
        dqf[cols, :] = dqt.astype(BF16).T

    score(0)
    score(1)
    ct_s[:HD, :] = cf[...].T
    vt_s[:HD, :] = vf[...].T
    kt_s[...] = kf[...].T
    soften(0)
    finish(0)
    score(2)
    soften(1)
    finish(1)
    back(0)
    soften(2)
    finish(2)
    back(1)
    back(2)

    outs = []

    def store(src, dst):
        cp = pltpu.make_async_copy(src, dst, out_sems.at[len(outs)])
        cp.start()
        outs.append(cp)

    store(o_s, part(out_ref, frame, 0))
    store(dq_s, part(out_ref, frame, 1))
    for s in (0, 2, 1):
        for a in range(2):
            for b, (lo, n) in enumerate(SPANS):
                at = slice(b * BLOCK, (b + 1) * BLOCK)
                if a == 0:
                    g = nt(qt_s[:HD, lo : lo + n], d_s[s, at, lo : lo + n])
                else:
                    g = nt(ct_s[:HD, lo : lo + n], p_s[s, at, lo : lo + n]) * (1.0 / SCALE)
                g = g.astype(BF16).T
                if edge and s == 2:
                    g = (g.astype(F32) + oldf[a * FRAME + b * BLOCK : a * FRAME + (b + 1) * BLOCK, :].astype(F32)).astype(BF16)
                gf[(a * 3 + s) * FRAME + b * BLOCK : (a * 3 + s) * FRAME + (b + 1) * BLOCK, :] = g
            if s == 1:
                store(gb_s.at[a, s], part(gown_ref, frame, a))
            elif not edge:
                store(gb_s.at[a, s], part(gswap_ref, s // 2, a))
            elif s == 0:
                store(gb_s.at[a, s], gedge_ref.at[:, a])
            else:
                store(gb_s.at[a, s], part(gswap_ref, core, a))
    for cp in outs:
        cp.wait()


def attend(core, mine, swap, bias, edge=None, old=()):
    frame = pltpu.VMEM((CHUNKS, CHUNK, HD), BF16)
    slots = pltpu.VMEM((3, CHUNKS, CHUNK, HD), BF16)
    pair = jax.ShapeDtypeStruct((PLANE, 2, CHUNK, HD), BF16)
    with_edge = edge is not None
    smem, vmem = pl.BlockSpec(memory_space=pltpu.SMEM), pl.BlockSpec(memory_space=pltpu.VMEM)
    edges = (edge,) if with_edge else ()
    shapes = (pair,) * 3 + ((jax.ShapeDtypeStruct((CHUNKS, 2, CHUNK, HD), BF16),) if with_edge else ())
    return pl.pallas_call(
        functools.partial(attend_kernel, with_edge),
        in_specs=[smem, ANY, ANY] + [ANY] * len(edges) + [vmem] + [ANY] * len(old),
        out_specs=(ANY,) * len(shapes),
        out_shape=shapes,
        scratch_shapes=[
            frame,
            frame,
            slots,
            slots,
            pltpu.VMEM((KEYS, HD), BF16),
            pltpu.VMEM((HD, KEYS), BF16),
            pltpu.VMEM((HD + 16, KEYS), BF16),
            pltpu.VMEM((2 * HD, FRAME), BF16),
            pltpu.VMEM((2 * HD, FRAME), BF16),
            pltpu.VMEM((3, 9 * BLOCK, BLOCK), F32),
            pltpu.VMEM((3, FRAME, FRAME), BF16),
            pltpu.VMEM((3, FRAME, FRAME), BF16),
            frame,
            frame,
            pltpu.VMEM((2, 3, CHUNKS, CHUNK, HD), BF16),
            pltpu.VMEM((2, CHUNKS, CHUNK, HD), BF16),
            pltpu.SemaphoreType.DMA((10,)),
            pltpu.SemaphoreType.DMA((8,)),
        ],
        input_output_aliases={5: 0, 6: 1, 7: 2} if with_edge else {},
        name="attend_edge" if with_edge else "attend_local",
    )(core, mine, swap, *edges, bias, *old)


def join_kernel(core_ref, own_ref, swap_ref, edge_ref, out_ref):
    core = core_ref[0]
    for f in range(2):
        here = jnp.where(core == f, 1.0, 0.0)
        for a in range(2):
            for h in range(CHUNKS):
                x = own_ref[f * CHUNKS + h, a].astype(F32) + swap_ref[f * CHUNKS + h, a].astype(F32)
                x = x + edge_ref[h, a].astype(F32) * here
                out_ref[f * CHUNKS + h, a] = x.astype(BF16)


def join(core, own, swap, edge):
    vmem = pl.BlockSpec(memory_space=pltpu.VMEM)
    return pl.pallas_call(
        join_kernel,
        in_specs=[pl.BlockSpec(memory_space=pltpu.SMEM), vmem, vmem, vmem],
        out_specs=vmem,
        out_shape=jax.ShapeDtypeStruct((PLANE, 2, CHUNK, HD), BF16),
        name="join",
    )(core, own, swap, edge)


def tile_bias(neighbours, frame, keyed):
    rows = lax.dynamic_slice_in_dim(neighbours, frame * TILES_F, TILES_F, 0)
    rows = jnp.where(rows >= 0, rows, -2 * TILES_F)
    slot = jnp.arange(HD, dtype=jnp.int32)
    base = sum(jnp.where(slot // TILES_F == i, k, 0) for i, k in enumerate(keyed))
    tiles = base * TILES_F + slot % TILES_F
    hit = jnp.any(rows[None, :, :] == tiles[:, None, None], axis=2)
    return jnp.repeat(jnp.where(hit, 0.0, MASKED).astype(BF16), TILE, axis=1)


def shards(queries, keys, values, cotangent, neighbours):
    plane = ("yl", "head")
    ring = lax.axis_size("sx")
    across = []
    for i in range(ring - 1):
        across.append((2 * i + 1, 2 * i + 2))
        across.append((2 * i + 2, 2 * i + 1))
    swap_pairs = [(0, 1), (1, 0)]
    core = lax.axis_index("co")
    first = 4 * lax.axis_index("sx")
    partner = first + 1 - core
    mid = partner + 2 * core
    bias_local = tile_bias(neighbours, first + 2 - core, (partner, first + 2 - core, partner + 2))
    bias_edge = tile_bias(neighbours, first + 3 * core, (first - 1 + 5 * core, first + 3 * core, mid))
    core_arr = jnp.full((1,), core, jnp.int32)

    mine = lax.all_to_all(pack(queries, keys, values, cotangent), plane, split_axis=0, concat_axis=0, tiled=True)
    kv = mine[:, 1:3]
    swap = lax.ppermute(kv, "co", swap_pairs)
    kv_edge = lax.dynamic_slice_in_dim(kv, core * CHUNKS, CHUNKS, 0)
    edge = lax.ppermute(kv_edge, ("sx", "co"), across)
    done = attend(core_arr, mine, swap, bias_local)
    packed, gown, gswap, gedge = attend(core_arr, mine, swap, bias_edge, edge, done)
    output, grad_query = unpack(lax.all_to_all(packed, plane, split_axis=0, concat_axis=0, tiled=True))
    gswap_in = lax.ppermute(gswap, "co", swap_pairs)
    gedge_in = lax.ppermute(gedge, ("sx", "co"), across)
    gown = join(core_arr, gown, gswap_in, gedge_in)
    grad_key, grad_value = unpack(lax.all_to_all(gown, plane, split_axis=0, concat_axis=0, tiled=True))
    return output, grad_query, grad_key, grad_value


def solution(mesh):
    view = Mesh(mesh.devices.reshape(mesh.devices.shape[0] // 4, 2, 2, -1), ("sx", "yl", "co", "head"))
    rows = P(("sx", "yl", "co", "head"), None)
    return jax.shard_map(
        shards,
        mesh=view,
        in_specs=(rows,) * 4 + (P(),),
        out_specs=(rows,) * 4,
        check_vma=False,
    )
```

time: 106 us -> 102 us (0.962)
  blocking collectives: 57.8 us -> 0 us
  waiting for transfers between devices: 13.1 us -> 42.4 us
  starting transfers between devices: 4.15 us -> 24.9 us
  local copies, waits for them, and re-layouts: 3.04 us -> 5.8 us
    all_to_all x2 -> x0, blocking collectives: 57.8 us -> none  [the longest x1 30.4 us: shards(): lax.all_to_all(pack(queries, keys, values, cotangent), plane, split_axis=...]
    all_to_all x0 -> x3, waiting for transfers between devices: none -> 35.2 us  [the longest x1 22.8 us: shards(): lax.all_to_all(pack(queries, keys, values, cotangent), plane, split_axis=...]
    all_to_all x0 -> x3, starting transfers between devices: none -> 19.3 us  [the longest x1 8.18 us: shards(): lax.all_to_all(pack(queries, keys, values, cotangent), plane, split_axis=...]
    ppermute x1, waiting for transfers between devices: 5.68 us -> 0.01 us  [shards(): edge = lax.ppermute(kv_edge, ('sx', 'co'), across)]
    unnamed x8 -> x16, local copies, waits for them, and re-layouts: 1.59 us -> 2.84 us
    ppermute x1, starting transfers between devices: 0.2 us -> 1.3 us  [shards(): gswap_in = lax.ppermute(gswap, 'co', swap_pairs)]
    pallas_call x2 -> x4, Pallas kernels: 21.3 us -> 21 us  [the longest x2 16.6 us: attend(): pl.pallas_call(functools.partial(attend_kernel, with_edge), in_specs=[sme...]
  transfers between devices with their start and end apart: 4 -> 7, of which waited for: 2 -> 4; matrix products, arithmetic and copies ran while one was open for 2% -> 3% of each run, Pallas kernels for 0% -> 13%
where the time goes in v2:
time: 102 us; the launch traced here: 101 us
  waiting for transfers between devices  42.4 us (42%)
  Pallas kernels  26.5 us (26%)
  starting transfers between devices  24.9 us (24%)
  local copies, waits for them, and re-layouts  5.8 us (6%)
    all_to_all x1, waiting for transfers between devices, shards(): lax.all_to_all(pack(queries, keys, values, cotangent), plane, split_axis=...  22.8 us
    pallas_call x2, Pallas kernels, attend(): pl.pallas_call(functools.partial(attend_kernel, with_edge), in_specs=[sme...  16.6 us
    all_to_all x1, waiting for transfers between devices, shards(): lax.all_to_all(gown, plane, split_axis=0, concat_axis=0, tiled=True)  11.4 us
    all_to_all x1, starting transfers between devices, shards(): lax.all_to_all(pack(queries, keys, values, cotangent), plane, split_axis=...  8.18 us
    ppermute x1, waiting for transfers between devices, shards(): gedge_in = lax.ppermute(gedge, ('sx', 'co'), across)  7.17 us
    all_to_all x1, starting transfers between devices, shards(): lax.all_to_all(gown, plane, split_axis=0, concat_axis=0, tiled=True)  6.21 us
    all_to_all x1, starting transfers between devices, shards(): lax.all_to_all(packed, plane, split_axis=0, concat_axis=0, tiled=True)  4.94 us
    pallas_call x2, Pallas kernels, unpack(): pl.pallas_call(unpack_kernel, out_shape=(shape,) * 2, name='unpack')(packed)  4.39 us
  transfers between devices with their start and end apart: 7, of which 4 were waited for; matrix products, arithmetic and copies ran while one was open for 3% of the time, Pallas kernels for 13%

profile of v2, /device:TPU:2, one launch (start us, length us, event | category | flops | bytes accessed | tf_op | source)
XLA Modules:
  0.0 100.9 jit_solution(11634609327051920690)
XLA Ops:
  0.6 2.8 %pack.1 = bf16[16,4,96,128]{3,2,1,0:T(8,128)(2,1)} custom-call(bf16[96,2048]{1,0:T(8,128)(2,1)} %q_ref.1, bf16[96,2048]{1,0:T(8,128)(2,1)} %k_ref.1, bf16[96,2048]{1,0:T(8,128)(2,1)} %v_ref.1, bf16[96,2048]{1,0:T(8,128)(2,1)} %c_ref.1), custom_call_target="tpu_custom_call" | custom-call | tf_op jit(solution)/shard_map/pack/pallas_call | solution.py:35
  3.4 8.2 %all-to-all-start = ((bf16[16,4,96,128]{3,2,1,0:T(8,128)(2,1)}), bf16[16,4,96,128]{3,2,1,0:T(8,128)(2,1)S(1)}, u32[]{:S(2)}, u32[]{:S(2)}) async-start(bf16[16,4,96,128]{3,2,1,0:T(8,128)(2,1)} %pack.1), calls=%async_computation | async-start | bytes 3145728 | tf_op jit(solution)/shard_map/all_to_all | solution.py:333
  11.6 0.1 compare_select_fusion
  11.7 0.1 copy.18
  11.8 0.1 compare_reduce_fusion.1
  12.0 22.8 %all-to-all-done.refs_0_ = bf16[16,4,96,128]{3,2,1,0:T(8,128)(2,1)S(1)} async-done(((bf16[16,4,96,128]{3,2,1,0:T(8,128)(2,1)}), bf16[16,4,96,128]{3,2,1,0:T(8,128)(2,1)S(1)}, u32[]{:S(2)}, u32[]{:S(2)}) %all-to-all-start) | async-done | bytes 1572896 | tf_op jit(solution)/shard_map/all_to_all | solution.py:333
  34.8 0.1 slice.4
  34.9 0.1 collective-permute-start
  35.0 1.0 constant_dynamic-slice_fusion
  36.0 2.3 %collective-permute-start.1 = (bf16[8,2,96,128]{3,2,1,0:T(8,128)(2,1)}, bf16[8,2,96,128]{3,2,1,0:T(8,128)(2,1)}, u32[]{:S(2)}, u32[]{:S(2)}) collective-permute-start(bf16[8,2,96,128]{3,2,1,0:T(8,128)(2,1)} %constant_dynamic-slice_fusion), channel_id=1, source_target_pairs={{8,32},{32,8},{40,64},{64,40},{72,96},{96,72},{9,33},{33,9},{41,65... | collective-permute-start | bytes 1179656 | tf_op jit(solution)/shard_map/ppermute | solution.py:337
  38.3 0.1 copy.19
  38.5 0.8 copy.21.refs_3_
  39.3 0.1 compare_reduce_fusion
  39.5 0.8 copy.20.refs_2_
  40.3 0.9 copy-done.3
  41.2 8.2 %attend_local.1 = (bf16[16,2,96,128]{3,2,1,0:T(8,128)(2,1)}, bf16[16,2,96,128]{3,2,1,0:T(8,128)(2,1)}, bf16[16,2,96,128]{3,2,1,0:T(8,128)(2,1)}) custom-call(s32[1]{0:T(128)} %bitcast.core_ref, bf16[16,4,96,128]{3,2,1,0:T(8,128)(2,1)} %copy-done, bf16[16,2,96,128]{3,2,1,0:T(8,128)(2,1)} %copy-done.3, bf16[128,768]{1,0:T(8,128)(2,1)} %copy.20.refs_2_), custom_call_target="tpu_custom_call" | custom-call | tf_op jit(solution)/shard_map/attend_local/pallas_call | solution.py:255
  49.4 0.0 collective-permute-done.1.refs_2_
  49.5 8.4 %attend_edge.1 = (bf16[16,2,96,128]{3,2,1,0:T(8,128)(2,1)}, bf16[16,2,96,128]{3,2,1,0:T(8,128)(2,1)}, bf16[16,2,96,128]{3,2,1,0:T(8,128)(2,1)}, bf16[8,2,96,128]{3,2,1,0:T(8,128)(2,1)}) custom-call(s32[1]{0:T(128)} %bitcast.core_ref, bf16[16,4,96,128]{3,2,1,0:T(8,128)(2,1)} %copy-done, ...), custom_call_target="tpu_custom_call", output_to_operand_aliasing={{0}: (5, {}), {1}: (6, {}), {2}: (7, {})} | custom-call | tf_op jit(solution)/shard_map/attend_edge/pallas_call | solution.py:255
  57.8 0.0 copy-start.7
  57.9 1.3 %collective-permute-start.2 = (bf16[16,2,96,128]{3,2,1,0:T(8,128)(2,1)}, bf16[16,2,96,128]{3,2,1,0:T(8,128)(2,1)S(1)}, u32[]{:S(2)}, u32[]{:S(2)}) collective-permute-start(bf16[16,2,96,128]{3,2,1,0:T(8,128)(2,1)} %get-tuple-element.22), channel_id=1, source_target_pairs={{0,8},{8,0},{1,9},{9,1},{2,10},{10,2},{3,11},{11,3},{4,12},{12,4},... | collective-permute-start | bytes 2359304 | tf_op jit(solution)/shard_map/ppermute | solution.py:341
  59.2 4.9 %all-to-all-start.1 = ((bf16[16,2,96,128]{3,2,1,0:T(8,128)(2,1)}), bf16[16,2,96,128]{3,2,1,0:T(8,128)(2,1)S(1)}, u32[]{:S(2)}, u32[]{:S(2)}) async-start(bf16[16,2,96,128]{3,2,1,0:T(8,128)(2,1)} %get-tuple-element.18), calls=%async_computation.1 | async-start | bytes 1572864 | tf_op jit(solution)/shard_map/all_to_all | solution.py:340
  64.1 1.9 %collective-permute-start.3 = (bf16[8,2,96,128]{3,2,1,0:T(8,128)(2,1)S(1)}, bf16[8,2,96,128]{3,2,1,0:T(8,128)(2,1)S(1)}, u32[]{:S(2)}, u32[]{:S(2)}) collective-permute-start(bf16[8,2,96,128]{3,2,1,0:T(8,128)(2,1)S(1)} %copy-done.7), channel_id=1, source_target_pairs={{8,32},{32,8},{40,64},{64,40},{72,96},{96,72},{9,33},{33,9},{41,65... | collective-permute-start | bytes 1179656 | tf_op jit(solution)/shard_map/ppermute | solution.py:342
  66.1 7.2 %collective-permute-done.3.edge_ref = bf16[8,2,96,128]{3,2,1,0:T(8,128)(2,1)S(1)} collective-permute-done((bf16[8,2,96,128]{3,2,1,0:T(8,128)(2,1)S(1)}, bf16[8,2,96,128]{3,2,1,0:T(8,128)(2,1)S(1)}, u32[]{:S(2)}, u32[]{:S(2)}) %collective-permute-start.3) | collective-permute-done | bytes 393248 | tf_op jit(solution)/shard_map/ppermute | solution.py:342
  73.2 0.7 copy-done.5
  74.0 0.3 copy-done.4
  74.3 2.7 %join.1 = bf16[16,2,96,128]{3,2,1,0:T(8,128)(2,1)} custom-call(s32[1]{0:T(128)} %bitcast.core_ref, bf16[16,2,96,128]{3,2,1,0:T(8,128)(2,1)} %get-tuple-element.21.own_ref, bf16[16,2,96,128]{3,2,1,0:T(8,128)(2,1)} %copy-done.4, bf16[8,2,96,128]{3,2,1,0:T(8,128)(2,1)} %copy-done.5), custom_call_target="tpu_custom_call" | custom-call | tf_op jit(solution)/shard_map/join/pallas_call | solution.py:298
  77.0 1.0 all-to-all-done.1.in_ref
  78.0 6.2 %all-to-all-start.2 = ((bf16[16,2,96,128]{3,2,1,0:T(8,128)(2,1)}), bf16[16,2,96,128]{3,2,1,0:T(8,128)(2,1)S(1)}, u32[]{:S(2)}, u32[]{:S(2)}) async-start(bf16[16,2,96,128]{3,2,1,0:T(8,128)(2,1)} %join.1), calls=%async_computation.2 | async-start | bytes 1572864 | tf_op jit(solution)/shard_map/all_to_all | solution.py:344
  84.2 2.2 %unpack.2 = (bf16[96,2048]{1,0:T(8,128)(2,1)}, bf16[96,2048]{1,0:T(8,128)(2,1)}) custom-call(bf16[16,2,96,128]{3,2,1,0:T(8,128)(2,1)} %copy-done.1), custom_call_target="tpu_custom_call" | custom-call | tf_op jit(solution)/shard_map/unpack/pallas_call | solution.py:50
  86.4 11.4 %all-to-all-done.2.in_ref = bf16[16,2,96,128]{3,2,1,0:T(8,128)(2,1)S(1)} async-done(((bf16[16,2,96,128]{3,2,1,0:T(8,128)(2,1)}), bf16[16,2,96,128]{3,2,1,0:T(8,128)(2,1)S(1)}, u32[]{:S(2)}, u32[]{:S(2)}) %all-to-all-start.2) | async-done | bytes 786464 | tf_op jit(solution)/shard_map/all_to_all | solution.py:344
  97.8 0.9 copy-done.2
  98.7 2.2 %unpack.3 = (bf16[96,2048]{1,0:T(8,128)(2,1)}, bf16[96,2048]{1,0:T(8,128)(2,1)}) custom-call(bf16[16,2,96,128]{3,2,1,0:T(8,128)(2,1)} %copy-done.2), custom_call_target="tpu_custom_call" | custom-call | tf_op jit(solution)/shard_map/unpack/pallas_call | solution.py:50
  (19 shorter events, 0.1 us)
Async XLA Ops:
  3.4 8.2 %copy-start.6 = (s32[192,27]{0,1:T(8,128)S(1)}, s32[192,27]{0,1:T(8,128)}, u32[]{:S(2)}) copy-start(s32[192,27]{0,1:T(8,128)} %param.9) | copy-start | bytes 62212
  3.4 31.4 %all-to-all-start = ((bf16[16,4,96,128]{3,2,1,0:T(8,128)(2,1)}), bf16[16,4,96,128]{3,2,1,0:T(8,128)(2,1)S(1)}, u32[]{:S(2)}, u32[]{:S(2)}) async-start(bf16[16,4,96,128]{3,2,1,0:T(8,128)(2,1)} %pack.1), calls=%async_computation | async-start | bytes 3145728 | tf_op jit(solution)/shard_map/all_to_all | solution.py:333
  34.8 4.6 %copy-start = (bf16[16,4,96,128]{3,2,1,0:T(8,128)(2,1)}, bf16[16,4,96,128]{3,2,1,0:T(8,128)(2,1)S(1)}, u32[]{:S(2)}) copy-start(bf16[16,4,96,128]{3,2,1,0:T(8,128)(2,1)S(1)} %all-to-all-done.refs_0_) | copy-start | bytes 4718596
  34.9 5.4 %collective-permute-start = (bf16[16,2,96,128]{3,2,1,0:T(8,128)(2,1)S(1)}, bf16[16,2,96,128]{3,2,1,0:T(8,128)(2,1)S(1)}, u32[]{:S(2)}, u32[]{:S(2)}) collective-permute-start(bf16[16,2,96,128]{3,2,1,0:T(8,128)(2,1)S(1)} %slice.4), channel_id=1, source_target_pairs={{0,8},{8,0},{1,9},{9,1},{2,10},{10,2},{3,11},{11,3},{4,12},{12,4},... | collective-permute-start | bytes 2359304 | tf_op jit(solution)/shard_map/ppermute | solution.py:335
  36.0 13.4 %collective-permute-start.1 = (bf16[8,2,96,128]{3,2,1,0:T(8,128)(2,1)}, bf16[8,2,96,128]{3,2,1,0:T(8,128)(2,1)}, u32[]{:S(2)}, u32[]{:S(2)}) collective-permute-start(bf16[8,2,96,128]{3,2,1,0:T(8,128)(2,1)} %constant_dynamic-slice_fusion), channel_id=1, source_target_pairs={{8,32},{32,8},{40,64},{64,40},{72,96},{96,72},{9,33},{33,9},{41,65... | collective-permute-start | bytes 1179656 | tf_op jit(solution)/shard_map/ppermute | solution.py:337
  40.3 0.9 copy-start.3
  57.8 6.3 %copy-start.7 = (bf16[8,2,96,128]{3,2,1,0:T(8,128)(2,1)S(1)}, bf16[8,2,96,128]{3,2,1,0:T(8,128)(2,1)}, u32[]{:S(2)}) copy-start(bf16[8,2,96,128]{3,2,1,0:T(8,128)(2,1)} %get-tuple-element.23) | copy-start | bytes 1179652
  57.9 15.4 %collective-permute-start.2 = (bf16[16,2,96,128]{3,2,1,0:T(8,128)(2,1)}, bf16[16,2,96,128]{3,2,1,0:T(8,128)(2,1)S(1)}, u32[]{:S(2)}, u32[]{:S(2)}) collective-permute-start(bf16[16,2,96,128]{3,2,1,0:T(8,128)(2,1)} %get-tuple-element.22), channel_id=1, source_target_pairs={{0,8},{8,0},{1,9},{9,1},{2,10},{10,2},{3,11},{11,3},{4,12},{12,4},... | collective-permute-start | bytes 2359304 | tf_op jit(solution)/shard_map/ppermute | solution.py:341
  59.2 18.8 %all-to-all-start.1 = ((bf16[16,2,96,128]{3,2,1,0:T(8,128)(2,1)}), bf16[16,2,96,128]{3,2,1,0:T(8,128)(2,1)S(1)}, u32[]{:S(2)}, u32[]{:S(2)}) async-start(bf16[16,2,96,128]{3,2,1,0:T(8,128)(2,1)} %get-tuple-element.18), calls=%async_computation.1 | async-start | bytes 1572864 | tf_op jit(solution)/shard_map/all_to_all | solution.py:340
  64.1 9.1 %collective-permute-start.3 = (bf16[8,2,96,128]{3,2,1,0:T(8,128)(2,1)S(1)}, bf16[8,2,96,128]{3,2,1,0:T(8,128)(2,1)S(1)}, u32[]{:S(2)}, u32[]{:S(2)}) collective-permute-start(bf16[8,2,96,128]{3,2,1,0:T(8,128)(2,1)S(1)} %copy-done.7), channel_id=1, source_target_pairs={{8,32},{32,8},{40,64},{64,40},{72,96},{96,72},{9,33},{33,9},{41,65... | collective-permute-start | bytes 1179656 | tf_op jit(solution)/shard_map/ppermute | solution.py:342
  73.2 0.7 copy-start.5
  73.2 1.0 %copy-start.4 = (bf16[16,2,96,128]{3,2,1,0:T(8,128)(2,1)}, bf16[16,2,96,128]{3,2,1,0:T(8,128)(2,1)S(1)}, u32[]{:S(2)}) copy-start(bf16[16,2,96,128]{3,2,1,0:T(8,128)(2,1)S(1)} %collective-permute-done.2.swap_ref) | copy-start | bytes 2359300
  78.0 6.2 %copy-start.1 = (bf16[16,2,96,128]{3,2,1,0:T(8,128)(2,1)}, bf16[16,2,96,128]{3,2,1,0:T(8,128)(2,1)S(1)}, u32[]{:S(2)}) copy-start(bf16[16,2,96,128]{3,2,1,0:T(8,128)(2,1)S(1)} %all-to-all-done.1.in_ref) | copy-start | bytes 2359300
  78.0 19.8 %all-to-all-start.2 = ((bf16[16,2,96,128]{3,2,1,0:T(8,128)(2,1)}), bf16[16,2,96,128]{3,2,1,0:T(8,128)(2,1)S(1)}, u32[]{:S(2)}, u32[]{:S(2)}) async-start(bf16[16,2,96,128]{3,2,1,0:T(8,128)(2,1)} %join.1), calls=%async_computation.2 | async-start | bytes 1572864 | tf_op jit(solution)/shard_map/all_to_all | solution.py:344
  97.8 0.9 copy-start.2

commit v3 on v2

v3 whole, which is shorter than its diff:
```python
import functools
import math

import jax
import jax.numpy as jnp
from jax import lax
from jax.experimental import pallas as pl
from jax.experimental.pallas import tpu as pltpu
from jax.sharding import Mesh, PartitionSpec as P

TILE = 64
TILES_F = 12
HD = 128
FRAME = TILE * TILES_F
BLOCK = 4 * TILE
KEYS = 3 * FRAME
CHUNKS = 8
CHUNK = FRAME // CHUNKS
PLANE = 16
MASKED = -1e30
SCALE = 1.0 / math.sqrt(HD)
LOG2E = 1.4426950408889634
ANY = pl.BlockSpec(memory_space=pl.ANY)
VMEM = pl.BlockSpec(memory_space=pltpu.VMEM)
F32 = jnp.float32
BF16 = jnp.bfloat16


def near(x):
    return pltpu.with_memory_space_constraint(x, pltpu.VMEM)


def far(x):
    return pltpu.with_memory_space_constraint(x, pltpu.HBM)


def enter_kernel(q_ref, k_ref, v_ref, c_ref, near_ref, out_ref, bias_ref, in_s, out_s, in_sem, out_sem):
    ins, outs = [], []
    for a, ref in enumerate((q_ref, k_ref, v_ref, c_ref)):
        ins.append(pltpu.make_async_copy(ref, in_s.at[a], in_sem.at[a]))
        outs.append(pltpu.make_async_copy(out_s.at[a], out_ref.at[:, a], out_sem.at[a]))
        ins[a].start()
    core, first = lax.axis_index("co"), 4 * lax.axis_index("sx")
    partner = first + 1 - core
    local, outer = first + 2 - core, first + 3 * core
    places = (
        (local, (partner, local, partner + 2)),
        (outer, (first - 1 + 5 * core, outer, partner + 2 * core)),
    )
    tiles = near_ref.shape[1]
    slot = lax.broadcasted_iota(jnp.int32, (HD, 1), 0)
    listed = near_ref[...]
    for which, (frame, keyed) in enumerate(places):
        base = jnp.zeros_like(slot)
        for i, k in enumerate(keyed):
            base = jnp.where(slot // TILES_F == i, k, base)
        tile = base * TILES_F + slot % TILES_F
        tile = jnp.where(tile < 0, -TILES_F, tile)
        hit = jnp.zeros((HD, tiles), F32)
        for j in range(listed.shape[0]):
            hit = jnp.where(listed[j : j + 1, :] == tile, 1.0, hit)
        owner = lax.broadcasted_iota(jnp.int32, (tiles, FRAME), 1) // TILE + frame * TILES_F
        spread = (owner == lax.broadcasted_iota(jnp.int32, (tiles, FRAME), 0)).astype(F32).astype(BF16)
        bias_ref[which] = jnp.where(nn(hit.astype(BF16), spread) > 0.5, 0.0, MASKED).astype(BF16)
    for a in range(4):
        ins[a].wait()
        for g in range(PLANE):
            out_s[a, g] = in_s[a, :, g * HD : (g + 1) * HD]
        outs[a].start()
    for cp in outs:
        cp.wait()


def enter(q, k, v, c, neighbours):
    return pl.pallas_call(
        enter_kernel,
        in_specs=[ANY] * 4 + [VMEM],
        out_specs=(ANY, VMEM),
        out_shape=(
            jax.ShapeDtypeStruct((PLANE, 4, CHUNK, HD), BF16),
            jax.ShapeDtypeStruct((2, HD, FRAME), BF16),
        ),
        scratch_shapes=[
            pltpu.VMEM((4, CHUNK, PLANE * HD), BF16),
            pltpu.VMEM((4, PLANE, CHUNK, HD), BF16),
            pltpu.SemaphoreType.DMA((4,)),
            pltpu.SemaphoreType.DMA((4,)),
        ],
        compiler_params=pltpu.CompilerParams(vmem_limit_bytes=32 * 2**20),
        name="enter",
    )(far(q), far(k), far(v), far(c), neighbours.T)


def unpack_kernel(in_ref, *refs):
    sem = refs[-1]
    copies = []
    for a, ref in enumerate(refs[:-1]):
        for g in range(PLANE):
            part = ref.at[:, g * HD : (g + 1) * HD]
            copies.append(pltpu.make_async_copy(in_ref.at[g, a], part, sem.at[a, g]))
    for cp in copies:
        cp.start()
    for cp in copies:
        cp.wait()


def unpack(packed):
    return pl.pallas_call(
        unpack_kernel,
        in_specs=[VMEM],
        out_specs=(ANY,) * 2,
        out_shape=(jax.ShapeDtypeStruct((CHUNK, PLANE * HD), BF16),) * 2,
        scratch_shapes=[pltpu.SemaphoreType.DMA((2, PLANE))],
        name="unpack",
    )(near(packed))


def nt(a, b):
    return lax.dot_general(a, b, (((1,), (1,)), ((), ())), preferred_element_type=F32)


def nn(a, b):
    return lax.dot_general(a, b, (((1,), (0,)), ((), ())), preferred_element_type=F32)


def group_rows(x):
    return x.reshape(x.shape[0] // 8, 8, x.shape[1])


def marks(shape, dim, row):
    return (lax.broadcasted_iota(jnp.int32, shape, dim) == row).astype(F32)


SPANS = ((0, 2 * BLOCK), (0, 3 * BLOCK), (BLOCK, 2 * BLOCK))


def attend_kernel(edge, *refs):
    refs = list(refs)
    mine_ref, swap_ref = refs[:2]
    del refs[:2]
    edge_ref = refs.pop(0) if edge else None
    bias_ref = refs.pop(0)
    old_refs = refs[:3] if edge else None
    if edge:
        del refs[:3]
    out_ref, gown_ref, gswap_ref = refs[:3]
    del refs[:3]
    gedge_ref = refs.pop(0) if edge else None
    (q_s, c_s, k_s, v_s, hot_s, kt_s, vt_s, qt_s, ct_s, s_s, p_s, d_s, o_s, dq_s, gb_s) = refs

    core = lax.axis_index("co")
    frame = core if edge else 1 - core

    for h in range(CHUNKS):
        q_s[h] = mine_ref[frame * CHUNKS + h, 0]
    for a, dst in ((0, k_s), (1, v_s)):
        for h in range(CHUNKS):
            if edge:
                dst[0, h] = edge_ref[h, a]
                dst[2, h] = swap_ref[core * CHUNKS + h, a]
            else:
                dst[0, h] = swap_ref[h, a]
                dst[2, h] = swap_ref[CHUNKS + h, a]
            dst[1, h] = mine_ref[frame * CHUNKS + h, 1 + a]
    for h in range(CHUNKS):
        c_s[h] = mine_ref[frame * CHUNKS + h, 3]

    lane = lax.broadcasted_iota(jnp.int32, (TILE, HD), 1)
    for t in range(3 * TILES_F):
        hot_s[t * TILE : (t + 1) * TILE, :] = (lane == t).astype(F32).astype(BF16)
    qt_s[HD:, :] = bias_ref[1 if edge else 0]
    vt_s[HD:, :] = marks((16, KEYS), 0, 0).astype(BF16)

    qf = q_s.reshape(FRAME, HD)
    cf = c_s.reshape(FRAME, HD)
    kf = k_s.reshape(KEYS, HD)
    vf = v_s.reshape(KEYS, HD)
    of = o_s.reshape(FRAME, HD)
    dqf = dq_s.reshape(FRAME, HD)
    gf = gb_s.reshape(2 * KEYS, HD)

    qt_s[:HD, :] = qf[...].T

    def keys(s, lo, n):
        return slice(s * FRAME + lo, s * FRAME + lo + n)

    tops = {}

    def score(r):
        lo, n = SPANS[r]
        cols = slice(r * BLOCK, (r + 1) * BLOCK)
        qt = qt_s[:, cols]
        top = None
        for s in range(3):
            for b in range(n // BLOCK):
                ks = keys(s, lo + b * BLOCK, BLOCK)
                st = nn(jnp.concatenate([kf[ks, :], hot_s[ks, :]], axis=1), qt)
                s_s[r, s * n + b * BLOCK : s * n + (b + 1) * BLOCK, :] = st
                got = jnp.max(group_rows(st), axis=0)
                top = got if top is None else jnp.maximum(top, got)
        tops[r] = jnp.max(top, axis=0, keepdims=True) * (SCALE * LOG2E)

    def soften(r):
        lo, n = SPANS[r]
        cols = slice(r * BLOCK, (r + 1) * BLOCK)
        for s in range(3):
            for t in range(n // TILE):
                e = jnp.exp2(s_s[r, s * n + t * TILE : s * n + (t + 1) * TILE, :] * (SCALE * LOG2E) - tops[r])
                p_s[s, lo + t * TILE : lo + (t + 1) * TILE, cols] = e.astype(BF16)

    tails = {}

    def finish(r):
        lo, n = SPANS[r]
        cols = slice(r * BLOCK, (r + 1) * BLOCK)
        ot = None
        for s in range(3):
            got = nn(vt_s[:, keys(s, lo, n)], p_s[s, lo : lo + n, cols])
            ot = got if ot is None else ot + got
        inv = 1.0 / ot[HD : HD + 1]
        out = (ot[:HD] * inv).astype(BF16)
        of[cols, :] = out.T
        c2 = (ct_s[:HD, cols].astype(F32) * (inv * SCALE)).astype(BF16)
        ct_s[:HD, cols] = c2
        dots = -jnp.sum(c2.astype(F32) * out.astype(F32), axis=0, keepdims=True)
        high = dots.astype(BF16).astype(F32)
        mid = (dots - high).astype(BF16).astype(F32)
        low = dots - high - mid
        shape = (HD, BLOCK)
        tail = marks(shape, 0, 0) * high + marks(shape, 0, 1) * mid + marks(shape, 0, 2) * low
        ct_s[HD:, cols] = tail.astype(BF16)

    unit = (lax.broadcasted_iota(jnp.int32, (BLOCK, HD), 1) < 3).astype(F32).astype(BF16)

    def back(r):
        lo, n = SPANS[r]
        cols = slice(r * BLOCK, (r + 1) * BLOCK)
        c2 = ct_s[:, cols]
        dqt = None
        for s in range(3):
            for b in range(n // BLOCK):
                ks = keys(s, lo + b * BLOCK, BLOCK)
                dp = nn(jnp.concatenate([vf[ks, :], unit], axis=1), c2)
                at = slice(lo + b * BLOCK, lo + (b + 1) * BLOCK)
                d_s[s, at, cols] = p_s[s, at, cols] * dp.astype(BF16)
            got = nn(kt_s[:, keys(s, lo, n)], d_s[s, lo : lo + n, cols])
            dqt = got if dqt is None else dqt + got
        dqf[cols, :] = dqt.astype(BF16).T

    score(0)
    score(1)
    ct_s[:HD, :] = cf[...].T
    vt_s[:HD, :] = vf[...].T
    kt_s[...] = kf[...].T
    soften(0)
    finish(0)
    score(2)
    soften(1)
    finish(1)
    back(0)
    soften(2)
    finish(2)
    back(1)
    back(2)

    place = frame if edge else 0

    def store(src, ref, index, a):
        for h in range(CHUNKS):
            ref[index * CHUNKS + h, a] = src[h]

    if edge:
        other = 1 - core
        for old, new in zip(old_refs[:2], (out_ref, gown_ref)):
            for a in range(2):
                for h in range(CHUNKS):
                    new[other * CHUNKS + h, a] = old[h, a]
        for a in range(2):
            for h in range(CHUNKS):
                gswap_ref[other * CHUNKS + h, a] = old_refs[2][other * CHUNKS + h, a]
    store(o_s, out_ref, place, 0)
    store(dq_s, out_ref, place, 1)
    for s in (0, 2, 1):
        for a in range(2):
            for b, (lo, n) in enumerate(SPANS):
                at = slice(b * BLOCK, (b + 1) * BLOCK)
                if a == 0:
                    g = nt(qt_s[:HD, lo : lo + n], d_s[s, at, lo : lo + n])
                else:
                    g = nt(ct_s[:HD, lo : lo + n], p_s[s, at, lo : lo + n]) * (1.0 / SCALE)
                row = (a * 3 + s) * FRAME + b * BLOCK
                gf[row : row + BLOCK, :] = g.astype(BF16).T
            if s == 1:
                store(gb_s.at[a, s], gown_ref, place, a)
            elif not edge:
                store(gb_s.at[a, s], gswap_ref, s // 2, a)
            elif s == 0:
                store(gb_s.at[a, s], gedge_ref, 0, a)
            else:
                for h in range(CHUNKS):
                    both = gb_s[a, s, h].astype(F32) + old_refs[2][core * CHUNKS + h, a].astype(F32)
                    gswap_ref[core * CHUNKS + h, a] = both.astype(BF16)


def attend(mine, swap, bias, edge=None, old=()):
    frame = pltpu.VMEM((CHUNKS, CHUNK, HD), BF16)
    slots = pltpu.VMEM((3, CHUNKS, CHUNK, HD), BF16)
    pair = jax.ShapeDtypeStruct((PLANE, 2, CHUNK, HD), BF16)
    half = jax.ShapeDtypeStruct((CHUNKS, 2, CHUNK, HD), BF16)
    out = pltpu.HBM((PLANE, 2, CHUNK, HD), BF16)
    with_edge = edge is not None
    edges = (near(edge),) if with_edge else ()
    shapes = (out, out, pair, half) if with_edge else (half, half, pair)
    return pl.pallas_call(
        functools.partial(attend_kernel, with_edge),
        in_specs=[VMEM, VMEM] + [VMEM] * len(edges) + [VMEM] + [VMEM] * len(old),
        out_specs=(VMEM,) * len(shapes),
        out_shape=shapes,
        scratch_shapes=[
            frame,
            frame,
            slots,
            slots,
            pltpu.VMEM((KEYS, HD), BF16),
            pltpu.VMEM((HD, KEYS), BF16),
            pltpu.VMEM((HD + 16, KEYS), BF16),
            pltpu.VMEM((2 * HD, FRAME), BF16),
            pltpu.VMEM((2 * HD, FRAME), BF16),
            pltpu.VMEM((3, 9 * BLOCK, BLOCK), F32),
            pltpu.VMEM((3, FRAME, FRAME), BF16),
            pltpu.VMEM((3, FRAME, FRAME), BF16),
            frame,
            frame,
            pltpu.VMEM((2, 3, CHUNKS, CHUNK, HD), BF16),
        ],
        compiler_params=pltpu.CompilerParams(vmem_limit_bytes=32 * 2**20),
        name="attend_edge" if with_edge else "attend_local",
    )(near(mine), near(swap), *edges, bias, *old)


def join_kernel(own_ref, swap_ref, edge_ref, out_ref):
    core = lax.axis_index("co")
    for f in range(2):
        here = jnp.where(core == f, 1.0, 0.0)
        for a in range(2):
            for h in range(CHUNKS):
                x = own_ref[f * CHUNKS + h, a].astype(F32) + swap_ref[f * CHUNKS + h, a].astype(F32)
                x = x + edge_ref[h, a].astype(F32) * here
                out_ref[f * CHUNKS + h, a] = x.astype(BF16)


def join(own, swap, edge):
    return pl.pallas_call(
        join_kernel,
        in_specs=[VMEM, VMEM, VMEM],
        out_specs=VMEM,
        out_shape=jax.ShapeDtypeStruct((PLANE, 2, CHUNK, HD), BF16),
        name="join",
    )(own, near(swap), near(edge))


def shards(queries, keys, values, cotangent, neighbours):
    plane = ("yl", "head")
    ring = lax.axis_size("sx")
    across = []
    for i in range(ring - 1):
        across.append((2 * i + 1, 2 * i + 2))
        across.append((2 * i + 2, 2 * i + 1))
    swap_pairs = [(0, 1), (1, 0)]
    core = lax.axis_index("co")
    sent, bias = enter(queries, keys, values, cotangent, neighbours)
    with jax.named_scope("enter_all"):
        mine = lax.all_to_all(sent, plane, split_axis=0, concat_axis=0, tiled=True)
    kv = mine[:, 1:3]
    swap = lax.ppermute(kv, "co", swap_pairs)
    kv_edge = lax.dynamic_slice_in_dim(kv, core * CHUNKS, CHUNKS, 0)
    edge = lax.ppermute(kv_edge, ("sx", "co"), across)
    done = attend(mine, swap, bias)
    packed, gown, gswap, gedge = attend(mine, swap, bias, edge, done)
    output, grad_query = unpack(lax.all_to_all(packed, plane, split_axis=0, concat_axis=0, tiled=True))
    gswap_in = lax.ppermute(gswap, "co", swap_pairs)
    gedge_in = lax.ppermute(gedge, ("sx", "co"), across)
    gown = join(gown, gswap_in, gedge_in)
    grad_key, grad_value = unpack(lax.all_to_all(gown, plane, split_axis=0, concat_axis=0, tiled=True))
    return output, grad_query, grad_key, grad_value


def solution(mesh):
    view = Mesh(mesh.devices.reshape(mesh.devices.shape[0] // 4, 2, 2, -1), ("sx", "yl", "co", "head"))
    rows = P(("sx", "yl", "co", "head"), None)
    return jax.shard_map(
        shards,
        mesh=view,
        in_specs=(rows,) * 4 + (P(),),
        out_specs=(rows,) * 4,
        check_vma=False,
    )
```

time: 102 us -> 88.8 us (0.87)
  blocking collectives: 0 us -> 30.2 us
  waiting for transfers between devices: 42.4 us -> 23.5 us
  starting transfers between devices: 24.9 us -> 13.7 us
  Pallas kernels: 26.5 us -> 17.7 us
  local copies, waits for them, and re-layouts: 5.8 us -> 1.59 us
    all_to_all x0 -> x1, blocking collectives: none -> 30.2 us  [shards(): mine = lax.all_to_all(sent, plane, split_axis=0, concat_axis=0, tiled=True)]
    all_to_all x1 -> x0, waiting for transfers between devices: 22.8 us -> none  [shards(): lax.all_to_all(pack(queries, keys, values, cotangent), plane, split_axis=...]
    pallas_call x6, Pallas kernels: 26.5 us -> 17.7 us  [the longest x2 11.6 us: attend(): pl.pallas_call(functools.partial(attend_kernel, with_edge), in_specs=[VME...]
    all_to_all x1 -> x0, starting transfers between devices: 8.18 us -> none  [shards(): lax.all_to_all(pack(queries, keys, values, cotangent), plane, split_axis=...]
    reshape x2 -> x0, local copies, waits for them, and re-layouts: 1.65 us -> none  [tile_bias(): return jnp.repeat(jnp.where(hit, 0.0, MASKED).astype(BF16), TILE, axis=1)]
    all_to_all x1, starting transfers between devices: 6.21 us -> 4.81 us  [shards(): lax.all_to_all(gown, plane, split_axis=0, concat_axis=0, tiled=True)]
    all_to_all x1, waiting for transfers between devices: 1.01 us -> 2.4 us  [shards(): lax.all_to_all(packed, plane, split_axis=0, concat_axis=0, tiled=True)]
    unnamed x16 -> x6, local copies, waits for them, and re-layouts: 2.84 us -> 1.5 us
  transfers between devices with their start and end apart: 7 -> 6, of which waited for: 4 -> 4; matrix products, arithmetic and copies ran while one was open for 3% -> 0% of each run, Pallas kernels for 13% -> 10%
where the time goes in v3:
time: 88.8 us; the launch traced here: 87.4 us
  blocking collectives  30.2 us (34%)
  waiting for transfers between devices  23.5 us (26%)
  Pallas kernels  17.7 us (20%)
  starting transfers between devices  13.7 us (15%)
  local copies, waits for them, and re-layouts  1.59 us (2%)
    all_to_all x1, blocking collectives, shards(): mine = lax.all_to_all(sent, plane, split_axis=0, concat_axis=0, tiled=True)  30.2 us
    all_to_all x1, waiting for transfers between devices, shards(): lax.all_to_all(gown, plane, split_axis=0, concat_axis=0, tiled=True)  12.7 us
    pallas_call x2, Pallas kernels, attend(): pl.pallas_call(functools.partial(attend_kernel, with_edge), in_specs=[VME...  11.6 us
    ppermute x1, waiting for transfers between devices, shards(): gedge_in = lax.ppermute(gedge, ('sx', 'co'), across)  7.11 us
    all_to_all x1, starting transfers between devices, shards(): lax.all_to_all(gown, plane, split_axis=0, concat_axis=0, tiled=True)  4.81 us
    all_to_all x1, starting transfers between devices, shards(): lax.all_to_all(packed, plane, split_axis=0, concat_axis=0, tiled=True)  3.81 us
    ppermute x1, starting transfers between devices, shards(): edge = lax.ppermute(kv_edge, ('sx', 'co'), across)  2.53 us
    all_to_all x1, waiting for transfers between devices, shards(): lax.all_to_all(packed, plane, split_axis=0, concat_axis=0, tiled=True)  2.4 us
  transfers between devices with their start and end apart: 6, of which 4 were waited for; matrix products, arithmetic and copies ran while one was open for 0% of the time, Pallas kernels for 10%

profile of v3, /device:TPU:2, one launch (start us, length us, event | category | flops | bytes accessed | tf_op | source)
XLA Modules:
  0.0 87.4 jit_solution(3045559528331581589)
XLA Ops:
  0.6 0.0 copy-start
  0.6 0.7 copy-done
  1.4 1.5 %enter.1 = (bf16[16,4,96,128]{3,2,1,0:T(8,128)(2,1)S(1)}, bf16[2,128,768]{2,1,0:T(8,128)(2,1)S(1)}) custom-call(bf16[96,2048]{1,0:T(8,128)(2,1)} %q_ref.1, bf16[96,2048]{1,0:T(8,128)(2,1)} %k_ref.1, bf16[96,2048]{1,0:T(8,128)(2,1)} %v_ref.1, bf16[96,2048]{1,0:T(8,128)(2,1)} %c_ref.1, s32[27,192]{1,0:T(8,128)S(1)} %bitcast.1), custom_call_target="tpu_custom_call" | custom-call | tf_op jit(solution)/shard_map/enter/pallas_call | solution.py:75
  2.9 30.2 %all_to_all.15.refs_0_ = bf16[16,4,96,128]{3,2,1,0:T(8,128)(2,1)S(1)} all-to-all(bf16[16,4,96,128]{3,2,1,0:T(8,128)(2,1)S(1)} %get-tuple-element.17), channel_id=1, replica_groups=mesh['sx'=4,'yl'=2,'co'=2,'head'=8] {'yl','head'}, dimensions={0} | all-to-all | bytes 3145728 | tf_op jit(solution)/shard_map/enter_all/all_to_all | solution.py:373
  33.1 0.1 slice.4
  33.2 0.1 collective-permute-start
  33.3 2.5 %collective-permute-start.1 = (bf16[8,2,96,128]{3,2,1,0:T(8,128)(2,1)S(1)}, bf16[8,2,96,128]{3,2,1,0:T(8,128)(2,1)S(1)}, u32[]{:S(2)}, u32[]{:S(2)}) collective-permute-start(bf16[8,2,96,128]{3,2,1,0:T(8,128)(2,1)S(1)} %constant_dynamic-slice_fusion), channel_id=1, source_target_pairs={{8,32},{32,8},{40,64},{64,40},{72,96},{96,72},{9,33},{33,9},{41,65... | collective-permute-start | bytes 1179656 | tf_op jit(solution)/shard_map/ppermute | solution.py:377
  35.8 0.0 collective-permute-done.refs_1_
  35.9 5.3 %attend_local.1 = (bf16[8,2,96,128]{3,2,1,0:T(8,128)(2,1)S(1)}, bf16[8,2,96,128]{3,2,1,0:T(8,128)(2,1)S(1)}, bf16[16,2,96,128]{3,2,1,0:T(8,128)(2,1)S(1)}) custom-call(bf16[16,4,96,128]{3,2,1,0:T(8,128)(2,1)S(1)} %all_to_all.15.refs_0_, bf16[16,2,96,128]{3,2,1,0:T(8,128)(2,1)S(1)} %collective-permute-done.refs_1_, ...), custom_call_target="tpu_custom_call" | custom-call | tf_op jit(solution)/shard_map/attend_local/pallas_call | solution.py:314
  41.2 1.2 %collective-permute-done.1.refs_2_ = bf16[8,2,96,128]{3,2,1,0:T(8,128)(2,1)S(1)} collective-permute-done((bf16[8,2,96,128]{3,2,1,0:T(8,128)(2,1)S(1)}, bf16[8,2,96,128]{3,2,1,0:T(8,128)(2,1)S(1)}, u32[]{:S(2)}, u32[]{:S(2)}) %collective-permute-start.1) | collective-permute-done | bytes 393248 | tf_op jit(solution)/shard_map/ppermute | solution.py:377
  42.4 6.2 %attend_edge.1 = (bf16[16,2,96,128]{3,2,1,0:T(8,128)(2,1)}, bf16[16,2,96,128]{3,2,1,0:T(8,128)(2,1)}, bf16[16,2,96,128]{3,2,1,0:T(8,128)(2,1)S(1)}, bf16[8,2,96,128]{3,2,1,0:T(8,128)(2,1)S(1)}) custom-call(bf16[16,4,96,128]{3,2,1,0:T(8,128)(2,1)S(1)} %all_to_all.15.refs_0_, bf16[16,2,96,128]{3,2,1,0:T(8,128)(2,1)S(1)} %collective-permute-done.refs_1_, ...), custom_call_target="tpu_custom_call" | custom-call | tf_op jit(solution)/shard_map/attend_edge/pallas_call | solution.py:314
  48.7 0.0 copy-start.1
  48.7 0.7 copy-done.1
  49.4 0.0 copy-start.2
  49.4 0.5 collective-permute-start.2
  49.9 3.8 %all-to-all-start.1 = ((bf16[16,2,96,128]{3,2,1,0:T(8,128)(2,1)}), bf16[16,2,96,128]{3,2,1,0:T(8,128)(2,1)S(1)}, u32[]{:S(2)}, u32[]{:S(2)}) async-start(bf16[16,2,96,128]{3,2,1,0:T(8,128)(2,1)} %get-tuple-element.22), calls=%async_computation.1 | async-start | bytes 1572864 | tf_op jit(solution)/shard_map/all_to_all | solution.py:380
  53.7 0.0 copy-done.2
  53.7 2.0 %collective-permute-start.3 = (bf16[8,2,96,128]{3,2,1,0:T(8,128)(2,1)S(1)}, bf16[8,2,96,128]{3,2,1,0:T(8,128)(2,1)S(1)}, u32[]{:S(2)}, u32[]{:S(2)}) collective-permute-start(bf16[8,2,96,128]{3,2,1,0:T(8,128)(2,1)S(1)} %copy-done.2), channel_id=1, source_target_pairs={{8,32},{32,8},{40,64},{64,40},{72,96},{96,72},{9,33},{33,9},{41,65... | collective-permute-start | bytes 1179656 | tf_op jit(solution)/shard_map/ppermute | solution.py:382
  55.7 7.1 %collective-permute-done.3.edge_ref = bf16[8,2,96,128]{3,2,1,0:T(8,128)(2,1)S(1)} collective-permute-done((bf16[8,2,96,128]{3,2,1,0:T(8,128)(2,1)S(1)}, bf16[8,2,96,128]{3,2,1,0:T(8,128)(2,1)S(1)}, u32[]{:S(2)}, u32[]{:S(2)}) %collective-permute-start.3) | collective-permute-done | bytes 393248 | tf_op jit(solution)/shard_map/ppermute | solution.py:382
  62.8 0.0 collective-permute-done.2.swap_ref
  62.8 2.4 %join.1 = bf16[16,2,96,128]{3,2,1,0:T(8,128)(2,1)} custom-call(bf16[16,2,96,128]{3,2,1,0:T(8,128)(2,1)} %get-tuple-element.25.own_ref, bf16[16,2,96,128]{3,2,1,0:T(8,128)(2,1)S(1)} %collective-permute-done.2.swap_ref, bf16[8,2,96,128]{3,2,1,0:T(8,128)(2,1)S(1)} %collective-permute-done.3.edge_ref), custom_call_target="tpu_custom_call" | custom-call | tf_op jit(solution)/shard_map/join/pallas_call | solution.py:353
  65.2 2.4 %all-to-all-done.1.in_ref = bf16[16,2,96,128]{3,2,1,0:T(8,128)(2,1)S(1)} async-done(((bf16[16,2,96,128]{3,2,1,0:T(8,128)(2,1)}), bf16[16,2,96,128]{3,2,1,0:T(8,128)(2,1)S(1)}, u32[]{:S(2)}, u32[]{:S(2)}) %all-to-all-start.1) | async-done | bytes 786464 | tf_op jit(solution)/shard_map/all_to_all | solution.py:380
  67.6 4.8 %all-to-all-start.2 = ((bf16[16,2,96,128]{3,2,1,0:T(8,128)(2,1)}), bf16[16,2,96,128]{3,2,1,0:T(8,128)(2,1)S(1)}, u32[]{:S(2)}, u32[]{:S(2)}) async-start(bf16[16,2,96,128]{3,2,1,0:T(8,128)(2,1)} %join.1), calls=%async_computation.2 | async-start | bytes 1572864 | tf_op jit(solution)/shard_map/all_to_all | solution.py:384
  72.4 1.1 %unpack.2 = (bf16[96,2048]{1,0:T(8,128)(2,1)}, bf16[96,2048]{1,0:T(8,128)(2,1)}) custom-call(bf16[16,2,96,128]{3,2,1,0:T(8,128)(2,1)S(1)} %all-to-all-done.1.in_ref), custom_call_target="tpu_custom_call" | custom-call | tf_op jit(solution)/shard_map/unpack/pallas_call | solution.py:108
  73.5 12.7 %all-to-all-done.2.in_ref = bf16[16,2,96,128]{3,2,1,0:T(8,128)(2,1)S(1)} async-done(((bf16[16,2,96,128]{3,2,1,0:T(8,128)(2,1)}), bf16[16,2,96,128]{3,2,1,0:T(8,128)(2,1)S(1)}, u32[]{:S(2)}, u32[]{:S(2)}) %all-to-all-start.2) | async-done | bytes 786464 | tf_op jit(solution)/shard_map/all_to_all | solution.py:384
  86.3 1.1 %unpack.3 = (bf16[96,2048]{1,0:T(8,128)(2,1)}, bf16[96,2048]{1,0:T(8,128)(2,1)}) custom-call(bf16[16,2,96,128]{3,2,1,0:T(8,128)(2,1)S(1)} %all-to-all-done.2.in_ref), custom_call_target="tpu_custom_call" | custom-call | tf_op jit(solution)/shard_map/unpack/pallas_call | solution.py:108
  (1 shorter events, 0.0 us)
Async XLA Ops:
  0.6 0.8 copy-start
  33.2 2.7 %collective-permute-start = (bf16[16,2,96,128]{3,2,1,0:T(8,128)(2,1)S(1)}, bf16[16,2,96,128]{3,2,1,0:T(8,128)(2,1)S(1)}, u32[]{:S(2)}, u32[]{:S(2)}) collective-permute-start(bf16[16,2,96,128]{3,2,1,0:T(8,128)(2,1)S(1)} %slice.4), channel_id=1, source_target_pairs={{0,8},{8,0},{1,9},{9,1},{2,10},{10,2},{3,11},{11,3},{4,12},{12,4},... | collective-permute-start | bytes 2359304 | tf_op jit(solution)/shard_map/ppermute | solution.py:375
  33.3 9.1 %collective-permute-start.1 = (bf16[8,2,96,128]{3,2,1,0:T(8,128)(2,1)S(1)}, bf16[8,2,96,128]{3,2,1,0:T(8,128)(2,1)S(1)}, u32[]{:S(2)}, u32[]{:S(2)}) collective-permute-start(bf16[8,2,96,128]{3,2,1,0:T(8,128)(2,1)S(1)} %constant_dynamic-slice_fusion), channel_id=1, source_target_pairs={{8,32},{32,8},{40,64},{64,40},{72,96},{96,72},{9,33},{33,9},{41,65... | collective-permute-start | bytes 1179656 | tf_op jit(solution)/shard_map/ppermute | solution.py:377
  48.7 0.7 copy-start.1
  49.4 4.3 %copy-start.2 = (bf16[8,2,96,128]{3,2,1,0:T(8,128)(2,1)S(1)}, bf16[8,2,96,128]{3,2,1,0:T(8,128)(2,1)}, u32[]{:S(2)}) copy-start(bf16[8,2,96,128]{3,2,1,0:T(8,128)(2,1)} %copy-done.1) | copy-start | bytes 1179652
  49.4 13.4 %collective-permute-start.2 = (bf16[16,2,96,128]{3,2,1,0:T(8,128)(2,1)S(1)}, bf16[16,2,96,128]{3,2,1,0:T(8,128)(2,1)S(1)}, u32[]{:S(2)}, u32[]{:S(2)}) collective-permute-start(bf16[16,2,96,128]{3,2,1,0:T(8,128)(2,1)S(1)} %get-tuple-element.26), channel_id=1, source_target_pairs={{0,8},{8,0},{1,9},{9,1},{2,10},{10,2},{3,11},{11,3},{4,12},{12,4},... | collective-permute-start | bytes 2359304 | tf_op jit(solution)/shard_map/ppermute | solution.py:381
  49.9 17.7 %all-to-all-start.1 = ((bf16[16,2,96,128]{3,2,1,0:T(8,128)(2,1)}), bf16[16,2,96,128]{3,2,1,0:T(8,128)(2,1)S(1)}, u32[]{:S(2)}, u32[]{:S(2)}) async-start(bf16[16,2,96,128]{3,2,1,0:T(8,128)(2,1)} %get-tuple-element.22), calls=%async_computation.1 | async-start | bytes 1572864 | tf_op jit(solution)/shard_map/all_to_all | solution.py:380
  53.7 9.1 %collective-permute-start.3 = (bf16[8,2,96,128]{3,2,1,0:T(8,128)(2,1)S(1)}, bf16[8,2,96,128]{3,2,1,0:T(8,128)(2,1)S(1)}, u32[]{:S(2)}, u32[]{:S(2)}) collective-permute-start(bf16[8,2,96,128]{3,2,1,0:T(8,128)(2,1)S(1)} %copy-done.2), channel_id=1, source_target_pairs={{8,32},{32,8},{40,64},{64,40},{72,96},{96,72},{9,33},{33,9},{41,65... | collective-permute-start | bytes 1179656 | tf_op jit(solution)/shard_map/ppermute | solution.py:382
  67.6 18.7 %all-to-all-start.2 = ((bf16[16,2,96,128]{3,2,1,0:T(8,128)(2,1)}), bf16[16,2,96,128]{3,2,1,0:T(8,128)(2,1)S(1)}, u32[]{:S(2)}, u32[]{:S(2)}) async-start(bf16[16,2,96,128]{3,2,1,0:T(8,128)(2,1)} %join.1), calls=%async_computation.2 | async-start | bytes 1572864 | tf_op jit(solution)/shard_map/all_to_all | solution.py:384

commit v4 on v3

v4 whole, which is shorter than its diff:
```python
import math

import jax
import jax.numpy as jnp
from jax import lax
from jax.experimental import pallas as pl
from jax.experimental.pallas import tpu as pltpu
from jax.sharding import Mesh, PartitionSpec as P


TILE = 64
TILES_F = 12
HD = 128
FRAME = TILE * TILES_F
BLOCK = 4 * TILE
KEYS = 3 * FRAME
CHUNKS = 8
CHUNK = FRAME // CHUNKS
PLANE = 16
MASKED = -1e30
SCALE = 1.0 / math.sqrt(HD)
LOG2E = 1.4426950408889634
ANY = pl.BlockSpec(memory_space=pl.ANY)
VMEM = pl.BlockSpec(memory_space=pltpu.VMEM)
F32 = jnp.float32
BF16 = jnp.bfloat16


def near(x):
    return pltpu.with_memory_space_constraint(x, pltpu.VMEM)


def far(x):
    return pltpu.with_memory_space_constraint(x, pltpu.HBM)


def room(mib):
    return pltpu.CompilerParams(vmem_limit_bytes=mib * 2**20)


def enter_kernel(q_ref, k_ref, v_ref, c_ref, near_ref, out_ref, bias_ref, near_s, in_s, out_s, in_sem, out_sem):
    listing = pltpu.make_async_copy(near_ref, near_s, in_sem.at[4])
    listing.start()
    ins, outs = [], []
    for a, ref in enumerate((q_ref, k_ref, v_ref, c_ref)):
        ins.append(pltpu.make_async_copy(ref, in_s.at[a], in_sem.at[a]))
        outs.append(pltpu.make_async_copy(out_s.at[a], out_ref.at[:, a], out_sem.at[a]))
        ins[a].start()
    core, first = lax.axis_index("co"), 4 * lax.axis_index("sx")
    partner = first + 1 - core
    local, outer = first + 2 - core, first + 3 * core
    places = (
        (local, (partner, local, partner + 2)),
        (outer, (first - 1 + 5 * core, outer, partner + 2 * core)),
    )
    tiles = near_ref.shape[1]
    slot = lax.broadcasted_iota(jnp.int32, (HD, 1), 0)
    listing.wait()
    listed = near_s[...]
    for which, (frame, keyed) in enumerate(places):
        base = jnp.zeros_like(slot)
        for i, k in enumerate(keyed):
            base = jnp.where(slot // TILES_F == i, k, base)
        tile = base * TILES_F + slot % TILES_F
        tile = jnp.where(tile < 0, -TILES_F, tile)
        hit = jnp.zeros((HD, tiles), F32)
        for j in range(listed.shape[0]):
            hit = jnp.where(listed[j : j + 1, :] == tile, 1.0, hit)
        owner = lax.broadcasted_iota(jnp.int32, (tiles, FRAME), 1) // TILE + frame * TILES_F
        spread = (owner == lax.broadcasted_iota(jnp.int32, (tiles, FRAME), 0)).astype(F32).astype(BF16)
        bias_ref[which] = jnp.where(nn(hit.astype(BF16), spread) > 0.5, 0.0, MASKED).astype(BF16)
    for a in range(4):
        ins[a].wait()
        for g in range(PLANE):
            out_s[a, g] = in_s[a, :, g * HD : (g + 1) * HD]
        outs[a].start()
    for cp in outs:
        cp.wait()


def enter(q, k, v, c, neighbours):
    return pl.pallas_call(
        enter_kernel,
        in_specs=[ANY] * 5,
        out_specs=(ANY, VMEM),
        out_shape=(
            jax.ShapeDtypeStruct((PLANE, 4, CHUNK, HD), BF16),
            jax.ShapeDtypeStruct((2, HD, FRAME), BF16),
        ),
        scratch_shapes=[
            pltpu.VMEM(neighbours.shape[::-1], jnp.int32),
            pltpu.VMEM((4, CHUNK, PLANE * HD), BF16),
            pltpu.VMEM((4, PLANE, CHUNK, HD), BF16),
            pltpu.SemaphoreType.DMA((5,)),
            pltpu.SemaphoreType.DMA((4,)),
        ],
        compiler_params=room(12),
        name="enter",
    )(far(q), far(k), far(v), far(c), far(neighbours.T))


def unpack_kernel(in_ref, *refs):
    sem = refs[-1]
    copies = []
    for a, ref in enumerate(refs[:-1]):
        for g in range(PLANE):
            part = ref.at[:, g * HD : (g + 1) * HD]
            copies.append(pltpu.make_async_copy(in_ref.at[g, a], part, sem.at[a, g]))
    for cp in copies:
        cp.start()
    for cp in copies:
        cp.wait()


def unpack(packed):
    return pl.pallas_call(
        unpack_kernel,
        in_specs=[VMEM],
        out_specs=(ANY,) * 4,
        out_shape=(jax.ShapeDtypeStruct((CHUNK, PLANE * HD), BF16),) * 4,
        scratch_shapes=[pltpu.SemaphoreType.DMA((4, PLANE))],
        compiler_params=room(4),
        name="unpack",
    )(near(packed))


def nt(a, b):
    return lax.dot_general(a, b, (((1,), (1,)), ((), ())), preferred_element_type=F32)


def nn(a, b):
    return lax.dot_general(a, b, (((1,), (0,)), ((), ())), preferred_element_type=F32)


def group_rows(x):
    return x.reshape(x.shape[0] // 8, 8, x.shape[1])


def marks(shape, dim, row):
    return (lax.broadcasted_iota(jnp.int32, shape, dim) == row).astype(F32)


SPANS = ((0, 2 * BLOCK), (0, 3 * BLOCK), (BLOCK, 2 * BLOCK))


def tokens(ref):
    return ref.reshape(ref.shape[0] * ref.shape[1], HD)


def keys(s, lo, n):
    return slice(s * FRAME + lo, s * FRAME + lo + n)


def block(r):
    return slice(r * BLOCK, (r + 1) * BLOCK)


def fetch(ref, index, a, dst):
    for h in range(CHUNKS):
        dst[h] = ref[index * CHUNKS + h, a]


def put(src, ref, index, a):
    for h in range(CHUNKS):
        ref[index * CHUNKS + h, a] = src[h]


class Scores:
    def __init__(self, k, hot, vt, qt, ct, c2, s, p, out):
        self.k, self.hot, self.vt, self.qt, self.ct, self.c2, self.s, self.p, self.out = k, hot, vt, qt, ct, c2, s, p, out
        self.tops, self.sums = {}, {}
        lane = lax.broadcasted_iota(jnp.int32, (TILE, HD), 1)
        for t in range(3 * TILES_F):
            hot[t * TILE : (t + 1) * TILE, :] = (lane == t).astype(F32).astype(BF16)
        vt[HD:, :] = marks((16, KEYS), 0, 0).astype(BF16)

    def score(self, r, s):
        lo, n = SPANS[r]
        kf = tokens(self.k)
        qt = self.qt[:, block(r)]
        for b in range(n // BLOCK):
            ks = keys(s, lo + b * BLOCK, BLOCK)
            st = nn(jnp.concatenate([kf[ks, :], self.hot[ks, :]], axis=1), qt)
            self.s[r, s * n + b * BLOCK : s * n + (b + 1) * BLOCK, :] = st
            got = jnp.max(group_rows(st), axis=0)
            self.tops[r] = jnp.maximum(self.tops[r], got) if r in self.tops else got
        if s == 2:
            self.tops[r] = jnp.max(self.tops[r], axis=0, keepdims=True) * (SCALE * LOG2E)

    def soften(self, r, s):
        lo, n = SPANS[r]
        for t in range(n // TILE):
            x = self.s[r, s * n + t * TILE : s * n + (t + 1) * TILE, :]
            e = jnp.exp2(x * (SCALE * LOG2E) - self.tops[r])
            self.p[s][lo + t * TILE : lo + (t + 1) * TILE, block(r)] = e.astype(BF16)
        got = nn(self.vt[:, keys(s, lo, n)], self.p[s][lo : lo + n, block(r)])
        self.sums[r] = self.sums[r] + got if r in self.sums else got

    def finish(self, r):
        cols = block(r)
        ot = self.sums[r]
        inv = 1.0 / ot[HD : HD + 1]
        out = (ot[:HD] * inv).astype(BF16)
        tokens(self.out)[cols, :] = out.T
        c2 = (self.ct[:, cols].astype(F32) * (inv * SCALE)).astype(BF16)
        self.c2[:HD, cols] = c2
        dots = -jnp.sum(c2.astype(F32) * out.astype(F32), axis=0, keepdims=True)
        high = dots.astype(BF16).astype(F32)
        mid = (dots - high).astype(BF16).astype(F32)
        low = dots - high - mid
        shape = (HD, BLOCK)
        tail = marks(shape, 0, 0) * high + marks(shape, 0, 1) * mid + marks(shape, 0, 2) * low
        self.c2[HD:, cols] = tail.astype(BF16)


class Grads:
    def __init__(self, v, kt, qt, c2, p, d):
        self.v, self.kt, self.qt, self.c2, self.p, self.d = v, kt, qt, c2, p, d
        self.sums = {}
        self.unit = (lax.broadcasted_iota(jnp.int32, (BLOCK, HD), 1) < 3).astype(F32).astype(BF16)

    def back(self, r, s):
        lo, n = SPANS[r]
        cols = block(r)
        vf = tokens(self.v)
        for b in range(n // BLOCK):
            at = slice(lo + b * BLOCK, lo + (b + 1) * BLOCK)
            rows = jnp.concatenate([vf[keys(s, lo + b * BLOCK, BLOCK), :], self.unit], axis=1)
            dp = nn(rows, self.c2[:, cols])
            self.d[s][at, cols] = self.p[s][at, cols] * dp.astype(BF16)
        got = nn(self.kt[:, keys(s, lo, n)], self.d[s][lo : lo + n, cols])
        self.sums[r] = self.sums[r] + got if r in self.sums else got

    def keyed(self, s, a):
        for b, (lo, n) in enumerate(SPANS):
            if a == 0:
                g = nt(self.qt[:HD, lo : lo + n], self.d[s][block(b), lo : lo + n])
            else:
                g = nt(self.c2[:HD, lo : lo + n], self.p[s][block(b), lo : lo + n]) * (1.0 / SCALE)
            yield block(b), g.astype(BF16).T


def run_scores(sc, ready):
    for s in range(3):
        sc.score(0, s)
    ready()
    for s in range(3):
        sc.score(1, s)
        sc.soften(0, s)
    sc.finish(0)
    for s in range(3):
        sc.score(2, s)
        sc.soften(1, s)
    sc.finish(1)


def local_kernel(
    mine_ref, swap_ref, bias_ref, out_ref, gown_ref, gswap_ref,
    q_s, c_s, o_s, g_s, k_s, v_s, hot_s, kt_s, vt_s, qt_s, ct_s, c2_s, s_s, p_s, d_s,
):
    frame = 1 - lax.axis_index("co")
    fetch(mine_ref, frame, 0, q_s)
    for a, dst in ((0, k_s), (1, v_s)):
        for s in range(3):
            for h in range(CHUNKS):
                dst[s * CHUNKS + h] = mine_ref[frame * CHUNKS + h, 1 + a] if s == 1 else swap_ref[s // 2 * CHUNKS + h, a]
    fetch(mine_ref, frame, 3, c_s)
    qt_s[:HD, :] = tokens(q_s)[...].T
    qt_s[HD:, :] = bias_ref[0]
    ps, ds = [p_s.at[s] for s in range(3)], [d_s.at[s] for s in range(3)]
    sc = Scores(k_s, hot_s, vt_s, qt_s, ct_s, c2_s, s_s, ps, o_s)
    gr = Grads(v_s, kt_s, qt_s, c2_s, ps, ds)

    def ready():
        vt_s[:HD, :] = tokens(v_s)[...].T
        ct_s[...] = tokens(c_s)[...].T

    run_scores(sc, ready)
    kt_s[...] = tokens(k_s)[...].T
    for s in range(3):
        gr.back(0, s)
        sc.soften(2, s)
    sc.finish(2)
    for s in range(3):
        gr.back(1, s)
        gr.back(2, s)
    for r in range(3):
        tokens(q_s)[block(r), :] = gr.sums[r].astype(BF16).T
    put(o_s, out_ref, 0, 0)
    put(q_s, out_ref, 0, 1)
    for s in (0, 2, 1):
        for a in range(2):
            for rows, g in gr.keyed(s, a):
                tokens(g_s.at[a, s])[rows, :] = g
            if s == 1:
                put(g_s.at[a, s], gown_ref, 0, a)
            else:
                put(g_s.at[a, s], gswap_ref, s // 2, a)


def outer_kernel(
    mine_ref, swap_ref, edge_ref, bias_ref, out_ref, p_ref, qt_ref, c2_ref, dqt_ref, gedge_ref,
    q_s, c_s, o_s, g_s, k_s, v_s, hot_s, kt_s, vt_s, ct_s, s_s, p_s, d_s,
):
    core = lax.axis_index("co")
    fetch(mine_ref, core, 0, q_s)
    for a, dst in ((0, k_s), (1, v_s)):
        for h in range(CHUNKS):
            dst[h] = edge_ref[h, a]
            dst[CHUNKS + h] = mine_ref[core * CHUNKS + h, 1 + a]
            dst[2 * CHUNKS + h] = swap_ref[core * CHUNKS + h, a]
    fetch(mine_ref, core, 3, c_s)
    qt_ref[:HD, :] = tokens(q_s)[...].T
    qt_ref[HD:, :] = bias_ref[1]
    ps = [p_s, p_ref.at[0], p_ref.at[1]]
    sc = Scores(k_s, hot_s, vt_s, qt_ref, ct_s, c2_ref, s_s, ps, o_s)
    gr = Grads(v_s, kt_s, qt_ref, c2_ref, ps, [d_s])

    def ready():
        vt_s[:HD, :] = tokens(v_s)[...].T
        ct_s[...] = tokens(c_s)[...].T

    run_scores(sc, ready)
    kt_s[...] = tokens(k_s)[:FRAME, :].T
    gr.back(0, 0)
    for s in range(3):
        sc.soften(2, s)
    sc.finish(2)
    gr.back(1, 0)
    gr.back(2, 0)
    for r in range(3):
        dqt_ref[:, block(r)] = gr.sums[r]
    put(o_s, out_ref, 0, 0)
    for a in range(2):
        for rows, g in gr.keyed(0, a):
            tokens(g_s.at[a])[rows, :] = g
        put(g_s.at[a], gedge_ref, 0, a)


def inner_kernel(
    mine_ref, swap_ref, p_ref, qt_ref, c2_ref, dqt_ref, old_ref, dq_ref, gown_ref, gswap_ref,
    g_s, k_s, v_s, kt_s, d_s,
):
    core = lax.axis_index("co")
    for a, dst in ((0, k_s), (1, v_s)):
        for h in range(CHUNKS):
            dst[h] = mine_ref[core * CHUNKS + h, 1 + a]
            dst[CHUNKS + h] = swap_ref[core * CHUNKS + h, a]
    gr = Grads(v_s, kt_s, qt_ref, c2_ref, [p_ref.at[s] for s in range(2)], [d_s.at[s] for s in range(2)])
    kt_s[...] = tokens(k_s)[...].T
    for r in range(3):
        for s in range(2):
            gr.back(r, s)
    for r in range(3):
        tokens(g_s.at[0, 0])[block(r), :] = (gr.sums[r] + dqt_ref[:, block(r)]).astype(BF16).T
    for h in range(CHUNKS):
        dq_ref[h] = g_s[0, 0, h]
    for s in (1, 0):
        for a in range(2):
            for rows, g in gr.keyed(s, a):
                tokens(g_s.at[a, s])[rows, :] = g
            for h in range(CHUNKS):
                if s == 0:
                    gown_ref[h, a] = g_s[a, s, h]
                else:
                    both = g_s[a, s, h].astype(F32) + old_ref[core * CHUNKS + h, a].astype(F32)
                    gswap_ref[core * CHUNKS + h, a] = both.astype(BF16)
                    gswap_ref[(1 - core) * CHUNKS + h, a] = old_ref[(1 - core) * CHUNKS + h, a]


PAIR = jax.ShapeDtypeStruct((PLANE, 2, CHUNK, HD), BF16)
HALF = jax.ShapeDtypeStruct((CHUNKS, 2, CHUNK, HD), BF16)
ONE = jax.ShapeDtypeStruct((CHUNKS, CHUNK, HD), BF16)


def frames(*shape):
    return pltpu.VMEM((*shape, CHUNK, HD), BF16)


def wide(rows):
    return pltpu.VMEM((rows, FRAME), BF16)


def attend_local(mine, swap, bias):
    square = pltpu.VMEM((3, FRAME, FRAME), BF16)
    return pl.pallas_call(
        local_kernel,
        in_specs=[VMEM] * 3,
        out_specs=(VMEM,) * 3,
        out_shape=(HALF, HALF, PAIR),
        scratch_shapes=[
            frames(CHUNKS),
            frames(CHUNKS),
            frames(CHUNKS),
            frames(2, 3, CHUNKS),
            frames(3 * CHUNKS),
            frames(3 * CHUNKS),
            pltpu.VMEM((KEYS, HD), BF16),
            pltpu.VMEM((HD, KEYS), BF16),
            pltpu.VMEM((HD + 16, KEYS), BF16),
            wide(2 * HD),
            wide(HD),
            wide(2 * HD),
            pltpu.VMEM((3, 9 * BLOCK, BLOCK), F32),
            square,
            square,
        ],
        compiler_params=room(26),
        name="attend_local",
    )(near(mine), near(swap), bias)


def attend_outer(mine, swap, edge, bias):
    return pl.pallas_call(
        outer_kernel,
        in_specs=[VMEM] * 4,
        out_specs=(VMEM,) * 6,
        out_shape=(
            jax.ShapeDtypeStruct((CHUNKS, 1, CHUNK, HD), BF16),
            jax.ShapeDtypeStruct((2, FRAME, FRAME), BF16),
            jax.ShapeDtypeStruct((2 * HD, FRAME), BF16),
            jax.ShapeDtypeStruct((2 * HD, FRAME), BF16),
            jax.ShapeDtypeStruct((HD, FRAME), F32),
            HALF,
        ),
        scratch_shapes=[
            frames(CHUNKS),
            frames(CHUNKS),
            frames(CHUNKS),
            frames(2, CHUNKS),
            frames(3 * CHUNKS),
            frames(3 * CHUNKS),
            pltpu.VMEM((KEYS, HD), BF16),
            wide(HD),
            pltpu.VMEM((HD + 16, KEYS), BF16),
            wide(HD),
            pltpu.VMEM((3, 9 * BLOCK, BLOCK), F32),
            wide(FRAME),
            wide(FRAME),
        ],
        compiler_params=room(26),
        name="attend_outer",
    )(near(mine), near(swap), near(edge), bias)


def attend_inner(mine, swap, p, qt, c2, dqt, old):
    return pl.pallas_call(
        inner_kernel,
        in_specs=[VMEM] * 7,
        out_specs=(VMEM,) * 3,
        out_shape=(ONE, HALF, PAIR),
        scratch_shapes=[
            frames(2, 2, CHUNKS),
            frames(2 * CHUNKS),
            frames(2 * CHUNKS),
            pltpu.VMEM((HD, 2 * FRAME), BF16),
            pltpu.VMEM((2, FRAME, FRAME), BF16),
        ],
        compiler_params=room(14),
        name="attend_inner",
    )(near(mine), near(swap), p, qt, c2, dqt, old)


def join_kernel(local_ref, outer_ref, dq_ref, lown_ref, eown_ref, swap_ref, edge_ref, out_ref):
    core = lax.axis_index("co")
    for h in range(CHUNKS):
        here, there = core * CHUNKS + h, (1 - core) * CHUNKS + h
        out_ref[there, 0] = local_ref[h, 0]
        out_ref[there, 1] = local_ref[h, 1]
        out_ref[here, 0] = outer_ref[h, 0]
        out_ref[here, 1] = dq_ref[h]
        for a in range(2):
            x = lown_ref[h, a].astype(F32) + swap_ref[there, a].astype(F32)
            out_ref[there, 2 + a] = x.astype(BF16)
            x = eown_ref[h, a].astype(F32) + swap_ref[here, a].astype(F32)
            out_ref[here, 2 + a] = (x + edge_ref[h, a].astype(F32)).astype(BF16)


def join(*parts):
    swap, edge = parts[-2:]
    return pl.pallas_call(
        join_kernel,
        in_specs=[VMEM] * 7,
        out_specs=VMEM,
        out_shape=jax.ShapeDtypeStruct((PLANE, 4, CHUNK, HD), BF16),
        compiler_params=room(10),
        name="join",
    )(*parts[:-2], near(swap), near(edge))


def shards(queries, keys, values, cotangent, neighbours):
    plane = ("yl", "head")
    ring = lax.axis_size("sx")
    across = []
    for i in range(ring - 1):
        across.append((2 * i + 1, 2 * i + 2))
        across.append((2 * i + 2, 2 * i + 1))
    swap_pairs = [(0, 1), (1, 0)]
    core = lax.axis_index("co")
    sent, bias = enter(queries, keys, values, cotangent, neighbours)
    mine = lax.all_to_all(sent, plane, split_axis=0, concat_axis=0, tiled=True)
    kv = mine[:, 1:3]
    swap = lax.ppermute(kv, "co", swap_pairs)
    kv_edge = lax.dynamic_slice_in_dim(kv, core * CHUNKS, CHUNKS, 0)
    edge = lax.ppermute(kv_edge, ("sx", "co"), across)
    local, lown, lswap = attend_local(mine, swap, bias)
    outer, *kept, gedge = attend_outer(mine, swap, edge, bias)
    gedge_in = lax.ppermute(gedge, ("sx", "co"), across)
    dq, eown, gswap = attend_inner(mine, swap, *kept, lswap)
    gswap_in = lax.ppermute(gswap, "co", swap_pairs)
    packed = join(local, outer, dq, lown, eown, gswap_in, gedge_in)
    return unpack(lax.all_to_all(packed, plane, split_axis=0, concat_axis=0, tiled=True))


def solution(mesh):
    view = Mesh(mesh.devices.reshape(mesh.devices.shape[0] // 4, 2, 2, -1), ("sx", "yl", "co", "head"))
    rows = P(("sx", "yl", "co", "head"), None)
    return jax.shard_map(
        shards,
        mesh=view,
        in_specs=(rows,) * 4 + (P(),),
        out_specs=(rows,) * 4,
        check_vma=False,
    )
```

time: 88.8 us -> 86.3 us (0.972); the launches traced: 87.4 us -> 86 us
  blocking collectives: 30.2 us -> 56.4 us
  waiting for transfers between devices: 23.5 us -> 8.21 us
  starting transfers between devices: 13.7 us -> 5.23 us
  Pallas kernels: 17.7 us -> 15.4 us
  local copies, waits for them, and re-layouts: 1.59 us -> 0.09 us
    all_to_all x0 -> x1, blocking collectives: none -> 26.2 us  [shards(): lax.all_to_all(packed, plane, split_axis=0, concat_axis=0, tiled=True)]
    all_to_all x2 -> x0, waiting for transfers between devices: 15.1 us -> none  [the longest x1 12.7 us: shards(): lax.all_to_all(gown, plane, split_axis=0, concat_axis=0, tiled=True)]
    all_to_all x2 -> x0, starting transfers between devices: 8.62 us -> none  [the longest x1 4.81 us: shards(): lax.all_to_all(gown, plane, split_axis=0, concat_axis=0, tiled=True)]
    pallas_call x6, Pallas kernels: 17.7 us -> 15.4 us  [the longest x1 5.35 us: attend_local(): pl.pallas_call(local_kernel, in_specs=[VMEM] * 3, out_specs=(VMEM,) * 3,...]
    unnamed x6 -> x0, local copies, waits for them, and re-layouts: 1.5 us -> none
  transfers between devices with their start and end apart: 6 -> 4, of which waited for: 4 -> 2; matrix products, arithmetic and copies ran while one was open for 0% -> 0% of each run, Pallas kernels for 10% -> 6%
where the time goes in v4:
time: 86.3 us; the launch traced here: 86 us
  blocking collectives  56.4 us (65%)
  Pallas kernels  15.4 us (18%)
  waiting for transfers between devices  8.21 us (10%)
  starting transfers between devices  5.23 us (6%)
    all_to_all x1, blocking collectives, shards(): mine = lax.all_to_all(sent, plane, split_axis=0, concat_axis=0, tiled=True)  30.2 us
    all_to_all x1, blocking collectives, shards(): lax.all_to_all(packed, plane, split_axis=0, concat_axis=0, tiled=True)  26.2 us
    ppermute x1, waiting for transfers between devices, shards(): gedge_in = lax.ppermute(gedge, ('sx', 'co'), across)  7.01 us
    pallas_call x1, Pallas kernels, attend_local(): pl.pallas_call(local_kernel, in_specs=[VMEM] * 3, out_specs=(VMEM,) * 3,...  5.35 us
    pallas_call x1, Pallas kernels, attend_outer(): pl.pallas_call(outer_kernel, in_specs=[VMEM] * 4, out_specs=(VMEM,) * 6,...  3.69 us
    ppermute x1, starting transfers between devices, shards(): edge = lax.ppermute(kv_edge, ('sx', 'co'), across)  2.53 us
    pallas_call x1, Pallas kernels, attend_inner(): pl.pallas_call(inner_kernel, in_specs=[VMEM] * 7, out_specs=(VMEM,) * 3,...  2.38 us
    pallas_call x1, Pallas kernels, enter(): pl.pallas_call(enter_kernel, in_specs=[ANY] * 5, out_specs=(ANY, VMEM), o...  2.08 us
  transfers between devices with their start and end apart: 4, of which 2 were waited for; matrix products, arithmetic and copies ran while one was open for 0% of the time, Pallas kernels for 6%

profile of v4, /device:TPU:2, one launch (start us, length us, event | category | flops | bytes accessed | tf_op | source)
XLA Modules:
  0.0 86.0 jit_solution(434212845509469418)
XLA Ops:
  0.6 2.1 %enter.1 = (bf16[16,4,96,128]{3,2,1,0:T(8,128)(2,1)S(1)}, bf16[2,128,768]{2,1,0:T(8,128)(2,1)S(1)}) custom-call(bf16[96,2048]{1,0:T(8,128)(2,1)} %q_ref.1, bf16[96,2048]{1,0:T(8,128)(2,1)} %k_ref.1, bf16[96,2048]{1,0:T(8,128)(2,1)} %v_ref.1, bf16[96,2048]{1,0:T(8,128)(2,1)} %c_ref.1, s32[27,192]{1,0:T(8,128)} %bitcast.1), custom_call_target="tpu_custom_call" | custom-call | tf_op jit(solution)/shard_map/enter/pallas_call | solution.py:82
  2.7 30.2 %all_to_all.10.mine_ref = bf16[16,4,96,128]{3,2,1,0:T(8,128)(2,1)S(1)} all-to-all(bf16[16,4,96,128]{3,2,1,0:T(8,128)(2,1)S(1)} %get-tuple-element.18), channel_id=1, replica_groups=mesh['sx'=4,'yl'=2,'co'=2,'head'=8] {'yl','head'}, dimensions={0} | all-to-all | bytes 3145728 | tf_op jit(solution)/shard_map/all_to_all | solution.py:501
  32.9 0.1 slice.4
  32.9 0.1 collective-permute-start
  33.1 2.5 %collective-permute-start.1 = (bf16[8,2,96,128]{3,2,1,0:T(8,128)(2,1)S(1)}, bf16[8,2,96,128]{3,2,1,0:T(8,128)(2,1)S(1)}, u32[]{:S(2)}, u32[]{:S(2)}) collective-permute-start(bf16[8,2,96,128]{3,2,1,0:T(8,128)(2,1)S(1)} %constant_dynamic-slice_fusion), channel_id=1, source_target_pairs={{8,32},{32,8},{40,64},{64,40},{72,96},{96,72},{9,33},{33,9},{41,65... | collective-permute-start | bytes 1179656 | tf_op jit(solution)/shard_map/ppermute | solution.py:505
  35.6 0.0 collective-permute-done.swap_ref
  35.6 5.3 %attend_local.1 = (bf16[8,2,96,128]{3,2,1,0:T(8,128)(2,1)S(1)}, bf16[8,2,96,128]{3,2,1,0:T(8,128)(2,1)S(1)}, bf16[16,2,96,128]{3,2,1,0:T(8,128)(2,1)S(1)}) custom-call(bf16[16,4,96,128]{3,2,1,0:T(8,128)(2,1)S(1)} %all_to_all.10.mine_ref, bf16[16,2,96,128]{3,2,1,0:T(8,128)(2,1)S(1)} %collective-permute-done.swap_ref, ...), custom_call_target="tpu_custom_call" | custom-call | tf_op jit(solution)/shard_map/attend_local/pallas_call | solution.py:386
  41.0 1.2 %collective-permute-done.1.edge_ref = bf16[8,2,96,128]{3,2,1,0:T(8,128)(2,1)S(1)} collective-permute-done((bf16[8,2,96,128]{3,2,1,0:T(8,128)(2,1)S(1)}, bf16[8,2,96,128]{3,2,1,0:T(8,128)(2,1)S(1)}, u32[]{:S(2)}, u32[]{:S(2)}) %collective-permute-start.1) | collective-permute-done | bytes 393248 | tf_op jit(solution)/shard_map/ppermute | solution.py:505
  42.2 3.7 %attend_outer.1 = (bf16[8,1,96,128]{3,2,1,0:T(8,128)(2,1)S(1)}, bf16[2,768,768]{2,1,0:T(8,128)(2,1)S(1)}, bf16[256,768]{1,0:T(8,128)(2,1)S(1)}, bf16[256,768]{1,...) custom-call(bf16[16,4,96,128]{3,2,1,0:T(8,128)(2,1)S(1)} %all_to_all.10.mine_ref, ...), custom_call_target="tpu_custom_call" | custom-call | tf_op jit(solution)/shard_map/attend_outer/pallas_call | solution.py:414
  45.9 2.4 %attend_inner.1 = (bf16[8,96,128]{2,1,0:T(8,128)(2,1)S(1)}, bf16[8,2,96,128]{3,2,1,0:T(8,128)(2,1)S(1)}, bf16[16,2,96,128]{3,2,1,0:T(8,128)(2,1)S(1)}) custom-call(bf16[16,4,96,128]{3,2,1,0:T(8,128)(2,1)S(1)} %all_to_all.10.mine_ref, bf16[16,2,96,128]{3,2,1,0:T(8,128)(2,1)S(1)} %collective-permute-done.swap_ref, ...), custom_call_target="tpu_custom_call" | custom-call | tf_op jit(solution)/shard_map/attend_inner/pallas_call | solution.py:447
  48.3 0.6 collective-permute-start.2
  48.8 2.1 %collective-permute-start.3 = (bf16[8,2,96,128]{3,2,1,0:T(8,128)(2,1)S(1)}, bf16[8,2,96,128]{3,2,1,0:T(8,128)(2,1)S(1)}, u32[]{:S(2)}, u32[]{:S(2)}) collective-permute-start(bf16[8,2,96,128]{3,2,1,0:T(8,128)(2,1)S(1)} %get-tuple-element.31), channel_id=1, source_target_pairs={{8,32},{32,8},{40,64},{64,40},{72,96},{96,72},{9,33},{33,9},{41,65... | collective-permute-start | bytes 1179656 | tf_op jit(solution)/shard_map/ppermute | solution.py:508
  50.9 7.0 %collective-permute-done.3.edge_ref = bf16[8,2,96,128]{3,2,1,0:T(8,128)(2,1)S(1)} collective-permute-done((bf16[8,2,96,128]{3,2,1,0:T(8,128)(2,1)S(1)}, bf16[8,2,96,128]{3,2,1,0:T(8,128)(2,1)S(1)}, u32[]{:S(2)}, u32[]{:S(2)}) %collective-permute-start.3) | collective-permute-done | bytes 393248 | tf_op jit(solution)/shard_map/ppermute | solution.py:508
  57.9 0.0 collective-permute-done.2.swap_ref
  57.9 0.2 join.1
  58.2 26.2 %all_to_all.11.in_ref = bf16[16,4,96,128]{3,2,1,0:T(8,128)(2,1)S(1)} all-to-all(bf16[16,4,96,128]{3,2,1,0:T(8,128)(2,1)S(1)} %join.1), channel_id=1, replica_groups=mesh['sx'=4,'yl'=2,'co'=2,'head'=8] {'yl','head'}, dimensions={0} | all-to-all | bytes 3145728 | tf_op jit(solution)/shard_map/all_to_all | solution.py:512
  84.4 1.7 %unpack.1 = (bf16[96,2048]{1,0:T(8,128)(2,1)}, bf16[96,2048]{1,0:T(8,128)(2,1)}, bf16[96,2048]{1,0:T(8,128)(2,1)}, bf16[96,2048]{1,0:T(8,128)(2,1)}) custom-call(bf16[16,4,96,128]{3,2,1,0:T(8,128)(2,1)S(1)} %all_to_all.11.in_ref), custom_call_target="tpu_custom_call" | custom-call | tf_op jit(solution)/shard_map/unpack/pallas_call | solution.py:116
  (1 shorter events, 0.0 us)
Async XLA Ops:
  32.9 2.7 %collective-permute-start = (bf16[16,2,96,128]{3,2,1,0:T(8,128)(2,1)S(1)}, bf16[16,2,96,128]{3,2,1,0:T(8,128)(2,1)S(1)}, u32[]{:S(2)}, u32[]{:S(2)}) collective-permute-start(bf16[16,2,96,128]{3,2,1,0:T(8,128)(2,1)S(1)} %slice.4), channel_id=1, source_target_pairs={{0,8},{8,0},{1,9},{9,1},{2,10},{10,2},{3,11},{11,3},{4,12},{12,4},... | collective-permute-start | bytes 2359304 | tf_op jit(solution)/shard_map/ppermute | solution.py:503
  33.1 9.1 %collective-permute-start.1 = (bf16[8,2,96,128]{3,2,1,0:T(8,128)(2,1)S(1)}, bf16[8,2,96,128]{3,2,1,0:T(8,128)(2,1)S(1)}, u32[]{:S(2)}, u32[]{:S(2)}) collective-permute-start(bf16[8,2,96,128]{3,2,1,0:T(8,128)(2,1)S(1)} %constant_dynamic-slice_fusion), channel_id=1, source_target_pairs={{8,32},{32,8},{40,64},{64,40},{72,96},{96,72},{9,33},{33,9},{41,65... | collective-permute-start | bytes 1179656 | tf_op jit(solution)/shard_map/ppermute | solution.py:505
  48.3 9.6 %collective-permute-start.2 = (bf16[16,2,96,128]{3,2,1,0:T(8,128)(2,1)S(1)}, bf16[16,2,96,128]{3,2,1,0:T(8,128)(2,1)S(1)}, u32[]{:S(2)}, u32[]{:S(2)}) collective-permute-start(bf16[16,2,96,128]{3,2,1,0:T(8,128)(2,1)S(1)} %get-tuple-element.30), channel_id=1, source_target_pairs={{0,8},{8,0},{1,9},{9,1},{2,10},{10,2},{3,11},{11,3},{4,12},{12,4},... | collective-permute-start | bytes 2359304 | tf_op jit(solution)/shard_map/ppermute | solution.py:510
  48.8 9.1 %collective-permute-start.3 = (bf16[8,2,96,128]{3,2,1,0:T(8,128)(2,1)S(1)}, bf16[8,2,96,128]{3,2,1,0:T(8,128)(2,1)S(1)}, u32[]{:S(2)}, u32[]{:S(2)}) collective-permute-start(bf16[8,2,96,128]{3,2,1,0:T(8,128)(2,1)S(1)} %get-tuple-element.31), channel_id=1, source_target_pairs={{8,32},{32,8},{40,64},{64,40},{72,96},{96,72},{9,33},{33,9},{41,65... | collective-permute-start | bytes 1179656 | tf_op jit(solution)/shard_map/ppermute | solution.py:508

commit v5 on v4

v5 whole, which is shorter than its diff:
```python
import math

import jax
import jax.numpy as jnp
from jax import lax
from jax.experimental import pallas as pl
from jax.experimental.pallas import tpu as pltpu
from jax.sharding import Mesh, PartitionSpec as P


TILE = 64
TILES_F = 12
HD = 128
FRAME = TILE * TILES_F
BLOCK = 4 * TILE
KEYS = 3 * FRAME
CHUNKS = 8
CHUNK = FRAME // CHUNKS
PLANE = 16
MASKED = -1e30
SCALE = 1.0 / math.sqrt(HD)
LOG2E = 1.4426950408889634
ANY = pl.BlockSpec(memory_space=pl.ANY)
VMEM = pl.BlockSpec(memory_space=pltpu.VMEM)
F32 = jnp.float32
BF16 = jnp.bfloat16


def near(x):
    return pltpu.with_memory_space_constraint(x, pltpu.VMEM)


def far(x):
    return pltpu.with_memory_space_constraint(x, pltpu.HBM)


def room(mib):
    return pltpu.CompilerParams(vmem_limit_bytes=mib * 2**20)


def enter_kernel(q_ref, k_ref, v_ref, c_ref, out_ref, in_s, in_sem):
    ins = []
    for a, ref in enumerate((q_ref, k_ref, v_ref, c_ref)):
        ins.append(pltpu.make_async_copy(ref, in_s.at[a], in_sem.at[a]))
        ins[a].start()
    for a in range(4):
        ins[a].wait()
        for g in range(PLANE):
            out_ref[g, a] = in_s[a, :, g * HD : (g + 1) * HD]


def enter(*parts):
    return pl.pallas_call(
        enter_kernel,
        in_specs=[ANY] * 4,
        out_specs=VMEM,
        out_shape=jax.ShapeDtypeStruct((PLANE, 4, CHUNK, HD), BF16),
        scratch_shapes=[pltpu.VMEM((4, CHUNK, PLANE * HD), BF16), pltpu.SemaphoreType.DMA((4,))],
        compiler_params=room(8),
        name="enter",
    )(*(far(x) for x in parts))


def unpack_kernel(in_ref, *refs):
    outs, (rows_s, sem) = refs[:-2], refs[-2:]
    copies = []
    for a, ref in enumerate(outs):
        for g in range(PLANE):
            rows_s[a, :, g * HD : (g + 1) * HD] = in_ref[g, a]
        copies.append(pltpu.make_async_copy(rows_s.at[a], ref, sem.at[a]))
        copies[a].start()
    for cp in copies:
        cp.wait()


def unpack(packed):
    return pl.pallas_call(
        unpack_kernel,
        in_specs=[VMEM],
        out_specs=(ANY,) * 4,
        out_shape=(jax.ShapeDtypeStruct((CHUNK, PLANE * HD), BF16),) * 4,
        scratch_shapes=[pltpu.VMEM((4, CHUNK, PLANE * HD), BF16), pltpu.SemaphoreType.DMA((4,))],
        compiler_params=room(6),
        name="unpack",
    )(near(packed))


def nt(a, b):
    return lax.dot_general(a, b, (((1,), (1,)), ((), ())), preferred_element_type=F32)


def nn(a, b):
    return lax.dot_general(a, b, (((1,), (0,)), ((), ())), preferred_element_type=F32)


def group_rows(x):
    return x.reshape(x.shape[0] // 8, 8, x.shape[1])


def marks(shape, dim, row):
    return (lax.broadcasted_iota(jnp.int32, shape, dim) == row).astype(F32)


SPANS = ((0, 2 * BLOCK), (0, 3 * BLOCK), (BLOCK, 2 * BLOCK))


def tokens(ref):
    return ref.reshape(ref.shape[0] * ref.shape[1], HD)


def keys(s, lo, n):
    return slice(s * FRAME + lo, s * FRAME + lo + n)


def block(r):
    return slice(r * BLOCK, (r + 1) * BLOCK)


def fetch(ref, index, a, dst):
    for h in range(CHUNKS):
        dst[h] = ref[index * CHUNKS + h, a]


def put(src, ref, index, a):
    for h in range(CHUNKS):
        ref[index * CHUNKS + h, a] = src[h]


def tile_bias(listed, frame, keyed):
    tiles = listed.shape[1]
    slot = lax.broadcasted_iota(jnp.int32, (HD, 1), 0)
    base = jnp.zeros_like(slot)
    for i, k in enumerate(keyed):
        base = jnp.where(slot // TILES_F == i, k, base)
    tile = base * TILES_F + slot % TILES_F
    tile = jnp.where(tile < 0, -TILES_F, tile)
    hit = jnp.zeros((HD, tiles), F32)
    for j in range(listed.shape[0]):
        hit = jnp.where(listed[j : j + 1, :] == tile, 1.0, hit)
    owner = lax.broadcasted_iota(jnp.int32, (tiles, FRAME), 1) // TILE + frame * TILES_F
    spread = (owner == lax.broadcasted_iota(jnp.int32, (tiles, FRAME), 0)).astype(F32).astype(BF16)
    return jnp.where(nn(hit.astype(BF16), spread) > 0.5, 0.0, MASKED).astype(BF16)


def set_hot(hot):
    lane = lax.broadcasted_iota(jnp.int32, (TILE, HD), 1)
    for t in range(3 * TILES_F):
        hot[t * TILE : (t + 1) * TILE, :] = (lane == t).astype(F32).astype(BF16)


class Scores:
    def __init__(self, slots, k, hot, vt, qt, s, p):
        self.slots, self.k, self.hot, self.vt, self.qt, self.s, self.p = slots, k, hot, vt, qt, s, p
        self.tops, self.sums = {}, {}
        vt[HD:, :] = marks((16, vt.shape[1]), 0, 0).astype(BF16)

    def score(self, r, i):
        lo, n = SPANS[r]
        kf = tokens(self.k)
        qt = self.qt[:, block(r)]
        for b in range(n // BLOCK):
            ks = keys(i, lo + b * BLOCK, BLOCK)
            hs = keys(self.slots[i], lo + b * BLOCK, BLOCK)
            st = nn(jnp.concatenate([kf[ks, :], self.hot[hs, :]], axis=1), qt)
            self.s[r, i * n + b * BLOCK : i * n + (b + 1) * BLOCK, :] = st
            got = jnp.max(group_rows(st), axis=0)
            self.tops[r] = jnp.maximum(self.tops[r], got) if r in self.tops else got
        if i == len(self.slots) - 1:
            self.tops[r] = jnp.max(self.tops[r], axis=0, keepdims=True) * (SCALE * LOG2E)

    def soften(self, r, i):
        lo, n = SPANS[r]
        for t in range(n // TILE):
            x = self.s[r, i * n + t * TILE : i * n + (t + 1) * TILE, :]
            e = jnp.exp2(x * (SCALE * LOG2E) - self.tops[r])
            self.p[i][lo + t * TILE : lo + (t + 1) * TILE, block(r)] = e.astype(BF16)
        got = nn(self.vt[:, keys(i, lo, n)], self.p[i][lo : lo + n, block(r)])
        self.sums[r] = self.sums[r] + got if r in self.sums else got


def settle(ot, r, ct, out_ref, *shares):
    cols = block(r)
    inv = 1.0 / ot[HD : HD + 1]
    out = (ot[:HD] * inv).astype(BF16)
    tokens(out_ref)[cols, :] = out.T
    for share, c2_ref in shares:
        factor = inv * SCALE if share is None else inv * SCALE * share
        c2 = (ct[:, cols].astype(F32) * factor).astype(BF16)
        c2_ref[:HD, cols] = c2
        dots = -jnp.sum(c2.astype(F32) * out.astype(F32), axis=0, keepdims=True)
        high = dots.astype(BF16).astype(F32)
        mid = (dots - high).astype(BF16).astype(F32)
        low = dots - high - mid
        shape = (HD, BLOCK)
        tail = marks(shape, 0, 0) * high + marks(shape, 0, 1) * mid + marks(shape, 0, 2) * low
        c2_ref[HD:, cols] = tail.astype(BF16)


class Grads:
    def __init__(self, v, kt, qt, c2, p, d):
        self.v, self.kt, self.qt, self.c2, self.p, self.d = v, kt, qt, c2, p, d
        self.sums = {}
        self.unit = (lax.broadcasted_iota(jnp.int32, (BLOCK, HD), 1) < 3).astype(F32).astype(BF16)

    def back(self, r, s):
        lo, n = SPANS[r]
        cols = block(r)
        vf = tokens(self.v)
        for b in range(n // BLOCK):
            at = slice(lo + b * BLOCK, lo + (b + 1) * BLOCK)
            rows = jnp.concatenate([vf[keys(s, lo + b * BLOCK, BLOCK), :], self.unit], axis=1)
            dp = nn(rows, self.c2[:, cols])
            self.d[s][at, cols] = self.p[s][at, cols] * dp.astype(BF16)
        got = nn(self.kt[:, keys(s, lo, n)], self.d[s][lo : lo + n, cols])
        self.sums[r] = self.sums[r] + got if r in self.sums else got

    def keyed(self, s, a):
        for b, (lo, n) in enumerate(SPANS):
            if a == 0:
                g = nt(self.qt[:HD, lo : lo + n], self.d[s][block(b), lo : lo + n])
            else:
                g = nt(self.c2[:HD, lo : lo + n], self.p[s][block(b), lo : lo + n]) * (1.0 / SCALE)
            yield block(b), g.astype(BF16).T


def early_kernel(
    mine_ref, swap_ref, near_ref,
    out_ref, p_ref, d_ref, qt_ref, c2_ref, ep_ref, eqt_ref, ect_ref, etop_ref, esum_ref,
    q_s, c_s, o_s, eq_s, ec_s, k_s, v_s, ek_s, ev_s, hot_s, kt_s, vt_s, evt_s, ct_s, s_s, es_s,
):
    core, first = lax.axis_index("co"), 4 * lax.axis_index("sx")
    partner = first + 1 - core
    local, outer = first + 2 - core, first + 3 * core
    frame = 1 - core
    fetch(mine_ref, frame, 0, q_s)
    for a, (dst, edst) in enumerate(((k_s, ek_s), (v_s, ev_s))):
        for h in range(CHUNKS):
            dst[h] = swap_ref[h, a]
            dst[CHUNKS + h] = mine_ref[frame * CHUNKS + h, 1 + a]
            dst[2 * CHUNKS + h] = swap_ref[CHUNKS + h, a]
            edst[h] = mine_ref[core * CHUNKS + h, 1 + a]
            edst[CHUNKS + h] = swap_ref[core * CHUNKS + h, a]
    fetch(mine_ref, frame, 3, c_s)
    fetch(mine_ref, core, 0, eq_s)
    fetch(mine_ref, core, 3, ec_s)
    set_hot(hot_s)
    listed = near_ref[...]
    qt_ref[:HD, :] = tokens(q_s)[...].T
    qt_ref[HD:, :] = tile_bias(listed, local, (partner, local, partner + 2))
    ps, ds = [p_ref.at[s] for s in range(3)], [d_ref.at[s] for s in range(3)]
    sc = Scores((0, 1, 2), k_s, hot_s, vt_s, qt_ref, s_s, ps)
    gr = Grads(v_s, kt_s, qt_ref, c2_ref, ps, ds)
    es = Scores((1, 2), ek_s, hot_s, evt_s, eqt_ref, es_s, [ep_ref.at[s] for s in range(2)])
    for s in range(3):
        sc.score(0, s)
    vt_s[:HD, :] = tokens(v_s)[...].T
    ct_s[...] = tokens(c_s)[...].T
    for s in range(3):
        sc.score(1, s)
        sc.soften(0, s)
    settle(sc.sums[0], 0, ct_s, o_s, (None, c2_ref))
    for s in range(3):
        sc.score(2, s)
        sc.soften(1, s)
    settle(sc.sums[1], 1, ct_s, o_s, (None, c2_ref))
    kt_s[...] = tokens(k_s)[...].T
    for s in range(3):
        gr.back(0, s)
        sc.soften(2, s)
    settle(sc.sums[2], 2, ct_s, o_s, (None, c2_ref))
    eqt_ref[:HD, :] = tokens(eq_s)[...].T
    eqt_ref[HD:, :] = tile_bias(listed, outer, (first - 1 + 5 * core, outer, partner + 2 * core))
    evt_s[:HD, :] = tokens(ev_s)[...].T
    ect_ref[...] = tokens(ec_s)[...].T
    for s in range(2):
        es.score(0, s)
    for s in range(2):
        es.score(1, s)
        es.soften(0, s)
        gr.back(1, s)
    gr.back(1, 2)
    for s in range(2):
        es.score(2, s)
        es.soften(1, s)
        gr.back(2, s)
    gr.back(2, 2)
    for s in range(2):
        es.soften(2, s)
    for r in range(3):
        tokens(q_s)[block(r), :] = gr.sums[r].astype(BF16).T
        etop_ref[:, block(r)] = jnp.broadcast_to(es.tops[r], (8, BLOCK))
        esum_ref[:, block(r)] = es.sums[r]
    put(o_s, out_ref, 0, 0)
    put(q_s, out_ref, 0, 1)


def outer_kernel(
    edge_ref, eqt_ref, ect_ref, etop_ref, esum_ref, out_ref, c2_ref, dqt_ref, gedge_ref,
    o_s, g_s, k_s, v_s, hot_s, kt_s, vt_s, c2_s, s_s, p_s, d_s,
):
    for a, dst in ((0, k_s), (1, v_s)):
        fetch(edge_ref, 0, a, dst)
    set_hot(hot_s)
    sc = Scores((0,), k_s, hot_s, vt_s, eqt_ref, s_s, [p_s])
    gr = Grads(v_s, kt_s, eqt_ref, c2_s, [p_s], [d_s])
    sc.score(0, 0)
    vt_s[:HD, :] = tokens(v_s)[...].T
    sc.score(1, 0)
    kt_s[...] = tokens(k_s)[...].T
    sc.score(2, 0)
    for r in range(3):
        sc.soften(r, 0)
    for r in range(3):
        old = etop_ref[0:1, block(r)]
        top = jnp.maximum(old, sc.tops[r])
        mine, edge = jnp.exp2(old - top), jnp.exp2(sc.tops[r] - top)
        total = esum_ref[:, block(r)] * mine + sc.sums[r] * edge
        settle(total, r, ect_ref, o_s, (edge, c2_s), (mine, c2_ref))
    for r in range(3):
        gr.back(r, 0)
    for r in range(3):
        dqt_ref[:, block(r)] = gr.sums[r]
    put(o_s, out_ref, 0, 0)
    for a in range(2):
        for rows, g in gr.keyed(0, a):
            tokens(g_s.at[a])[rows, :] = g
        put(g_s.at[a], gedge_ref, 0, a)


def late_kernel(
    mine_ref, swap_ref, ep_ref, eqt_ref, c2_ref, dqt_ref, lp_ref, ld_ref, lqt_ref, lc2_ref,
    dq_ref, lown_ref, gown_ref, gswap_ref, g_s, old_s, k_s, v_s, kt_s, d_s,
):
    core = lax.axis_index("co")
    for a, dst in ((0, k_s), (1, v_s)):
        for h in range(CHUNKS):
            dst[h] = mine_ref[core * CHUNKS + h, 1 + a]
            dst[CHUNKS + h] = swap_ref[core * CHUNKS + h, a]
    gr = Grads(v_s, kt_s, eqt_ref, c2_ref, [ep_ref.at[s] for s in range(2)], [d_s.at[s] for s in range(2)])
    done = Grads(None, None, lqt_ref, lc2_ref, [lp_ref.at[s] for s in range(3)], [ld_ref.at[s] for s in range(3)])
    kt_s[...] = tokens(k_s)[...].T
    for r in range(3):
        for s in range(2):
            gr.back(r, s)
    for r in range(3):
        tokens(g_s.at[0, 0])[block(r), :] = (gr.sums[r] + dqt_ref[:, block(r)]).astype(BF16).T
    for h in range(CHUNKS):
        dq_ref[h] = g_s[0, 0, h]
    for a in range(2):
        for i in range(2):
            for rows, g in done.keyed(2 * i, a):
                tokens(old_s.at[a, i])[rows, :] = g
        for rows, g in gr.keyed(1, a):
            tokens(g_s.at[a, 1])[rows, :] = g
        for h in range(CHUNKS):
            both = g_s[a, 1, h].astype(F32) + old_s[a, core, h].astype(F32)
            gswap_ref[core * CHUNKS + h, a] = both.astype(BF16)
            gswap_ref[(1 - core) * CHUNKS + h, a] = old_s[a, 1 - core, h]
    for a in range(2):
        for source, ref, s in ((gr, gown_ref, 0), (done, lown_ref, 1)):
            for rows, g in source.keyed(s, a):
                tokens(g_s.at[a, s])[rows, :] = g
            for h in range(CHUNKS):
                ref[h, a] = g_s[a, s, h]


PAIR = jax.ShapeDtypeStruct((PLANE, 2, CHUNK, HD), BF16)
HALF = jax.ShapeDtypeStruct((CHUNKS, 2, CHUNK, HD), BF16)
ONE = jax.ShapeDtypeStruct((CHUNKS, CHUNK, HD), BF16)


def frames(*shape):
    return pltpu.VMEM((*shape, CHUNK, HD), BF16)


def wide(rows):
    return pltpu.VMEM((rows, FRAME), BF16)


def held(*shape):
    return jax.ShapeDtypeStruct(shape, BF16)


def attend_early(mine, swap, neighbours):
    return pl.pallas_call(
        early_kernel,
        in_specs=[VMEM] * 3,
        out_specs=(VMEM,) * 10,
        out_shape=(
            HALF,
            held(3, FRAME, FRAME),
            held(3, FRAME, FRAME),
            held(2 * HD, FRAME),
            held(2 * HD, FRAME),
            held(2, FRAME, FRAME),
            held(2 * HD, FRAME),
            held(HD, FRAME),
            jax.ShapeDtypeStruct((8, FRAME), F32),
            jax.ShapeDtypeStruct((HD + 16, FRAME), F32),
        ),
        scratch_shapes=[frames(CHUNKS)] * 5
        + [frames(3 * CHUNKS)] * 2
        + [frames(2 * CHUNKS)] * 2
        + [
            pltpu.VMEM((KEYS, HD), BF16),
            pltpu.VMEM((HD, KEYS), BF16),
            pltpu.VMEM((HD + 16, KEYS), BF16),
            pltpu.VMEM((HD + 16, 2 * FRAME), BF16),
            wide(HD),
            pltpu.VMEM((3, 9 * BLOCK, BLOCK), F32),
            pltpu.VMEM((3, 6 * BLOCK, BLOCK), F32),
        ],
        compiler_params=room(34),
        name="attend_early",
    )(near(mine), near(swap), neighbours.T)


def attend_outer(edge, *kept):
    return pl.pallas_call(
        outer_kernel,
        in_specs=[VMEM] * 5,
        out_specs=(VMEM,) * 4,
        out_shape=(
            held(CHUNKS, 1, CHUNK, HD),
            held(2 * HD, FRAME),
            jax.ShapeDtypeStruct((HD, FRAME), F32),
            HALF,
        ),
        scratch_shapes=[
            frames(CHUNKS),
            frames(2, CHUNKS),
            frames(CHUNKS),
            frames(CHUNKS),
            pltpu.VMEM((KEYS, HD), BF16),
            wide(HD),
            wide(HD + 16),
            wide(2 * HD),
            pltpu.VMEM((3, 3 * BLOCK, BLOCK), F32),
            wide(FRAME),
            wide(FRAME),
        ],
        compiler_params=room(16),
        name="attend_outer",
    )(near(edge), *kept)


def attend_late(mine, swap, *kept):
    return pl.pallas_call(
        late_kernel,
        in_specs=[VMEM] * 10,
        out_specs=(VMEM,) * 4,
        out_shape=(ONE, HALF, HALF, PAIR),
        scratch_shapes=[
            frames(2, 2, CHUNKS),
            frames(2, 2, CHUNKS),
            frames(2 * CHUNKS),
            frames(2 * CHUNKS),
            pltpu.VMEM((HD, 2 * FRAME), BF16),
            pltpu.VMEM((2, FRAME, FRAME), BF16),
        ],
        compiler_params=room(14),
        name="attend_late",
    )(near(mine), near(swap), *kept)


def join_kernel(local_ref, outer_ref, dq_ref, lown_ref, eown_ref, swap_ref, edge_ref, out_ref):
    core = lax.axis_index("co")
    for h in range(CHUNKS):
        here, there = core * CHUNKS + h, (1 - core) * CHUNKS + h
        out_ref[there, 0] = local_ref[h, 0]
        out_ref[there, 1] = local_ref[h, 1]
        out_ref[here, 0] = outer_ref[h, 0]
        out_ref[here, 1] = dq_ref[h]
        for a in range(2):
            x = lown_ref[h, a].astype(F32) + swap_ref[there, a].astype(F32)
            out_ref[there, 2 + a] = x.astype(BF16)
            x = eown_ref[h, a].astype(F32) + swap_ref[here, a].astype(F32)
            out_ref[here, 2 + a] = (x + edge_ref[h, a].astype(F32)).astype(BF16)


def join(*parts):
    swap, edge = parts[-2:]
    return pl.pallas_call(
        join_kernel,
        in_specs=[VMEM] * 7,
        out_specs=VMEM,
        out_shape=jax.ShapeDtypeStruct((PLANE, 4, CHUNK, HD), BF16),
        compiler_params=room(10),
        name="join",
    )(*parts[:-2], near(swap), near(edge))


def shards(queries, keys, values, cotangent, neighbours):
    plane = ("yl", "head")
    ring = lax.axis_size("sx")
    across = []
    for i in range(ring - 1):
        across.append((2 * i + 1, 2 * i + 2))
        across.append((2 * i + 2, 2 * i + 1))
    swap_pairs = [(0, 1), (1, 0)]
    core = lax.axis_index("co")
    sent = enter(queries, keys, values, cotangent)
    mine = lax.all_to_all(sent, plane, split_axis=0, concat_axis=0, tiled=True)
    kv = mine[:, 1:3]
    swap = lax.ppermute(kv, "co", swap_pairs)
    kv_edge = lax.dynamic_slice_in_dim(kv, core * CHUNKS, CHUNKS, 0)
    edge = lax.ppermute(kv_edge, ("sx", "co"), across)
    local, lp, ld, lqt, lc2, ep, eqt, *kept = attend_early(mine, swap, neighbours)
    outer, c2, dqt, gedge = attend_outer(edge, eqt, *kept)
    gedge_in = lax.ppermute(gedge, ("sx", "co"), across)
    dq, lown, eown, gswap = attend_late(mine, swap, ep, eqt, c2, dqt, lp, ld, lqt, lc2)
    gswap_in = lax.ppermute(gswap, "co", swap_pairs)
    packed = join(local, outer, dq, lown, eown, gswap_in, gedge_in)
    return unpack(lax.all_to_all(packed, plane, split_axis=0, concat_axis=0, tiled=True))


def solution(mesh):
    view = Mesh(mesh.devices.reshape(mesh.devices.shape[0] // 4, 2, 2, -1), ("sx", "yl", "co", "head"))
    rows = P(("sx", "yl", "co", "head"), None)
    return jax.shard_map(
        shards,
        mesh=view,
        in_specs=(rows,) * 4 + (P(),),
        out_specs=(rows,) * 4,
        check_vma=False,
    )
```

time: 86.3 us -> 85.4 us (0.990)
  transfers between devices with their start and end apart: 4 -> 4, of which waited for: 2 -> 2; matrix products, arithmetic and copies ran while one was open for 0% -> 0% of each run, Pallas kernels for 6% -> 7%
where the time goes in v5:
time: 85.4 us; the launch traced here: 85.1 us
  blocking collectives  56.4 us (66%)
  Pallas kernels  15.1 us (18%)
  waiting for transfers between devices  7.64 us (9%)
  starting transfers between devices  5.22 us (6%)
    all_to_all x1, blocking collectives, shards(): mine = lax.all_to_all(sent, plane, split_axis=0, concat_axis=0, tiled=True)  30.2 us
    all_to_all x1, blocking collectives, shards(): lax.all_to_all(packed, plane, split_axis=0, concat_axis=0, tiled=True)  26.2 us
    ppermute x1, waiting for transfers between devices, shards(): gedge_in = lax.ppermute(gedge, ('sx', 'co'), across)  7.01 us
    pallas_call x1, Pallas kernels, attend_early(): pl.pallas_call(early_kernel, in_specs=[VMEM] * 3, out_specs=(VMEM,) * 10,...  5.91 us
    pallas_call x1, Pallas kernels, attend_late(): pl.pallas_call(late_kernel, in_specs=[VMEM] * 10, out_specs=(VMEM,) * 4,...  3.96 us
    ppermute x1, starting transfers between devices, shards(): edge = lax.ppermute(kv_edge, ('sx', 'co'), across)  2.53 us
    pallas_call x1, Pallas kernels, attend_outer(): pl.pallas_call(outer_kernel, in_specs=[VMEM] * 5, out_specs=(VMEM,) * 4,...  2.23 us
    ppermute x1, starting transfers between devices, shards(): gedge_in = lax.ppermute(gedge, ('sx', 'co'), across)  2.06 us
  transfers between devices with their start and end apart: 4, of which 2 were waited for; matrix products, arithmetic and copies ran while one was open for 0% of the time, Pallas kernels for 7%

profile of v5, /device:TPU:2, one launch (start us, length us, event | category | flops | bytes accessed | tf_op | source)
XLA Modules:
  0.0 85.1 jit_solution(2560198098380634584)
XLA Ops:
  0.6 1.5 %enter.1 = bf16[16,4,96,128]{3,2,1,0:T(8,128)(2,1)S(1)} custom-call(bf16[96,2048]{1,0:T(8,128)(2,1)} %q_ref.1, bf16[96,2048]{1,0:T(8,128)(2,1)} %k_ref.1, bf16[96,2048]{1,0:T(8,128)(2,1)} %v_ref.1, bf16[96,2048]{1,0:T(8,128)(2,1)} %c_ref.1), custom_call_target="tpu_custom_call" | custom-call | tf_op jit(solution)/shard_map/enter/pallas_call | solution.py:53
  2.1 30.2 %all_to_all.10.mine_ref = bf16[16,4,96,128]{3,2,1,0:T(8,128)(2,1)S(1)} all-to-all(bf16[16,4,96,128]{3,2,1,0:T(8,128)(2,1)S(1)} %enter.1), channel_id=1, replica_groups=mesh['sx'=4,'yl'=2,'co'=2,'head'=8] {'yl','head'}, dimensions={0} | all-to-all | bytes 3145728 | tf_op jit(solution)/shard_map/all_to_all | solution.py:503
  32.3 0.0 copy-start
  32.3 0.1 slice.4
  32.3 0.1 collective-permute-start
  32.5 2.5 %collective-permute-start.1 = (bf16[8,2,96,128]{3,2,1,0:T(8,128)(2,1)S(1)}, bf16[8,2,96,128]{3,2,1,0:T(8,128)(2,1)S(1)}, u32[]{:S(2)}, u32[]{:S(2)}) collective-permute-start(bf16[8,2,96,128]{3,2,1,0:T(8,128)(2,1)S(1)} %constant_dynamic-slice_fusion), channel_id=1, source_target_pairs={{8,32},{32,8},{40,64},{64,40},{72,96},{96,72},{9,33},{33,9},{41,65... | collective-permute-start | bytes 1179656 | tf_op jit(solution)/shard_map/ppermute | solution.py:507
  35.0 0.0 collective-permute-done.swap_ref
  35.0 0.0 copy-done
  35.0 5.9 %attend_early.1 = (bf16[8,2,96,128]{3,2,1,0:T(8,128)(2,1)S(1)}, bf16[3,768,768]{2,1,0:T(8,128)(2,1)S(1)}, bf16[3,768,768]{2,1,0:T(8,128)(2,1)S(1)}, bf16[256,768...) custom-call(bf16[16,4,96,128]{3,2,1,0:T(8,128)(2,1)S(1)} %all_to_all, ...), custom_call_target="tpu_custom_call" | custom-call | tf_op jit(solution)/shard_map/attend_early/pallas_call | solution.py:385
  40.9 0.6 collective-permute-done.1.edge_ref
  41.6 2.2 %attend_outer.1 = (bf16[8,1,96,128]{3,2,1,0:T(8,128)(2,1)S(1)}, bf16[256,768]{1,0:T(8,128)(2,1)S(1)}, f32[128,768]{1,0:T(8,128)S(1)}, bf16[8,2,96,128]{3,2,1,0:T(8,128)(2,1)S(1)}) custom-call(bf16[8,2,96,128]{3,2,1,0:T(8,128)(2,1)S(1)} %collective-permute-done.1.edge_ref, bf16[256,768]{1,0:T(8,128)(2,1)S(1)} %get-tuple-element.23.eqt_ref, ...), custom_call_target="tpu_custom_call" | custom-call | tf_op jit(solution)/shard_map/attend_outer/pallas_call | solution.py:419
  43.8 4.0 %attend_late.1 = (bf16[8,96,128]{2,1,0:T(8,128)(2,1)S(1)}, bf16[8,2,96,128]{3,2,1,0:T(8,128)(2,1)S(1)}, bf16[8,2,96,128]{3,2,1,0:T(8,128)(2,1)S(1)}, bf16[16,2,96,128]{3,2,1,0:T(8,128)(2,1)S(1)}) custom-call(bf16[16,4,96,128]{3,2,1,0:T(8,128)(2,1)S(1)} %all_to_all.10.mine_ref, bf16[16,2,96,128]{3,2,1,0:T(8,128)(2,1)S(1)} %collective-permute-done.swap_ref, ...), custom_call_target="tpu_custom_call" | custom-call | tf_op jit(solution)/shard_map/attend_late/pallas_call | solution.py:448
  47.8 0.5 collective-permute-start.2
  48.3 2.1 %collective-permute-start.3 = (bf16[8,2,96,128]{3,2,1,0:T(8,128)(2,1)S(1)}, bf16[8,2,96,128]{3,2,1,0:T(8,128)(2,1)S(1)}, u32[]{:S(2)}, u32[]{:S(2)}) collective-permute-start(bf16[8,2,96,128]{3,2,1,0:T(8,128)(2,1)S(1)} %get-tuple-element.39), channel_id=1, source_target_pairs={{8,32},{32,8},{40,64},{64,40},{72,96},{96,72},{9,33},{33,9},{41,65... | collective-permute-start | bytes 1179656 | tf_op jit(solution)/shard_map/ppermute | solution.py:510
  50.4 7.0 %collective-permute-done.3.edge_ref = bf16[8,2,96,128]{3,2,1,0:T(8,128)(2,1)S(1)} collective-permute-done((bf16[8,2,96,128]{3,2,1,0:T(8,128)(2,1)S(1)}, bf16[8,2,96,128]{3,2,1,0:T(8,128)(2,1)S(1)}, u32[]{:S(2)}, u32[]{:S(2)}) %collective-permute-start.3) | collective-permute-done | bytes 393248 | tf_op jit(solution)/shard_map/ppermute | solution.py:510
  57.4 0.0 collective-permute-done.2.swap_ref
  57.4 0.3 join.1
  57.7 26.2 %all_to_all.11.in_ref = bf16[16,4,96,128]{3,2,1,0:T(8,128)(2,1)S(1)} all-to-all(bf16[16,4,96,128]{3,2,1,0:T(8,128)(2,1)S(1)} %join.1), channel_id=1, replica_groups=mesh['sx'=4,'yl'=2,'co'=2,'head'=8] {'yl','head'}, dimensions={0} | all-to-all | bytes 3145728 | tf_op jit(solution)/shard_map/all_to_all | solution.py:514
  83.9 1.3 %unpack.1 = (bf16[96,2048]{1,0:T(8,128)(2,1)}, bf16[96,2048]{1,0:T(8,128)(2,1)}, bf16[96,2048]{1,0:T(8,128)(2,1)}, bf16[96,2048]{1,0:T(8,128)(2,1)}) custom-call(bf16[16,4,96,128]{3,2,1,0:T(8,128)(2,1)S(1)} %all_to_all.11.in_ref), custom_call_target="tpu_custom_call" | custom-call | tf_op jit(solution)/shard_map/unpack/pallas_call | solution.py:77
  (1 shorter events, 0.0 us)
Async XLA Ops:
  32.3 2.8 %copy-start = (s32[192,27]{0,1:T(8,128)S(1)}, s32[192,27]{0,1:T(8,128)}, u32[]{:S(2)}) copy-start(s32[192,27]{0,1:T(8,128)} %param.9) | copy-start | bytes 62212
  32.3 2.7 %collective-permute-start = (bf16[16,2,96,128]{3,2,1,0:T(8,128)(2,1)S(1)}, bf16[16,2,96,128]{3,2,1,0:T(8,128)(2,1)S(1)}, u32[]{:S(2)}, u32[]{:S(2)}) collective-permute-start(bf16[16,2,96,128]{3,2,1,0:T(8,128)(2,1)S(1)} %slice.4), channel_id=1, source_target_pairs={{0,8},{8,0},{1,9},{9,1},{2,10},{10,2},{3,11},{11,3},{4,12},{12,4},... | collective-permute-start | bytes 2359304 | tf_op jit(solution)/shard_map/ppermute | solution.py:505
  32.5 9.1 %collective-permute-start.1 = (bf16[8,2,96,128]{3,2,1,0:T(8,128)(2,1)S(1)}, bf16[8,2,96,128]{3,2,1,0:T(8,128)(2,1)S(1)}, u32[]{:S(2)}, u32[]{:S(2)}) collective-permute-start(bf16[8,2,96,128]{3,2,1,0:T(8,128)(2,1)S(1)} %constant_dynamic-slice_fusion), channel_id=1, source_target_pairs={{8,32},{32,8},{40,64},{64,40},{72,96},{96,72},{9,33},{33,9},{41,65... | collective-permute-start | bytes 1179656 | tf_op jit(solution)/shard_map/ppermute | solution.py:507
  47.8 9.6 %collective-permute-start.2 = (bf16[16,2,96,128]{3,2,1,0:T(8,128)(2,1)S(1)}, bf16[16,2,96,128]{3,2,1,0:T(8,128)(2,1)S(1)}, u32[]{:S(2)}, u32[]{:S(2)}) collective-permute-start(bf16[16,2,96,128]{3,2,1,0:T(8,128)(2,1)S(1)} %get-tuple-element.38), channel_id=1, source_target_pairs={{0,8},{8,0},{1,9},{9,1},{2,10},{10,2},{3,11},{11,3},{4,12},{12,4},... | collective-permute-start | bytes 2359304 | tf_op jit(solution)/shard_map/ppermute | solution.py:512
  48.3 9.1 %collective-permute-start.3 = (bf16[8,2,96,128]{3,2,1,0:T(8,128)(2,1)S(1)}, bf16[8,2,96,128]{3,2,1,0:T(8,128)(2,1)S(1)}, u32[]{:S(2)}, u32[]{:S(2)}) collective-permute-start(bf16[8,2,96,128]{3,2,1,0:T(8,128)(2,1)S(1)} %get-tuple-element.39), channel_id=1, source_target_pairs={{8,32},{32,8},{40,64},{64,40},{72,96},{96,72},{9,33},{33,9},{41,65... | collective-permute-start | bytes 1179656 | tf_op jit(solution)/shard_map/ppermute | solution.py:510

commit v6 on v5

--- a/solution.py
+++ b/solution.py
@@ -18,6 +18,7 @@
 CHUNK = FRAME // CHUNKS
 PLANE = 16
 MASKED = -1e30
+USED = 48
 SCALE = 1.0 / math.sqrt(HD)
 LOG2E = 1.4426950408889634
 ANY = pl.BlockSpec(memory_space=pl.ANY)
@@ -128,13 +129,13 @@
 
 def tile_bias(listed, frame, keyed):
     tiles = listed.shape[1]
-    slot = lax.broadcasted_iota(jnp.int32, (HD, 1), 0)
+    slot = lax.broadcasted_iota(jnp.int32, (USED, 1), 0)
     base = jnp.zeros_like(slot)
     for i, k in enumerate(keyed):
         base = jnp.where(slot // TILES_F == i, k, base)
     tile = base * TILES_F + slot % TILES_F
     tile = jnp.where(tile < 0, -TILES_F, tile)
-    hit = jnp.zeros((HD, tiles), F32)
+    hit = jnp.zeros((USED, tiles), F32)
     for j in range(listed.shape[0]):
         hit = jnp.where(listed[j : j + 1, :] == tile, 1.0, hit)
     owner = lax.broadcasted_iota(jnp.int32, (tiles, FRAME), 1) // TILE + frame * TILES_F
@@ -142,10 +143,17 @@
     return jnp.where(nn(hit.astype(BF16), spread) > 0.5, 0.0, MASKED).astype(BF16)
 
 
-def set_hot(hot):
+def set_hot(hot, slots):
     lane = lax.broadcasted_iota(jnp.int32, (TILE, HD), 1)
-    for t in range(3 * TILES_F):
+    for t in range(slots * TILES_F):
         hot[t * TILE : (t + 1) * TILE, :] = (lane == t).astype(F32).astype(BF16)
+
+
+def over_keys(wide_ref, parts, r):
+    lo, n = SPANS[r]
+    left = [wide_ref[:, keys(i, lo, n)] for i in range(len(parts))]
+    right = [part[lo : lo + n, block(r)] for part in parts]
+    return nn(jnp.concatenate(left, axis=1), jnp.concatenate(right, axis=0))
 
 
 class Scores:
@@ -163,10 +171,11 @@
             hs = keys(self.slots[i], lo + b * BLOCK, BLOCK)
             st = nn(jnp.concatenate([kf[ks, :], self.hot[hs, :]], axis=1), qt)
             self.s[r, i * n + b * BLOCK : i * n + (b + 1) * BLOCK, :] = st
-            got = jnp.max(group_rows(st), axis=0)
-            self.tops[r] = jnp.maximum(self.tops[r], got) if r in self.tops else got
         if i == len(self.slots) - 1:
-            self.tops[r] = jnp.max(self.tops[r], axis=0, keepdims=True) * (SCALE * LOG2E)
+            top = jnp.full((8, BLOCK), 2 * MASKED, F32)
+            for t in range(len(self.slots) * n // TILE):
+                top = jnp.maximum(top, jnp.max(group_rows(self.s[r, t * TILE : (t + 1) * TILE, :]), axis=0))
+            self.tops[r] = jnp.max(top, axis=0, keepdims=True) * (SCALE * LOG2E)
 
     def soften(self, r, i):
         lo, n = SPANS[r]
@@ -174,45 +183,46 @@
             x = self.s[r, i * n + t * TILE : i * n + (t + 1) * TILE, :]
             e = jnp.exp2(x * (SCALE * LOG2E) - self.tops[r])
             self.p[i][lo + t * TILE : lo + (t + 1) * TILE, block(r)] = e.astype(BF16)
-        got = nn(self.vt[:, keys(i, lo, n)], self.p[i][lo : lo + n, block(r)])
-        self.sums[r] = self.sums[r] + got if r in self.sums else got
-
-
-def settle(ot, r, ct, out_ref, *shares):
-    cols = block(r)
+        if i == len(self.slots) - 1:
+            self.sums[r] = over_keys(self.vt, self.p, r)
+
+
+def weigh(cols, ct, factor, out, c2_ref):
+    c2 = (ct[:, cols].astype(F32) * factor).astype(BF16)
+    c2_ref[:HD, cols] = c2
+    dots = -jnp.sum(c2.astype(F32) * out.astype(F32), axis=0, keepdims=True)
+    high = dots.astype(BF16).astype(F32)
+    mid = (dots - high).astype(BF16).astype(F32)
+    low = dots - high - mid
+    shape = (HD, BLOCK)
+    tail = marks(shape, 0, 0) * high + marks(shape, 0, 1) * mid + marks(shape, 0, 2) * low
+    c2_ref[HD:, cols] = tail.astype(BF16)
+
+
+def settle(ot, r, ct, out_ref, c2_ref):
     inv = 1.0 / ot[HD : HD + 1]
     out = (ot[:HD] * inv).astype(BF16)
-    tokens(out_ref)[cols, :] = out.T
-    for share, c2_ref in shares:
-        factor = inv * SCALE if share is None else inv * SCALE * share
-        c2 = (ct[:, cols].astype(F32) * factor).astype(BF16)
-        c2_ref[:HD, cols] = c2
-        dots = -jnp.sum(c2.astype(F32) * out.astype(F32), axis=0, keepdims=True)
-        high = dots.astype(BF16).astype(F32)
-        mid = (dots - high).astype(BF16).astype(F32)
-        low = dots - high - mid
-        shape = (HD, BLOCK)
-        tail = marks(shape, 0, 0) * high + marks(shape, 0, 1) * mid + marks(shape, 0, 2) * low
-        c2_ref[HD:, cols] = tail.astype(BF16)
+    tokens(out_ref)[block(r), :] = out.T
+    weigh(block(r), ct, inv * SCALE, out, c2_ref)
 
 
 class Grads:
     def __init__(self, v, kt, qt, c2, p, d):
         self.v, self.kt, self.qt, self.c2, self.p, self.d = v, kt, qt, c2, p, d
-        self.sums = {}
         self.unit = (lax.broadcasted_iota(jnp.int32, (BLOCK, HD), 1) < 3).astype(F32).astype(BF16)
 
-    def back(self, r, s):
+    def back(self, r, s, held=None):
         lo, n = SPANS[r]
         cols = block(r)
         vf = tokens(self.v)
         for b in range(n // BLOCK):
             at = slice(lo + b * BLOCK, lo + (b + 1) * BLOCK)
-            rows = jnp.concatenate([vf[keys(s, lo + b * BLOCK, BLOCK), :], self.unit], axis=1)
-            dp = nn(rows, self.c2[:, cols])
+            value = vf[keys(s if held is None else held, lo + b * BLOCK, BLOCK), :]
+            dp = nn(jnp.concatenate([value, self.unit], axis=1), self.c2[:, cols])
             self.d[s][at, cols] = self.p[s][at, cols] * dp.astype(BF16)
-        got = nn(self.kt[:, keys(s, lo, n)], self.d[s][lo : lo + n, cols])
-        self.sums[r] = self.sums[r] + got if r in self.sums else got
+
+    def query(self, r):
+        return over_keys(self.kt, self.d, r)
 
     def keyed(self, s, a):
         for b, (lo, n) in enumerate(SPANS):
@@ -226,7 +236,7 @@
 def early_kernel(
     mine_ref, swap_ref, near_ref,
     out_ref, p_ref, d_ref, qt_ref, c2_ref, ep_ref, eqt_ref, ect_ref, etop_ref, esum_ref,
-    q_s, c_s, o_s, eq_s, ec_s, k_s, v_s, ek_s, ev_s, hot_s, kt_s, vt_s, evt_s, ct_s, s_s, es_s,
+    q_s, c_s, o_s, eq_s, ec_s, k_s, v_s, ek_s, ev_s, hot_s, vt_s, evt_s, ct_s, s_s, es_s,
 ):
     core, first = lax.axis_index("co"), 4 * lax.axis_index("sx")
     partner = first + 1 - core
@@ -243,13 +253,14 @@
     fetch(mine_ref, frame, 3, c_s)
     fetch(mine_ref, core, 0, eq_s)
     fetch(mine_ref, core, 3, ec_s)
-    set_hot(hot_s)
+    set_hot(hot_s, 3)
     listed = near_ref[...]
     qt_ref[:HD, :] = tokens(q_s)[...].T
-    qt_ref[HD:, :] = tile_bias(listed, local, (partner, local, partner + 2))
-    ps, ds = [p_ref.at[s] for s in range(3)], [d_ref.at[s] for s in range(3)]
+    qt_ref[HD + USED :, :] = jnp.zeros((HD - USED, FRAME), BF16)
+    qt_ref[HD : HD + USED, :] = tile_bias(listed, local, (partner, local, partner + 2))
+    ps = [p_ref.at[s] for s in range(3)]
     sc = Scores((0, 1, 2), k_s, hot_s, vt_s, qt_ref, s_s, ps)
-    gr = Grads(v_s, kt_s, qt_ref, c2_ref, ps, ds)
+    gr = Grads(v_s, None, qt_ref, c2_ref, ps, [d_ref.at[0], None, d_ref.at[1]])
     es = Scores((1, 2), ek_s, hot_s, evt_s, eqt_ref, es_s, [ep_ref.at[s] for s in range(2)])
     for s in range(3):
         sc.score(0, s)
@@ -258,18 +269,19 @@
     for s in range(3):
         sc.score(1, s)
         sc.soften(0, s)
-    settle(sc.sums[0], 0, ct_s, o_s, (None, c2_ref))
+    settle(sc.sums[0], 0, ct_s, o_s, c2_ref)
     for s in range(3):
         sc.score(2, s)
         sc.soften(1, s)
-    settle(sc.sums[1], 1, ct_s, o_s, (None, c2_ref))
-    kt_s[...] = tokens(k_s)[...].T
+    settle(sc.sums[1], 1, ct_s, o_s, c2_ref)
     for s in range(3):
-        gr.back(0, s)
         sc.soften(2, s)
-    settle(sc.sums[2], 2, ct_s, o_s, (None, c2_ref))
+        if s != 1:
+            gr.back(0, s)
+    settle(sc.sums[2], 2, ct_s, o_s, c2_ref)
     eqt_ref[:HD, :] = tokens(eq_s)[...].T
-    eqt_ref[HD:, :] = tile_bias(listed, outer, (first - 1 + 5 * core, outer, partner + 2 * core))
+    eqt_ref[HD + USED :, :] = jnp.zeros((HD - USED, FRAME), BF16)
+    eqt_ref[HD : HD + USED, :] = tile_bias(listed, outer, (first - 1 + 5 * core, outer, partner + 2 * core))
     evt_s[:HD, :] = tokens(ev_s)[...].T
     ect_ref[...] = tokens(ec_s)[...].T
     for s in range(2):
@@ -277,91 +289,113 @@
     for s in range(2):
         es.score(1, s)
         es.soften(0, s)
-        gr.back(1, s)
-    gr.back(1, 2)
+        gr.back(1, 2 * s)
     for s in range(2):
         es.score(2, s)
         es.soften(1, s)
-        gr.back(2, s)
-    gr.back(2, 2)
+        gr.back(2, 2 * s)
     for s in range(2):
         es.soften(2, s)
     for r in range(3):
-        tokens(q_s)[block(r), :] = gr.sums[r].astype(BF16).T
         etop_ref[:, block(r)] = jnp.broadcast_to(es.tops[r], (8, BLOCK))
         esum_ref[:, block(r)] = es.sums[r]
     put(o_s, out_ref, 0, 0)
-    put(q_s, out_ref, 0, 1)
 
 
 def outer_kernel(
-    edge_ref, eqt_ref, ect_ref, etop_ref, esum_ref, out_ref, c2_ref, dqt_ref, gedge_ref,
-    o_s, g_s, k_s, v_s, hot_s, kt_s, vt_s, c2_s, s_s, p_s, d_s,
+    edge_ref, eqt_ref, ect_ref, etop_ref, esum_ref, outt_ref, factor_ref, d_ref, gedge_ref,
+    g_s, k_s, v_s, hot_s, vt_s, c2_s, s_s, p_s,
 ):
     for a, dst in ((0, k_s), (1, v_s)):
         fetch(edge_ref, 0, a, dst)
-    set_hot(hot_s)
+    set_hot(hot_s, 1)
     sc = Scores((0,), k_s, hot_s, vt_s, eqt_ref, s_s, [p_s])
-    gr = Grads(v_s, kt_s, eqt_ref, c2_s, [p_s], [d_s])
+    gr = Grads(v_s, None, eqt_ref, c2_s, [p_s], [d_ref])
     sc.score(0, 0)
     vt_s[:HD, :] = tokens(v_s)[...].T
     sc.score(1, 0)
-    kt_s[...] = tokens(k_s)[...].T
     sc.score(2, 0)
     for r in range(3):
         sc.soften(r, 0)
     for r in range(3):
-        old = etop_ref[0:1, block(r)]
+        cols = block(r)
+        old = etop_ref[0:1, cols]
         top = jnp.maximum(old, sc.tops[r])
         mine, edge = jnp.exp2(old - top), jnp.exp2(sc.tops[r] - top)
-        total = esum_ref[:, block(r)] * mine + sc.sums[r] * edge
-        settle(total, r, ect_ref, o_s, (edge, c2_s), (mine, c2_ref))
+        total = esum_ref[:, cols] * mine + sc.sums[r] * edge
+        inv = 1.0 / total[HD : HD + 1]
+        out = (total[:HD] * inv).astype(BF16)
+        outt_ref[:, cols] = out
+        factor_ref[:, cols] = jnp.broadcast_to(inv * SCALE * mine, (8, BLOCK))
+        weigh(cols, ect_ref, inv * SCALE * edge, out, c2_s)
     for r in range(3):
         gr.back(r, 0)
-    for r in range(3):
-        dqt_ref[:, block(r)] = gr.sums[r]
-    put(o_s, out_ref, 0, 0)
-    for a in range(2):
+    for a in (1, 0):
         for rows, g in gr.keyed(0, a):
             tokens(g_s.at[a])[rows, :] = g
         put(g_s.at[a], gedge_ref, 0, a)
 
 
-def late_kernel(
-    mine_ref, swap_ref, ep_ref, eqt_ref, c2_ref, dqt_ref, lp_ref, ld_ref, lqt_ref, lc2_ref,
-    dq_ref, lown_ref, gown_ref, gswap_ref, g_s, old_s, k_s, v_s, kt_s, d_s,
+def share_kernel(
+    swap_ref, ep_ref, eqt_ref, ect_ref, outt_ref, factor_ref, lp_ref, ld_ref, lqt_ref, lc2_ref,
+    d_ref, gswap_ref, c2_ref, out_ref, g_s, old_s, v_s,
 ):
     core = lax.axis_index("co")
-    for a, dst in ((0, k_s), (1, v_s)):
+    for r in range(3):
+        weigh(block(r), ect_ref, factor_ref[0:1, block(r)], outt_ref[:, block(r)], c2_ref)
+        tokens(g_s.at[0])[block(r), :] = outt_ref[:, block(r)].T
+    put(g_s.at[0], out_ref, 0, 0)
+    fetch(swap_ref, core, 1, v_s)
+    gr = Grads(v_s, None, eqt_ref, c2_ref, [ep_ref.at[1]], [d_ref])
+    done = Grads(None, None, lqt_ref, lc2_ref, [lp_ref.at[0], lp_ref.at[2]], [ld_ref.at[0], ld_ref.at[1]])
+    for r in range(3):
+        gr.back(r, 0)
+    for a in (1, 0):
+        for i in range(2):
+            for rows, g in done.keyed(i, a):
+                tokens(old_s.at[a, i])[rows, :] = g
+        for rows, g in gr.keyed(0, a):
+            tokens(g_s.at[a])[rows, :] = g
         for h in range(CHUNKS):
-            dst[h] = mine_ref[core * CHUNKS + h, 1 + a]
-            dst[CHUNKS + h] = swap_ref[core * CHUNKS + h, a]
-    gr = Grads(v_s, kt_s, eqt_ref, c2_ref, [ep_ref.at[s] for s in range(2)], [d_s.at[s] for s in range(2)])
-    done = Grads(None, None, lqt_ref, lc2_ref, [lp_ref.at[s] for s in range(3)], [ld_ref.at[s] for s in range(3)])
-    kt_s[...] = tokens(k_s)[...].T
-    for r in range(3):
-        for s in range(2):
-            gr.back(r, s)
-    for r in range(3):
-        tokens(g_s.at[0, 0])[block(r), :] = (gr.sums[r] + dqt_ref[:, block(r)]).astype(BF16).T
-    for h in range(CHUNKS):
-        dq_ref[h] = g_s[0, 0, h]
-    for a in range(2):
-        for i in range(2):
-            for rows, g in done.keyed(2 * i, a):
-                tokens(old_s.at[a, i])[rows, :] = g
-        for rows, g in gr.keyed(1, a):
-            tokens(g_s.at[a, 1])[rows, :] = g
-        for h in range(CHUNKS):
-            both = g_s[a, 1, h].astype(F32) + old_s[a, core, h].astype(F32)
+            both = g_s[a, h].astype(F32) + old_s[a, core, h].astype(F32)
             gswap_ref[core * CHUNKS + h, a] = both.astype(BF16)
             gswap_ref[(1 - core) * CHUNKS + h, a] = old_s[a, 1 - core, h]
+
+
+def late_kernel(
+    mine_ref, swap_ref, edge_ref, ep_ref, eqt_ref, c2_ref, d0_ref, ed_ref, lp_ref, ld_ref, lqt_ref, lc2_ref,
+    edq_ref, ldq_ref, eown_ref, lown_ref, g_s, k_s, v_s, lk_s, lv_s, kt_s, lkt_s, d_s, ld_s,
+):
+    core = lax.axis_index("co")
+    frame = 1 - core
+    for h in range(CHUNKS):
+        v_s[h] = mine_ref[core * CHUNKS + h, 2]
+        k_s[h] = edge_ref[h, 0]
+        k_s[CHUNKS + h] = mine_ref[core * CHUNKS + h, 1]
+        k_s[2 * CHUNKS + h] = swap_ref[core * CHUNKS + h, 0]
+        lv_s[h] = mine_ref[frame * CHUNKS + h, 2]
+        lk_s[h] = swap_ref[h, 0]
+        lk_s[CHUNKS + h] = mine_ref[frame * CHUNKS + h, 1]
+        lk_s[2 * CHUNKS + h] = swap_ref[CHUNKS + h, 0]
+    gr = Grads(v_s, kt_s, eqt_ref, c2_ref, [None, ep_ref.at[0], None], [d0_ref, d_s, ed_ref])
+    done = Grads(lv_s, lkt_s, lqt_ref, lc2_ref, [None, lp_ref.at[1], None], [ld_ref.at[0], ld_s, ld_ref.at[1]])
+    kt_s[...] = tokens(k_s)[...].T
+    lkt_s[...] = tokens(lk_s)[...].T
+    for r in range(3):
+        gr.back(r, 1, 0)
+        done.back(r, 1, 0)
+    for r in range(3):
+        tokens(g_s.at[0])[block(r), :] = gr.query(r).astype(BF16).T
+        tokens(g_s.at[1])[block(r), :] = done.query(r).astype(BF16).T
+    for h in range(CHUNKS):
+        edq_ref[h] = g_s[0, h]
+        ldq_ref[h] = g_s[1, h]
     for a in range(2):
-        for source, ref, s in ((gr, gown_ref, 0), (done, lown_ref, 1)):
+        for i, (source, ref, s) in enumerate(((gr, eown_ref, 1), (done, lown_ref, 1))):
             for rows, g in source.keyed(s, a):
-                tokens(g_s.at[a, s])[rows, :] = g
+                tokens(g_s.at[2 + 2 * a + i])[rows, :] = g
             for h in range(CHUNKS):
-                ref[h, a] = g_s[a, s, h]
+                ref[h, a] = g_s[2 + 2 * a + i, h]
 
 
 PAIR = jax.ShapeDtypeStruct((PLANE, 2, CHUNK, HD), BF16)
@@ -387,9 +421,9 @@
         in_specs=[VMEM] * 3,
         out_specs=(VMEM,) * 10,
         out_shape=(
-            HALF,
+            held(CHUNKS, 1, CHUNK, HD),
             held(3, FRAME, FRAME),
-            held(3, FRAME, FRAME),
+            held(2, FRAME, FRAME),
             held(2 * HD, FRAME),
             held(2 * HD, FRAME),
             held(2, FRAME, FRAME),
@@ -403,7 +437,6 @@
         + [frames(2 * CHUNKS)] * 2
         + [
             pltpu.VMEM((KEYS, HD), BF16),
-            pltpu.VMEM((HD, KEYS), BF16),
             pltpu.VMEM((HD + 16, KEYS), BF16),
             pltpu.VMEM((HD + 16, 2 * FRAME), BF16),
             wide(HD),
@@ -421,22 +454,19 @@
         in_specs=[VMEM] * 5,
         out_specs=(VMEM,) * 4,
         out_shape=(
-            held(CHUNKS, 1, CHUNK, HD),
-            held(2 * HD, FRAME),
-            jax.ShapeDtypeStruct((HD, FRAME), F32),
+            held(HD, FRAME),
+            jax.ShapeDtypeStruct((8, FRAME), F32),
+            held(FRAME, FRAME),
             HALF,
         ),
         scratch_shapes=[
-            frames(CHUNKS),
             frames(2, CHUNKS),
             frames(CHUNKS),
             frames(CHUNKS),
-            pltpu.VMEM((KEYS, HD), BF16),
-            wide(HD),
+            pltpu.VMEM((FRAME, HD), BF16),
             wide(HD + 16),
             wide(2 * HD),
             pltpu.VMEM((3, 3 * BLOCK, BLOCK), F32),
-            wide(FRAME),
             wide(FRAME),
         ],
         compiler_params=room(16),
@@ -444,33 +474,48 @@
     )(near(edge), *kept)
 
 
-def attend_late(mine, swap, *kept):
-    return pl.pallas_call(
-        late_kernel,
+def attend_share(swap, *kept):
+    return pl.pallas_call(
+        share_kernel,
         in_specs=[VMEM] * 10,
         out_specs=(VMEM,) * 4,
-        out_shape=(ONE, HALF, HALF, PAIR),
+        out_shape=(held(FRAME, FRAME), PAIR, held(2 * HD, FRAME), held(CHUNKS, 1, CHUNK, HD)),
+        scratch_shapes=[frames(2, CHUNKS), frames(2, 2, CHUNKS), frames(CHUNKS)],
+        compiler_params=room(8),
+        name="attend_share",
+    )(near(swap), *kept)
+
+
+def attend_late(mine, swap, edge, *kept):
+    return pl.pallas_call(
+        late_kernel,
+        in_specs=[VMEM] * 12,
+        out_specs=(VMEM,) * 4,
+        out_shape=(ONE, ONE, HALF, HALF),
         scratch_shapes=[
-            frames(2, 2, CHUNKS),
-            frames(2, 2, CHUNKS),
-            frames(2 * CHUNKS),
-            frames(2 * CHUNKS),
-            pltpu.VMEM((HD, 2 * FRAME), BF16),
-            pltpu.VMEM((2, FRAME, FRAME), BF16),
+            frames(6, CHUNKS),
+            frames(3 * CHUNKS),
+            frames(CHUNKS),
+            frames(3 * CHUNKS),
+            frames(CHUNKS),
+            pltpu.VMEM((HD, KEYS), BF16),
+            pltpu.VMEM((HD, KEYS), BF16),
+            wide(FRAME),
+            wide(FRAME),
         ],
         compiler_params=room(14),
         name="attend_late",
-    )(near(mine), near(swap), *kept)
-
-
-def join_kernel(local_ref, outer_ref, dq_ref, lown_ref, eown_ref, swap_ref, edge_ref, out_ref):
+    )(near(mine), near(swap), near(edge), *kept)
+
+
+def join_kernel(local_ref, outer_ref, ldq_ref, edq_ref, lown_ref, eown_ref, swap_ref, edge_ref, out_ref):
     core = lax.axis_index("co")
     for h in range(CHUNKS):
         here, there = core * CHUNKS + h, (1 - core) * CHUNKS + h
         out_ref[there, 0] = local_ref[h, 0]
-        out_ref[there, 1] = local_ref[h, 1]
+        out_ref[there, 1] = ldq_ref[h]
         out_ref[here, 0] = outer_ref[h, 0]
-        out_ref[here, 1] = dq_ref[h]
+        out_ref[here, 1] = edq_ref[h]
         for a in range(2):
             x = lown_ref[h, a].astype(F32) + swap_ref[there, a].astype(F32)
             out_ref[there, 2 + a] = x.astype(BF16)
@@ -482,7 +527,7 @@
     swap, edge = parts[-2:]
     return pl.pallas_call(
         join_kernel,
-        in_specs=[VMEM] * 7,
+        in_specs=[VMEM] * 8,
         out_specs=VMEM,
         out_shape=jax.ShapeDtypeStruct((PLANE, 4, CHUNK, HD), BF16),
         compiler_params=room(10),
@@ -506,11 +551,13 @@
     kv_edge = lax.dynamic_slice_in_dim(kv, core * CHUNKS, CHUNKS, 0)
     edge = lax.ppermute(kv_edge, ("sx", "co"), across)
     local, lp, ld, lqt, lc2, ep, eqt, *kept = attend_early(mine, swap, neighbours)
-    outer, c2, dqt, gedge = attend_outer(edge, eqt, *kept)
+    ect = kept[0]
+    outt, factor, d0, gedge = attend_outer(edge, eqt, *kept)
     gedge_in = lax.ppermute(gedge, ("sx", "co"), across)
-    dq, lown, eown, gswap = attend_late(mine, swap, ep, eqt, c2, dqt, lp, ld, lqt, lc2)
+    ed, gswap, c2, outer = attend_share(swap, ep, eqt, ect, outt, factor, lp, ld, lqt, lc2)
     gswap_in = lax.ppermute(gswap, "co", swap_pairs)
-    packed = join(local, outer, dq, lown, eown, gswap_in, gedge_in)
+    edq, ldq, eown, lown = attend_late(mine, swap, edge, ep, eqt, c2, d0, ed, lp, ld, lqt, lc2)
+    packed = join(local, outer, ldq, edq, lown, eown, gswap_in, gedge_in)
     return unpack(lax.all_to_all(packed, plane, split_axis=0, concat_axis=0, tiled=True))
 
 

time: 85.4 us -> 83.7 us (0.980)
  waiting for transfers between devices: 7.64 us -> 5.6 us
    ppermute x1, waiting for transfers between devices: 7.01 us -> 4.01 us  [shards(): gedge_in = lax.ppermute(gedge, ('sx', 'co'), across)]
    pallas_call x2 -> x3, Pallas kernels: 4.22 us -> 5.37 us  [the longest x1 2.82 us: attend_late(): pl.pallas_call(late_kernel, in_specs=[VMEM] * 12, out_specs=(VMEM,) * 4,...]
    ppermute x1, waiting for transfers between devices: 0.62 us -> 1.59 us  [shards(): edge = lax.ppermute(kv_edge, ('sx', 'co'), across)]
    pallas_call x1, Pallas kernels: 5.91 us -> 4.95 us  [attend_early(): pl.pallas_call(early_kernel, in_specs=[VMEM] * 3, out_specs=(VMEM,) * 10,...]
  transfers between devices with their start and end apart: 4 -> 4, of which waited for: 2 -> 2; matrix products, arithmetic and copies ran while one was open for 0% -> 0% of each run, Pallas kernels for 7% -> 9%
where the time goes in v6:
time: 83.7 us; the launch traced here: 83.4 us
  blocking collectives  56.4 us (67%)
  Pallas kernels  15 us (18%)
  waiting for transfers between devices  5.6 us (7%)
  starting transfers between devices  5.42 us (6%)
  between operations  0.89 us (1%)
    all_to_all x1, blocking collectives, shards(): mine = lax.all_to_all(sent, plane, split_axis=0, concat_axis=0, tiled=True)  30.2 us
    all_to_all x1, blocking collectives, shards(): lax.all_to_all(packed, plane, split_axis=0, concat_axis=0, tiled=True)  26.2 us
    pallas_call x1, Pallas kernels, attend_early(): pl.pallas_call(early_kernel, in_specs=[VMEM] * 3, out_specs=(VMEM,) * 10,...  4.95 us
    ppermute x1, waiting for transfers between devices, shards(): gedge_in = lax.ppermute(gedge, ('sx', 'co'), across)  4.01 us
    pallas_call x1, Pallas kernels, attend_late(): pl.pallas_call(late_kernel, in_specs=[VMEM] * 12, out_specs=(VMEM,) * 4,...  2.82 us
    ppermute x1, starting transfers between devices, shards(): edge = lax.ppermute(kv_edge, ('sx', 'co'), across)  2.53 us
    pallas_call x1, Pallas kernels, attend_share(): pl.pallas_call(share_kernel, in_specs=[VMEM] * 10, out_specs=(VMEM,) * 4,...  2.3 us
    ppermute x1, starting transfers between devices, shards(): gedge_in = lax.ppermute(gedge, ('sx', 'co'), across)  2.24 us
  transfers between devices with their start and end apart: 4, of which 2 were waited for; matrix products, arithmetic and copies ran while one was open for 0% of the time, Pallas kernels for 9%

profile of v6, /device:TPU:2, one launch (start us, length us, event | category | flops | bytes accessed | tf_op | source)
XLA Modules:
  0.0 83.4 jit_solution(4683669234650253749)
XLA Ops:
  0.6 1.5 %enter.1 = bf16[16,4,96,128]{3,2,1,0:T(8,128)(2,1)S(1)} custom-call(bf16[96,2048]{1,0:T(8,128)(2,1)} %q_ref.1, bf16[96,2048]{1,0:T(8,128)(2,1)} %k_ref.1, bf16[96,2048]{1,0:T(8,128)(2,1)} %v_ref.1, bf16[96,2048]{1,0:T(8,128)(2,1)} %c_ref.1), custom_call_target="tpu_custom_call" | custom-call | tf_op jit(solution)/shard_map/enter/pallas_call | solution.py:54
  2.1 30.2 %all_to_all.10.mine_ref = bf16[16,4,96,128]{3,2,1,0:T(8,128)(2,1)S(1)} all-to-all(bf16[16,4,96,128]{3,2,1,0:T(8,128)(2,1)S(1)} %enter.1), channel_id=1, replica_groups=mesh['sx'=4,'yl'=2,'co'=2,'head'=8] {'yl','head'}, dimensions={0} | all-to-all | bytes 3145728 | tf_op jit(solution)/shard_map/all_to_all | solution.py:548
  32.3 0.0 copy-start
  32.3 0.1 slice.4
  32.3 0.1 collective-permute-start
  32.5 2.5 %collective-permute-start.1 = (bf16[8,2,96,128]{3,2,1,0:T(8,128)(2,1)S(1)}, bf16[8,2,96,128]{3,2,1,0:T(8,128)(2,1)S(1)}, u32[]{:S(2)}, u32[]{:S(2)}) collective-permute-start(bf16[8,2,96,128]{3,2,1,0:T(8,128)(2,1)S(1)} %constant_dynamic-slice_fusion), channel_id=1, source_target_pairs={{8,32},{32,8},{40,64},{64,40},{72,96},{96,72},{9,33},{33,9},{41,65... | collective-permute-start | bytes 1179656 | tf_op jit(solution)/shard_map/ppermute | solution.py:552
  35.0 0.0 collective-permute-done.swap_ref
  35.0 0.0 copy-done
  35.0 4.9 %attend_early.1 = (bf16[8,1,96,128]{3,2,1,0:T(8,128)(2,1)S(1)}, bf16[3,768,768]{2,1,0:T(8,128)(2,1)S(1)}, bf16[2,768,768]{2,1,0:T(8,128)(2,1)S(1)}, bf16[256,768...) custom-call(bf16[16,4,96,128]{3,2,1,0:T(8,128)(2,1)S(1)} %all_to_all, ...), custom_call_target="tpu_custom_call" | custom-call | tf_op jit(solution)/shard_map/attend_early/pallas_call | solution.py:419
  40.0 1.6 %collective-permute-done.1.edge_ref = bf16[8,2,96,128]{3,2,1,0:T(8,128)(2,1)S(1)} collective-permute-done((bf16[8,2,96,128]{3,2,1,0:T(8,128)(2,1)S(1)}, bf16[8,2,96,128]{3,2,1,0:T(8,128)(2,1)S(1)}, u32[]{:S(2)}, u32[]{:S(2)}) %collective-permute-start.1) | collective-permute-done | bytes 393248 | tf_op jit(solution)/shard_map/ppermute | solution.py:552
  41.6 2.0 %attend_outer.1 = (bf16[128,768]{1,0:T(8,128)(2,1)S(1)}, f32[8,768]{1,0:T(8,128)S(1)}, bf16[768,768]{1,0:T(8,128)(2,1)S(1)}, bf16[8,2,96,128]{3,2,1,0:T(8,128)(2,1)S(1)}) custom-call(bf16[8,2,96,128]{3,2,1,0:T(8,128)(2,1)S(1)} %collective-permute-done.1.edge_ref, bf16[256,768]{1,0:T(8,128)(2,1)S(1)} %get-tuple-element.28.eqt_ref, ...), custom_call_target="tpu_custom_call" | custom-call | tf_op jit(solution)/shard_map/attend_outer/pallas_call | solution.py:452
  43.5 2.3 %attend_share.1 = (bf16[768,768]{1,0:T(8,128)(2,1)S(1)}, bf16[16,2,96,128]{3,2,1,0:T(8,128)(2,1)S(1)}, bf16[256,768]{1,0:T(8,128)(2,1)S(1)}, bf16[8,1,96,128]{3,2,1,0:T(8,128)(2,1)S(1)}) custom-call(bf16[16,2,96,128]{3,2,1,0:T(8,128)(2,1)S(1)} %collective-permute-done.swap_ref, bf16[2,768,768]{2,1,0:T(8,128)(2,1)S(1)} %get-tuple-element.27.ep_ref, ...), custom_call_target="tpu_custom_call" | custom-call | tf_op jit(solution)/shard_map/attend_share/pallas_call | solution.py:478
  45.9 0.6 collective-permute-start.2
  46.4 2.2 %collective-permute-start.3 = (bf16[8,2,96,128]{3,2,1,0:T(8,128)(2,1)S(1)}, bf16[8,2,96,128]{3,2,1,0:T(8,128)(2,1)S(1)}, u32[]{:S(2)}, u32[]{:S(2)}) collective-permute-start(bf16[8,2,96,128]{3,2,1,0:T(8,128)(2,1)S(1)} %get-tuple-element.47), channel_id=1, source_target_pairs={{8,32},{32,8},{40,64},{64,40},{72,96},{96,72},{9,33},{33,9},{41,65... | collective-permute-start | bytes 1179656 | tf_op jit(solution)/shard_map/ppermute | solution.py:556
  48.7 2.8 %attend_late.1 = (bf16[8,96,128]{2,1,0:T(8,128)(2,1)S(1)}, bf16[8,96,128]{2,1,0:T(8,128)(2,1)S(1)}, bf16[8,2,96,128]{3,2,1,0:T(8,128)(2,1)S(1)}, bf16[8,2,96,128]{3,2,1,0:T(8,128)(2,1)S(1)}) custom-call(bf16[16,4,96,128]{3,2,1,0:T(8,128)(2,1)S(1)} %all_to_all.10.mine_ref, bf16[16,2,96,128]{3,2,1,0:T(8,128)(2,1)S(1)} %collective-permute-done.swap_ref, ...), custom_call_target="tpu_custom_call" | custom-call | tf_op jit(solution)/shard_map/attend_late/pallas_call | solution.py:490
  51.5 4.0 %collective-permute-done.3.edge_ref = bf16[8,2,96,128]{3,2,1,0:T(8,128)(2,1)S(1)} collective-permute-done((bf16[8,2,96,128]{3,2,1,0:T(8,128)(2,1)S(1)}, bf16[8,2,96,128]{3,2,1,0:T(8,128)(2,1)S(1)}, u32[]{:S(2)}, u32[]{:S(2)}) %collective-permute-start.3) | collective-permute-done | bytes 393248 | tf_op jit(solution)/shard_map/ppermute | solution.py:556
  55.5 0.0 collective-permute-done.2.swap_ref
  55.5 0.3 join.1
  55.8 26.2 %all_to_all.11.in_ref = bf16[16,4,96,128]{3,2,1,0:T(8,128)(2,1)S(1)} all-to-all(bf16[16,4,96,128]{3,2,1,0:T(8,128)(2,1)S(1)} %join.1), channel_id=1, replica_groups=mesh['sx'=4,'yl'=2,'co'=2,'head'=8] {'yl','head'}, dimensions={0} | all-to-all | bytes 3145728 | tf_op jit(solution)/shard_map/all_to_all | solution.py:561
  82.0 1.3 %unpack.1 = (bf16[96,2048]{1,0:T(8,128)(2,1)}, bf16[96,2048]{1,0:T(8,128)(2,1)}, bf16[96,2048]{1,0:T(8,128)(2,1)}, bf16[96,2048]{1,0:T(8,128)(2,1)}) custom-call(bf16[16,4,96,128]{3,2,1,0:T(8,128)(2,1)S(1)} %all_to_all.11.in_ref), custom_call_target="tpu_custom_call" | custom-call | tf_op jit(solution)/shard_map/unpack/pallas_call | solution.py:78
  (1 shorter events, 0.0 us)
Async XLA Ops:
  32.3 2.8 %copy-start = (s32[192,27]{0,1:T(8,128)S(1)}, s32[192,27]{0,1:T(8,128)}, u32[]{:S(2)}) copy-start(s32[192,27]{0,1:T(8,128)} %param.9) | copy-start | bytes 62212
  32.3 2.7 %collective-permute-start = (bf16[16,2,96,128]{3,2,1,0:T(8,128)(2,1)S(1)}, bf16[16,2,96,128]{3,2,1,0:T(8,128)(2,1)S(1)}, u32[]{:S(2)}, u32[]{:S(2)}) collective-permute-start(bf16[16,2,96,128]{3,2,1,0:T(8,128)(2,1)S(1)} %slice.4), channel_id=1, source_target_pairs={{0,8},{8,0},{1,9},{9,1},{2,10},{10,2},{3,11},{11,3},{4,12},{12,4},... | collective-permute-start | bytes 2359304 | tf_op jit(solution)/shard_map/ppermute | solution.py:550
  32.5 9.1 %collective-permute-start.1 = (bf16[8,2,96,128]{3,2,1,0:T(8,128)(2,1)S(1)}, bf16[8,2,96,128]{3,2,1,0:T(8,128)(2,1)S(1)}, u32[]{:S(2)}, u32[]{:S(2)}) collective-permute-start(bf16[8,2,96,128]{3,2,1,0:T(8,128)(2,1)S(1)} %constant_dynamic-slice_fusion), channel_id=1, source_target_pairs={{8,32},{32,8},{40,64},{64,40},{72,96},{96,72},{9,33},{33,9},{41,65... | collective-permute-start | bytes 1179656 | tf_op jit(solution)/shard_map/ppermute | solution.py:552
  45.9 9.7 %collective-permute-start.2 = (bf16[16,2,96,128]{3,2,1,0:T(8,128)(2,1)S(1)}, bf16[16,2,96,128]{3,2,1,0:T(8,128)(2,1)S(1)}, u32[]{:S(2)}, u32[]{:S(2)}) collective-permute-start(bf16[16,2,96,128]{3,2,1,0:T(8,128)(2,1)S(1)} %get-tuple-element.46), channel_id=1, source_target_pairs={{0,8},{8,0},{1,9},{9,1},{2,10},{10,2},{3,11},{11,3},{4,12},{12,4},... | collective-permute-start | bytes 2359304 | tf_op jit(solution)/shard_map/ppermute | solution.py:558
  46.4 9.1 %collective-permute-start.3 = (bf16[8,2,96,128]{3,2,1,0:T(8,128)(2,1)S(1)}, bf16[8,2,96,128]{3,2,1,0:T(8,128)(2,1)S(1)}, u32[]{:S(2)}, u32[]{:S(2)}) collective-permute-start(bf16[8,2,96,128]{3,2,1,0:T(8,128)(2,1)S(1)} %get-tuple-element.47), channel_id=1, source_target_pairs={{8,32},{32,8},{40,64},{64,40},{72,96},{96,72},{9,33},{33,9},{41,65... | collective-permute-start | bytes 1179656 | tf_op jit(solution)/shard_map/ppermute | solution.py:556

commit v7 on v6

--- a/solution.py
+++ b/solution.py
@@ -314,9 +314,10 @@
     sc.score(0, 0)
     vt_s[:HD, :] = tokens(v_s)[...].T
     sc.score(1, 0)
+    sc.soften(0, 0)
     sc.score(2, 0)
-    for r in range(3):
-        sc.soften(r, 0)
+    sc.soften(1, 0)
+    sc.soften(2, 0)
     for r in range(3):
         cols = block(r)
         old = etop_ref[0:1, cols]
@@ -328,12 +329,15 @@
         outt_ref[:, cols] = out
         factor_ref[:, cols] = jnp.broadcast_to(inv * SCALE * mine, (8, BLOCK))
         weigh(cols, ect_ref, inv * SCALE * edge, out, c2_s)
+    value_terms = gr.keyed(0, 1)
     for r in range(3):
         gr.back(r, 0)
-    for a in (1, 0):
-        for rows, g in gr.keyed(0, a):
-            tokens(g_s.at[a])[rows, :] = g
-        put(g_s.at[a], gedge_ref, 0, a)
+        rows, g = next(value_terms)
+        tokens(g_s.at[1])[rows, :] = g
+    put(g_s.at[1], gedge_ref, 0, 1)
+    for rows, g in gr.keyed(0, 0):
+        tokens(g_s.at[0])[rows, :] = g
+    put(g_s.at[0], gedge_ref, 0, 0)
 
 
 def share_kernel(

time: 83.7 us -> 83.5 us (level)
  no operation moved by 1% of the time
where the time goes in v7:
time: 83.5 us; the launch traced here: 83.2 us
  blocking collectives  56.4 us (68%)
  Pallas kernels  14.9 us (18%)
  waiting for transfers between devices  5.61 us (7%)
  starting transfers between devices  5.41 us (6%)
  between operations  0.89 us (1%)
    all_to_all x1, blocking collectives, shards(): mine = lax.all_to_all(sent, plane, split_axis=0, concat_axis=0, tiled=True)  30.2 us
    all_to_all x1, blocking collectives, shards(): lax.all_to_all(packed, plane, split_axis=0, concat_axis=0, tiled=True)  26.2 us
    pallas_call x1, Pallas kernels, attend_early(): pl.pallas_call(early_kernel, in_specs=[VMEM] * 3, out_specs=(VMEM,) * 10,...  4.95 us
    ppermute x1, waiting for transfers between devices, shards(): gedge_in = lax.ppermute(gedge, ('sx', 'co'), across)  4.02 us
    pallas_call x1, Pallas kernels, attend_late(): pl.pallas_call(late_kernel, in_specs=[VMEM] * 12, out_specs=(VMEM,) * 4,...  2.82 us
    ppermute x1, starting transfers between devices, shards(): edge = lax.ppermute(kv_edge, ('sx', 'co'), across)  2.53 us
    pallas_call x1, Pallas kernels, attend_share(): pl.pallas_call(share_kernel, in_specs=[VMEM] * 10, out_specs=(VMEM,) * 4,...  2.31 us
    ppermute x1, starting transfers between devices, shards(): gedge_in = lax.ppermute(gedge, ('sx', 'co'), across)  2.24 us
  transfers between devices with their start and end apart: 4, of which 2 were waited for; matrix products, arithmetic and copies ran while one was open for 0% of the time, Pallas kernels for 9%

profile of v7, /device:TPU:2, one launch (start us, length us, event | category | flops | bytes accessed | tf_op | source)
XLA Modules:
  0.0 83.2 jit_solution(8193010407607675516)
XLA Ops:
  0.6 1.5 %enter.1 = bf16[16,4,96,128]{3,2,1,0:T(8,128)(2,1)S(1)} custom-call(bf16[96,2048]{1,0:T(8,128)(2,1)} %q_ref.1, bf16[96,2048]{1,0:T(8,128)(2,1)} %k_ref.1, bf16[96,2048]{1,0:T(8,128)(2,1)} %v_ref.1, bf16[96,2048]{1,0:T(8,128)(2,1)} %c_ref.1), custom_call_target="tpu_custom_call" | custom-call | tf_op jit(solution)/shard_map/enter/pallas_call | solution.py:54
  2.1 30.2 %all_to_all.10.mine_ref = bf16[16,4,96,128]{3,2,1,0:T(8,128)(2,1)S(1)} all-to-all(bf16[16,4,96,128]{3,2,1,0:T(8,128)(2,1)S(1)} %enter.1), channel_id=1, replica_groups=mesh['sx'=4,'yl'=2,'co'=2,'head'=8] {'yl','head'}, dimensions={0} | all-to-all | bytes 3145728 | tf_op jit(solution)/shard_map/all_to_all | solution.py:552
  32.3 0.0 copy-start
  32.3 0.1 slice.4
  32.3 0.1 collective-permute-start
  32.5 2.5 %collective-permute-start.1 = (bf16[8,2,96,128]{3,2,1,0:T(8,128)(2,1)S(1)}, bf16[8,2,96,128]{3,2,1,0:T(8,128)(2,1)S(1)}, u32[]{:S(2)}, u32[]{:S(2)}) collective-permute-start(bf16[8,2,96,128]{3,2,1,0:T(8,128)(2,1)S(1)} %constant_dynamic-slice_fusion), channel_id=1, source_target_pairs={{8,32},{32,8},{40,64},{64,40},{72,96},{96,72},{9,33},{33,9},{41,65... | collective-permute-start | bytes 1179656 | tf_op jit(solution)/shard_map/ppermute | solution.py:556
  35.0 0.0 collective-permute-done.swap_ref
  35.0 0.0 copy-done
  35.0 4.9 %attend_early.1 = (bf16[8,1,96,128]{3,2,1,0:T(8,128)(2,1)S(1)}, bf16[3,768,768]{2,1,0:T(8,128)(2,1)S(1)}, bf16[2,768,768]{2,1,0:T(8,128)(2,1)S(1)}, bf16[256,768...) custom-call(bf16[16,4,96,128]{3,2,1,0:T(8,128)(2,1)S(1)} %all_to_all, ...), custom_call_target="tpu_custom_call" | custom-call | tf_op jit(solution)/shard_map/attend_early/pallas_call | solution.py:423
  40.0 1.6 %collective-permute-done.1.edge_ref = bf16[8,2,96,128]{3,2,1,0:T(8,128)(2,1)S(1)} collective-permute-done((bf16[8,2,96,128]{3,2,1,0:T(8,128)(2,1)S(1)}, bf16[8,2,96,128]{3,2,1,0:T(8,128)(2,1)S(1)}, u32[]{:S(2)}, u32[]{:S(2)}) %collective-permute-start.1) | collective-permute-done | bytes 393248 | tf_op jit(solution)/shard_map/ppermute | solution.py:556
  41.6 1.8 %attend_outer.1 = (bf16[128,768]{1,0:T(8,128)(2,1)S(1)}, f32[8,768]{1,0:T(8,128)S(1)}, bf16[768,768]{1,0:T(8,128)(2,1)S(1)}, bf16[8,2,96,128]{3,2,1,0:T(8,128)(2,1)S(1)}) custom-call(bf16[8,2,96,128]{3,2,1,0:T(8,128)(2,1)S(1)} %collective-permute-done.1.edge_ref, bf16[256,768]{1,0:T(8,128)(2,1)S(1)} %get-tuple-element.28.eqt_ref, ...), custom_call_target="tpu_custom_call" | custom-call | tf_op jit(solution)/shard_map/attend_outer/pallas_call | solution.py:456
  43.4 2.3 %attend_share.1 = (bf16[768,768]{1,0:T(8,128)(2,1)S(1)}, bf16[16,2,96,128]{3,2,1,0:T(8,128)(2,1)S(1)}, bf16[256,768]{1,0:T(8,128)(2,1)S(1)}, bf16[8,1,96,128]{3,2,1,0:T(8,128)(2,1)S(1)}) custom-call(bf16[16,2,96,128]{3,2,1,0:T(8,128)(2,1)S(1)} %collective-permute-done.swap_ref, bf16[2,768,768]{2,1,0:T(8,128)(2,1)S(1)} %get-tuple-element.27.ep_ref, ...), custom_call_target="tpu_custom_call" | custom-call | tf_op jit(solution)/shard_map/attend_share/pallas_call | solution.py:482
  45.7 0.6 collective-permute-start.2
  46.3 2.2 %collective-permute-start.3 = (bf16[8,2,96,128]{3,2,1,0:T(8,128)(2,1)S(1)}, bf16[8,2,96,128]{3,2,1,0:T(8,128)(2,1)S(1)}, u32[]{:S(2)}, u32[]{:S(2)}) collective-permute-start(bf16[8,2,96,128]{3,2,1,0:T(8,128)(2,1)S(1)} %get-tuple-element.47), channel_id=1, source_target_pairs={{8,32},{32,8},{40,64},{64,40},{72,96},{96,72},{9,33},{33,9},{41,65... | collective-permute-start | bytes 1179656 | tf_op jit(solution)/shard_map/ppermute | solution.py:560
  48.5 2.8 %attend_late.1 = (bf16[8,96,128]{2,1,0:T(8,128)(2,1)S(1)}, bf16[8,96,128]{2,1,0:T(8,128)(2,1)S(1)}, bf16[8,2,96,128]{3,2,1,0:T(8,128)(2,1)S(1)}, bf16[8,2,96,128]{3,2,1,0:T(8,128)(2,1)S(1)}) custom-call(bf16[16,4,96,128]{3,2,1,0:T(8,128)(2,1)S(1)} %all_to_all.10.mine_ref, bf16[16,2,96,128]{3,2,1,0:T(8,128)(2,1)S(1)} %collective-permute-done.swap_ref, ...), custom_call_target="tpu_custom_call" | custom-call | tf_op jit(solution)/shard_map/attend_late/pallas_call | solution.py:494
  51.3 4.0 %collective-permute-done.3.edge_ref = bf16[8,2,96,128]{3,2,1,0:T(8,128)(2,1)S(1)} collective-permute-done((bf16[8,2,96,128]{3,2,1,0:T(8,128)(2,1)S(1)}, bf16[8,2,96,128]{3,2,1,0:T(8,128)(2,1)S(1)}, u32[]{:S(2)}, u32[]{:S(2)}) %collective-permute-start.3) | collective-permute-done | bytes 393248 | tf_op jit(solution)/shard_map/ppermute | solution.py:560
  55.4 0.0 collective-permute-done.2.swap_ref
  55.4 0.3 join.1
  55.6 26.2 %all_to_all.11.in_ref = bf16[16,4,96,128]{3,2,1,0:T(8,128)(2,1)S(1)} all-to-all(bf16[16,4,96,128]{3,2,1,0:T(8,128)(2,1)S(1)} %join.1), channel_id=1, replica_groups=mesh['sx'=4,'yl'=2,'co'=2,'head'=8] {'yl','head'}, dimensions={0} | all-to-all | bytes 3145728 | tf_op jit(solution)/shard_map/all_to_all | solution.py:565
  81.8 1.3 %unpack.1 = (bf16[96,2048]{1,0:T(8,128)(2,1)}, bf16[96,2048]{1,0:T(8,128)(2,1)}, bf16[96,2048]{1,0:T(8,128)(2,1)}, bf16[96,2048]{1,0:T(8,128)(2,1)}) custom-call(bf16[16,4,96,128]{3,2,1,0:T(8,128)(2,1)S(1)} %all_to_all.11.in_ref), custom_call_target="tpu_custom_call" | custom-call | tf_op jit(solution)/shard_map/unpack/pallas_call | solution.py:78
  (1 shorter events, 0.0 us)
Async XLA Ops:
  32.3 2.8 %copy-start = (s32[192,27]{0,1:T(8,128)S(1)}, s32[192,27]{0,1:T(8,128)}, u32[]{:S(2)}) copy-start(s32[192,27]{0,1:T(8,128)} %param.9) | copy-start | bytes 62212
  32.3 2.7 %collective-permute-start = (bf16[16,2,96,128]{3,2,1,0:T(8,128)(2,1)S(1)}, bf16[16,2,96,128]{3,2,1,0:T(8,128)(2,1)S(1)}, u32[]{:S(2)}, u32[]{:S(2)}) collective-permute-start(bf16[16,2,96,128]{3,2,1,0:T(8,128)(2,1)S(1)} %slice.4), channel_id=1, source_target_pairs={{0,8},{8,0},{1,9},{9,1},{2,10},{10,2},{3,11},{11,3},{4,12},{12,4},... | collective-permute-start | bytes 2359304 | tf_op jit(solution)/shard_map/ppermute | solution.py:554
  32.5 9.1 %collective-permute-start.1 = (bf16[8,2,96,128]{3,2,1,0:T(8,128)(2,1)S(1)}, bf16[8,2,96,128]{3,2,1,0:T(8,128)(2,1)S(1)}, u32[]{:S(2)}, u32[]{:S(2)}) collective-permute-start(bf16[8,2,96,128]{3,2,1,0:T(8,128)(2,1)S(1)} %constant_dynamic-slice_fusion), channel_id=1, source_target_pairs={{8,32},{32,8},{40,64},{64,40},{72,96},{96,72},{9,33},{33,9},{41,65... | collective-permute-start | bytes 1179656 | tf_op jit(solution)/shard_map/ppermute | solution.py:556
  45.7 9.7 %collective-permute-start.2 = (bf16[16,2,96,128]{3,2,1,0:T(8,128)(2,1)S(1)}, bf16[16,2,96,128]{3,2,1,0:T(8,128)(2,1)S(1)}, u32[]{:S(2)}, u32[]{:S(2)}) collective-permute-start(bf16[16,2,96,128]{3,2,1,0:T(8,128)(2,1)S(1)} %get-tuple-element.46), channel_id=1, source_target_pairs={{0,8},{8,0},{1,9},{9,1},{2,10},{10,2},{3,11},{11,3},{4,12},{12,4},... | collective-permute-start | bytes 2359304 | tf_op jit(solution)/shard_map/ppermute | solution.py:562
  46.3 9.1 %collective-permute-start.3 = (bf16[8,2,96,128]{3,2,1,0:T(8,128)(2,1)S(1)}, bf16[8,2,96,128]{3,2,1,0:T(8,128)(2,1)S(1)}, u32[]{:S(2)}, u32[]{:S(2)}) collective-permute-start(bf16[8,2,96,128]{3,2,1,0:T(8,128)(2,1)S(1)} %get-tuple-element.47), channel_id=1, source_target_pairs={{8,32},{32,8},{40,64},{64,40},{72,96},{96,72},{9,33},{33,9},{41,65... | collective-permute-start | bytes 1179656 | tf_op jit(solution)/shard_map/ppermute | solution.py:560
